TPU v7x, 32 devices: a whole 2x2x4 slice. The times are simulated.
32 devices in a mesh: shard: 4 (over y, x), head: 4 (over z), tensor: 2 (over core).
Axes of the slice: x: 2, y: 2, z: 4, core: 2. Of those that a mesh axis runs over, the one named last changes fastest.
Arguments:
- tokens: bfloat16 [1152, 4, 2048], P(None, 'shard', ('head', 'tensor')), may hold values from -6 to 6
- seq_lengths: int32 [16], replicated, may hold values from 1 to 1024, as said below
- dealing: int32 [16], replicated, may hold values from 0 to 15, as said below
- gain_mixer: float32 [2048], replicated, may hold values from 0.5 to 1.5
- w_query: bfloat16 [2048, 2048], P('shard', ('head', 'tensor')), may hold values from -0.125 to 0.125
- w_key: bfloat16 [2048, 2048], P('shard', ('head', 'tensor')), may hold values from -0.125 to 0.125
- w_value: bfloat16 [2048, 2048], P('shard', ('head', 'tensor')), may hold values from -0.125 to 0.125
- w_gate: bfloat16 [2048, 2048], P('shard', ('head', 'tensor')), may hold values from -0.125 to 0.125
- w_beta: bfloat16 [2048, 16], P('shard', ('head', 'tensor')), may hold values from -0.125 to 0.125
- conv_weight: float32 [4, 3, 2048], P(None, None, ('head', 'tensor')), may hold values from -3 to 3
- gain_heads: float32 [128], replicated, may hold values from 0.5 to 1.5
- w_out: bfloat16 [2048, 2048], P(('head', 'tensor'), 'shard'), may hold values from -0.25 to 0.25
- gain_ffn: float32 [2048], replicated, may hold values from 0.5 to 1.5
- w_up_gate: bfloat16 [2048, 5632], P('shard', ('head', 'tensor')), may hold values from -0.125 to 0.125
- w_up: bfloat16 [2048, 5632], P('shard', ('head', 'tensor')), may hold values from -0.125 to 0.125
- w_down: bfloat16 [5632, 2048], P(('head', 'tensor'), 'shard'), may hold values from -0.15625 to 0.15625
- cotangent: bfloat16 [5120, 2048], P('shard', ('head', 'tensor')), may hold values from -6 to 6
Outputs:
- block_out: bfloat16 [5120, 2048], P('shard', ('head', 'tensor'))
- d_tokens: float32 [1152, 4, 2048], P(None, 'shard', ('head', 'tensor'))
- d_gain_mixer: float32 [2048], replicated
- d_w_query: float32 [2048, 2048], P('shard', ('head', 'tensor'))
- d_w_key: float32 [2048, 2048], P('shard', ('head', 'tensor'))
- d_w_value: float32 [2048, 2048], P('shard', ('head', 'tensor'))
- d_w_gate: float32 [2048, 2048], P('shard', ('head', 'tensor'))
- d_w_beta: float32 [2048, 16], P('shard', ('head', 'tensor'))
- d_conv_weight: float32 [4, 3, 2048], replicated
- d_gain_heads: float32 [128], replicated
- d_w_out: float32 [2048, 2048], P(('head', 'tensor'), 'shard')
- d_gain_ffn: float32 [2048], replicated
- d_w_up_gate: float32 [2048, 5632], P('shard', ('head', 'tensor'))
- d_w_up: float32 [2048, 5632], P('shard', ('head', 'tensor'))
- d_w_down: float32 [5632, 2048], P(('head', 'tensor'), 'shard')
Inputs may be any that keep to these rules, and one draw needn't show every extreme that they name: `seq_lengths`: the sequences at dealt positions 4 g to 4 g + 3 have lengths that sum to 1152; rounded up to multiples of 64 they sum to at most 1280, which some group reaches; some sequence has 1024 tokens. `dealing`: a permutation of the 16 sequence numbers.
All inputs are finite; a program needn't handle non-finite values.
Results may differ from a plain program's by a relative error of at most 0.015.
Values may be sent and summed in bfloat16 or wider, within the bound.
A program may use at most 256 MiB of HBM per device.

v0:
```python
import jax
import jax.numpy as jnp
from jax import lax
from jax.sharding import PartitionSpec as P

D = 2048
HD = 128
CONV = 4
BLOCK = 64
SEQ_DEV = 4
REAL_DEV = 1152
CAP = 1280


EPSILON = 1e-06
HEAD_FLOOR = 0.01
HIGHEST = lax.Precision.HIGHEST


def int_sum(values, along_axis):
    return jnp.sum(values, axis=along_axis)


def layout(seq_lengths, dealing, group_idx):
    total_seqs = seq_lengths.shape[0]
    starts = jnp.cumsum(seq_lengths, dtype=jnp.int32) - seq_lengths
    chosen = lax.dynamic_slice_in_dim(dealing, group_idx * SEQ_DEV, SEQ_DEV)
    picked = (chosen[:, None] == jnp.arange(total_seqs, dtype=jnp.int32)[None, :]).astype(jnp.int32)
    own_length = int_sum(picked * seq_lengths[None, :], 1)
    own_start = int_sum(picked * starts[None, :], 1)
    padded = (own_length + BLOCK - 1) // BLOCK * BLOCK
    buffer_start = jnp.cumsum(padded, dtype=jnp.int32) - padded
    row_ids = jnp.arange(CAP, dtype=jnp.int32)
    member = int_sum((row_ids[:, None] >= buffer_start[None, :]).astype(jnp.int32), 1) - 1
    owned_by = (member[:, None] == jnp.arange(SEQ_DEV, dtype=jnp.int32)[None, :]).astype(jnp.int32)
    position = row_ids - int_sum(owned_by * buffer_start[None, :], 1)
    row_length = int_sum(owned_by * own_length[None, :], 1)
    seq_first = int_sum(owned_by * own_start[None, :], 1)
    filled = position < row_length
    return (seq_first + position, position, filled, seq_first, own_start, own_length)


def congruent(lower_end, upper_end, residue, modulus):
    return (upper_end - 1 - residue) // modulus - (lower_end - 1 - residue) // modulus


def matmul(left, right):
    return jnp.dot(left, right, preferred_element_type=jnp.float32)


def matmul_t(left, right):
    return lax.dot_general(
        left, right, (((1,), (1,)), ((), ())), preferred_element_type=jnp.float32
    )


def t_matmul(left, right):
    return lax.dot_general(
        left, right, (((0,), (0,)), ((), ())), preferred_element_type=jnp.float32
    )


def short_conv(stacked, weight, position):
    summed = weight[0][None] * stacked
    for offset in range(1, CONV):
        shifted = jnp.concatenate(
            [jnp.zeros((offset,) + stacked.shape[1:], jnp.float32), stacked[:-offset]], axis=0
        )
        summed = (
            summed
            + weight[offset][None]
            * shifted
            * (position >= offset).astype(jnp.float32)[:, None, None]
        )
    return summed


def delta_rule(queries, key_rows, value_rows, beta_rows, persist):
    row_count, head_count, head_size = queries.shape
    blocks = row_count // BLOCK

    def to_blocks(values):
        return values.reshape(blocks, BLOCK, head_count, -1).transpose(0, 2, 1, 3)

    q_blk = to_blocks(queries)
    k_blk = to_blocks(key_rows)
    v_blk = to_blocks(value_rows)
    b_blk = to_blocks(beta_rows[..., None])
    key_grams = jnp.einsum("nhid,nhjd->nhij", k_blk, k_blk, precision=HIGHEST)
    strict = jnp.tril(jnp.ones((BLOCK, BLOCK), jnp.float32), -1)
    lower_incl = jnp.tril(jnp.ones((BLOCK, BLOCK), jnp.float32))
    identity = jnp.eye(BLOCK, dtype=jnp.float32)
    system = identity + strict * (b_blk * key_grams)
    inverse = lax.linalg.triangular_solve(
        system,
        jnp.broadcast_to(identity, system.shape),
        left_side=True,
        lower=True,
        unit_diagonal=True,
    )
    w_blk = jnp.einsum("nhij,nhjd->nhid", inverse, b_blk * k_blk, precision=HIGHEST)
    u_blk = jnp.einsum("nhij,nhjd->nhid", inverse, b_blk * v_blk, precision=HIGHEST)
    scores = jnp.einsum("nhid,nhjd->nhij", q_blk, k_blk, precision=HIGHEST) * lower_incl

    def advance(memory, inputs):
        q_part, k_part, w_part, u_part, s_part, p_part = inputs
        memory = memory * p_part
        fresh_vals = u_part - jnp.einsum("hid,hde->hie", w_part, memory, precision=HIGHEST)
        output = jnp.einsum("hid,hde->hie", q_part, memory, precision=HIGHEST) + jnp.einsum(
            "hij,hje->hie", s_part, fresh_vals, precision=HIGHEST
        )
        memory = memory + jnp.einsum("hid,hie->hde", k_part, fresh_vals, precision=HIGHEST)
        return (memory, output)

    start_mem = jnp.zeros((head_count, head_size, head_size), jnp.float32)
    _, outputs = lax.scan(advance, start_mem, (q_blk, k_blk, w_blk, u_blk, scores, persist))
    return outputs.transpose(0, 2, 1, 3).reshape(row_count, head_count, head_size)


def mixer_piece(q_in, k_in, v_in, g_in, b_in, conv_in, gain_in, position, filled_f, persist):
    row_count = q_in.shape[0]
    head_count = q_in.shape[1] // HD
    stacked = jnp.stack([q_in, k_in, v_in], axis=1)
    active = jax.nn.silu(short_conv(stacked, conv_in, position)) * filled_f[:, None, None]

    def unit_norm(values):
        values = values.reshape(row_count, head_count, HD)
        return values * lax.rsqrt(jnp.sum(values * values, axis=2, keepdims=True) + EPSILON)

    queries = unit_norm(active[:, 0])
    key_rows = unit_norm(active[:, 1])
    value_rows = active[:, 2].reshape(row_count, head_count, HD)
    beta_rows = jax.nn.sigmoid(b_in)
    core_out = delta_rule(queries, key_rows, value_rows, beta_rows, persist)
    normal = (
        core_out
        * lax.rsqrt(jnp.maximum(jnp.mean(core_out * core_out, axis=2, keepdims=True), HEAD_FLOOR))
        * gain_in
    )
    gate_rows = jax.nn.silu(g_in.reshape(row_count, head_count, HD))
    return (normal * gate_rows).reshape(row_count, head_count * HD)


def full_rows(piece_in):
    return lax.all_gather(piece_in, ("head", "tensor"), axis=1, tiled=True)


def shares(partial_sum):
    return lax.psum_scatter(partial_sum, ("head", "tensor"), scatter_dimension=1, tiled=True)


def norm_back(grad_n, kept_rows, row_scale, gain_part):
    weighted = grad_n * gain_part[None, :]
    totals = lax.psum(jnp.sum(weighted * kept_rows, axis=1), ("head", "tensor"))
    back_rows = (
        row_scale[:, None] * weighted
        - kept_rows * (row_scale * row_scale * row_scale * totals / D)[:, None]
    )
    gain_grad = jnp.sum(grad_n * kept_rows * row_scale[:, None], axis=0)
    return (back_rows, gain_grad)


def body(
    tokens,
    seq_lengths,
    dealing,
    gain_mixer,
    w_query,
    w_key,
    w_value,
    w_gate,
    w_beta,
    conv_weight,
    gain_heads,
    w_out,
    gain_ffn,
    w_up_gate,
    w_up,
    w_down,
    cotangent,
):
    shards = lax.axis_size("shard")
    device = lax.axis_index("shard")
    part_width = tokens.shape[2]
    col_start = lax.axis_index(("head", "tensor")) * part_width
    per_peer = CAP // shards + SEQ_DEV
    total_seqs = seq_lengths.shape[0]
    finish = jnp.cumsum(seq_lengths, dtype=jnp.int32)
    starts = finish - seq_lengths
    own_rows = tokens.reshape(REAL_DEV, part_width)
    packed_ids = jnp.arange(REAL_DEV, dtype=jnp.int32) * shards + device
    inside = (
        (packed_ids[:, None] >= starts[None, :]) & (packed_ids[:, None] < finish[None, :])
    ).astype(jnp.int32)
    seq_ids = jnp.arange(total_seqs, dtype=jnp.int32)
    matches = (dealing[:, None] == seq_ids[None, :]).astype(jnp.int32)
    seq_home = int_sum(matches * (seq_ids // SEQ_DEV)[:, None], 0)
    target = int_sum(inside * seq_home[None, :], 1)
    to_peer = (target[:, None] == jnp.arange(shards, dtype=jnp.int32)[None, :]).astype(jnp.int32)
    order_in = int_sum(to_peer * (jnp.cumsum(to_peer, axis=0, dtype=jnp.int32) - 1), 1)
    sent_slot = target * per_peer + order_in
    outbox = jnp.zeros((shards * per_peer, part_width), jnp.bfloat16).at[sent_slot].set(own_rows)
    arrived = lax.all_to_all(
        outbox.reshape(shards, per_peer, part_width),
        "shard",
        split_axis=0,
        concat_axis=0,
        tiled=True,
    )
    natural, position, filled, seq_first, own_start, own_length = layout(
        seq_lengths, dealing, device
    )
    source = natural % shards
    earlier = own_start[None, :] < seq_first[:, None]
    span_counts = congruent(
        own_start[None, :], (own_start + own_length)[None, :], source[:, None], shards
    )
    arrival = int_sum(jnp.where(earlier, span_counts, 0), 1) + congruent(
        seq_first, natural, source, shards
    )
    recv_slot = source * per_peer + arrival
    take_slot = jnp.where(filled, recv_slot, 0)
    received = arrived.reshape(shards * per_peer, part_width)[take_slot]
    x_rows = jnp.where(filled[:, None], received, jnp.zeros_like(received))
    filled_f = filled.astype(jnp.float32)
    persist = (position.reshape(-1, BLOCK)[:, 0] != 0).astype(jnp.float32)
    gathered = (
        lax.all_gather(w_query, "shard", axis=0, tiled=True),
        lax.all_gather(w_key, "shard", axis=0, tiled=True),
        lax.all_gather(w_value, "shard", axis=0, tiled=True),
        lax.all_gather(w_gate, "shard", axis=0, tiled=True),
        lax.all_gather(w_beta, "shard", axis=0, tiled=True),
        lax.all_gather(w_out, "shard", axis=1, tiled=True),
        lax.all_gather(w_up_gate, "shard", axis=0, tiled=True),
        lax.all_gather(w_up, "shard", axis=0, tiled=True),
        lax.all_gather(w_down, "shard", axis=1, tiled=True),
    )
    (
        full_query,
        full_key,
        full_value,
        full_gate,
        full_beta,
        full_out,
        full_up_gate,
        full_up,
        full_down,
    ) = gathered
    rows_full = full_rows(x_rows).astype(jnp.float32)
    scale_one = lax.rsqrt(jnp.mean(rows_full * rows_full, axis=1) + EPSILON)
    normed = (rows_full * scale_one[:, None] * gain_mixer[None, :]).astype(jnp.bfloat16)
    q_pre = matmul(normed, full_query)
    k_pre = matmul(normed, full_key)
    v_pre = matmul(normed, full_value)
    g_pre = matmul(normed, full_gate)
    beta_pre = matmul(normed, full_beta)

    def local_mixer(q_in, k_in, v_in, g_in, b_in, conv_in, gain_in):
        return mixer_piece(
            q_in, k_in, v_in, g_in, b_in, conv_in, gain_in, position, filled_f, persist
        )

    mixed_f32, mixer_pull = jax.vjp(
        local_mixer, q_pre, k_pre, v_pre, g_pre, beta_pre, conv_weight, gain_heads
    )
    mixed = mixed_f32.astype(jnp.bfloat16)
    branch = shares(matmul(mixed, full_out))
    dealt_f32 = x_rows.astype(jnp.float32)
    hidden = dealt_f32 + branch
    held_low = hidden.astype(jnp.bfloat16)
    held_full = full_rows(held_low).astype(jnp.float32)
    scale_two = lax.rsqrt(jnp.mean(held_full * held_full, axis=1) + EPSILON)
    normed_two = (held_full * scale_two[:, None] * gain_ffn[None, :]).astype(jnp.bfloat16)
    gate_act = matmul(normed_two, full_up_gate)
    up_act = matmul(normed_two, full_up)
    sig_gate = jax.nn.sigmoid(gate_act)
    product = (gate_act * sig_gate * up_act).astype(jnp.bfloat16)
    block_out = (hidden + shares(matmul(product, full_down))).astype(jnp.bfloat16)
    cot_full = full_rows(cotangent)
    d_product = matmul_t(cot_full, full_down)
    d_w_down = t_matmul(product, cot_full)
    d_gate = (d_product * up_act * sig_gate * (1.0 + gate_act * (1.0 - sig_gate))).astype(
        jnp.bfloat16
    )
    d_up = (d_product * gate_act * sig_gate).astype(jnp.bfloat16)
    d_w_up_gate = t_matmul(normed_two, d_gate)
    d_w_up = t_matmul(normed_two, d_up)
    d_normed_two = shares(matmul_t(d_gate, full_up_gate) + matmul_t(d_up, full_up))
    held_part = held_low.astype(jnp.float32)
    ffn_gain_part = lax.dynamic_slice_in_dim(gain_ffn, col_start, part_width)
    d_from_ffn, ffn_gain_grad = norm_back(d_normed_two, held_part, scale_two, ffn_gain_part)
    d_hidden = cotangent.astype(jnp.float32) + d_from_ffn
    d_branch_full = full_rows(d_hidden.astype(jnp.bfloat16))
    d_mixed = matmul_t(d_branch_full, full_out)
    d_w_out = t_matmul(mixed, d_branch_full)
    d_q, d_k, d_v, d_g, d_b, d_conv, d_gain_heads_part = mixer_pull(d_mixed)
    d_q_low = d_q.astype(jnp.bfloat16)
    d_k_low = d_k.astype(jnp.bfloat16)
    d_v_low = d_v.astype(jnp.bfloat16)
    d_g_low = d_g.astype(jnp.bfloat16)
    beta_f32 = full_beta.astype(jnp.float32)
    d_normed_terms = (
        matmul_t(d_q_low, full_query)
        + matmul_t(d_k_low, full_key)
        + matmul_t(d_v_low, full_value)
        + matmul_t(d_g_low, full_gate)
    )
    d_normed_terms = d_normed_terms + jnp.einsum("rh,dh->rd", d_b, beta_f32, precision=HIGHEST)
    d_normed = shares(d_normed_terms)
    d_w_query = t_matmul(normed, d_q_low)
    d_w_key = t_matmul(normed, d_k_low)
    d_w_value = t_matmul(normed, d_v_low)
    d_w_gate = t_matmul(normed, d_g_low)
    d_w_beta = jnp.einsum(
        "rd,rh->dh", normed, d_b, precision=HIGHEST, preferred_element_type=jnp.float32
    )
    mixer_gain_part = lax.dynamic_slice_in_dim(gain_mixer, col_start, part_width)
    d_from_mixer, mixer_gain_grad = norm_back(d_normed, dealt_f32, scale_one, mixer_gain_part)
    d_dealt = d_hidden + d_from_mixer
    post_slot = jnp.where(filled, recv_slot, shards * per_peer)
    outbox_back = (
        jnp.zeros((shards * per_peer, part_width), jnp.float32)
        .at[post_slot]
        .set(d_dealt, mode="drop")
    )
    arrived_back = lax.all_to_all(
        outbox_back.reshape(shards, per_peer, part_width).astype(jnp.bfloat16),
        "shard",
        split_axis=0,
        concat_axis=0,
        tiled=True,
    ).astype(jnp.float32)
    d_tokens = arrived_back.reshape(shards * per_peer, part_width)[sent_slot].reshape(
        REAL_DEV, 1, part_width
    )
    mixer_gain_full = lax.dynamic_update_slice(
        jnp.zeros((D,), jnp.float32), mixer_gain_grad, (col_start,)
    )
    ffn_gain_full = lax.dynamic_update_slice(
        jnp.zeros((D,), jnp.float32), ffn_gain_grad, (col_start,)
    )
    conv_full = lax.dynamic_update_slice(
        jnp.zeros((CONV, 3, D), jnp.float32), d_conv, (0, 0, col_start)
    )
    small_sums = lax.psum(
        (mixer_gain_full, conv_full, d_gain_heads_part, ffn_gain_full), ("shard", "head", "tensor")
    )
    grad_sums = (
        lax.psum_scatter(
            d_w_query.astype(jnp.bfloat16), "shard", scatter_dimension=0, tiled=True
        ).astype(jnp.float32),
        lax.psum_scatter(
            d_w_key.astype(jnp.bfloat16), "shard", scatter_dimension=0, tiled=True
        ).astype(jnp.float32),
        lax.psum_scatter(
            d_w_value.astype(jnp.bfloat16), "shard", scatter_dimension=0, tiled=True
        ).astype(jnp.float32),
        lax.psum_scatter(
            d_w_gate.astype(jnp.bfloat16), "shard", scatter_dimension=0, tiled=True
        ).astype(jnp.float32),
        lax.psum_scatter(
            d_w_beta.astype(jnp.bfloat16), "shard", scatter_dimension=0, tiled=True
        ).astype(jnp.float32),
        lax.psum_scatter(
            d_w_out.astype(jnp.bfloat16), "shard", scatter_dimension=1, tiled=True
        ).astype(jnp.float32),
        lax.psum_scatter(
            d_w_up_gate.astype(jnp.bfloat16), "shard", scatter_dimension=0, tiled=True
        ).astype(jnp.float32),
        lax.psum_scatter(
            d_w_up.astype(jnp.bfloat16), "shard", scatter_dimension=0, tiled=True
        ).astype(jnp.float32),
        lax.psum_scatter(
            d_w_down.astype(jnp.bfloat16), "shard", scatter_dimension=1, tiled=True
        ).astype(jnp.float32),
    )
    return (
        block_out,
        d_tokens,
        small_sums[0],
        grad_sums[0],
        grad_sums[1],
        grad_sums[2],
        grad_sums[3],
        grad_sums[4],
        small_sums[1],
        small_sums[2],
        grad_sums[5],
        small_sums[3],
        grad_sums[6],
        grad_sums[7],
        grad_sums[8],
    )


def solution(mesh):
    placed = (
        P(None, "shard", ("head", "tensor")),
        P(),
        P(),
        P(),
        P("shard", ("head", "tensor")),
        P("shard", ("head", "tensor")),
        P("shard", ("head", "tensor")),
        P("shard", ("head", "tensor")),
        P("shard", ("head", "tensor")),
        P(None, None, ("head", "tensor")),
        P(),
        P(("head", "tensor"), "shard"),
        P(),
        P("shard", ("head", "tensor")),
        P("shard", ("head", "tensor")),
        P(("head", "tensor"), "shard"),
        P("shard", ("head", "tensor")),
    )
    return jax.shard_map(
        body,
        mesh=mesh,
        in_specs=placed,
        out_specs=(
            P("shard", ("head", "tensor")),
            P(None, "shard", ("head", "tensor")),
            P(),
            P("shard", ("head", "tensor")),
            P("shard", ("head", "tensor")),
            P("shard", ("head", "tensor")),
            P("shard", ("head", "tensor")),
            P("shard", ("head", "tensor")),
            P(),
            P(),
            P(("head", "tensor"), "shard"),
            P(),
            P("shard", ("head", "tensor")),
            P("shard", ("head", "tensor")),
            P(("head", "tensor"), "shard"),
        ),
        check_vma=False,
    )
```

profile of v0, /device:TPU:0, one launch (start us, length us, event | category | flops | bytes accessed | tf_op | source)
XLA Modules:
  0.0 2162.5 jit_solution(5966821520040974205)
XLA Ops:
  52.9 44.9 %all-gather.13.cloned.1.call-done = bf16[1280,2048]{1,0:T(8,128)(2,1)} async-done(((bf16[1280,256]{1,0:T(8,128)(2,1)}), bf16[1280,2048]{1,0:T(8,128)(2,1)}) %all-gather.13.cloned.1.call-update) | async-done | bytes 5242896 | tf_op jit(solution)/shard_map/all_gather | solution.py:145
  105.4 19.1 all-gather.19.cloned.1.call-done
  128.8 24.2 %all-gather.17.cloned.1.call-done = bf16[2048,256]{1,0:T(8,128)(2,1)} async-done(((bf16[512,256]{1,0:T(8,128)(2,1)}), bf16[2048,256]{1,0:T(8,128)(2,1)}) %all-gather.17.cloned.1.call-update) | async-done | bytes 1048592 | tf_op jit(solution)/shard_map/all_gather | solution.py:229
  157.3 24.0 %all-gather.15.cloned.1.call-done = bf16[2048,256]{1,0:T(8,128)(2,1)} async-done(((bf16[512,256]{1,0:T(8,128)(2,1)}), bf16[2048,256]{1,0:T(8,128)(2,1)}) %all-gather.15.cloned.1.call-update) | async-done | bytes 1048592 | tf_op jit(solution)/shard_map/all_gather | solution.py:228
  218.4 198.2 %custom-call.5 = f32[20,2,1,64,64]{3,4,2,1,0:T(8,128)} custom-call(f32[20,2,1,64,64]{4,3,2,1,0:T(8,128)} %add_bitcast_fusion), custom_call_target="InvertDiagBlocksLowerTriangular" | custom-call | tf_op jit(solution)/shard_map/jvp()/triangular_solve | solution.py:94
  434.5 175.3 %while.42 = (s32[]{:T(128)}, f32[2,128,128]{2,1,0:T(8,128)S(1)}, f32[20,2,64,128]{3,2,1,0:T(8,128)}, f32[20,2,128,128]{3,2,1,0:T(8,128)}, f32[20,2,64,128]{3,2,1...) while((s32[]{:T(128)}, f32[2,128,128]{2,1,0:T(8,128)S(1)}, ...), condition=%wide.region_19.20_spmd.clone, body=%wide.region_18.19_spmd.clone.sunk | while | flops 88408064 | bytes 1577630 | solution.py:116
  633.6 109.5 %reduce-scatter.16.cloned.1.call-done = f32[1280,256]{1,0:T(8,128)} async-done(((f32[1280,2048]{1,0:T(8,128)}), f32[1280,256]{1,0:T(8,128)}) %reduce-scatter.16.cloned.1.call-update) | async-done | bytes 1310736 | tf_op jit(solution)/shard_map/reduce_scatter | solution.py:149
  748.8 51.9 %all-gather.25.cloned.1.call-done = bf16[1280,2048]{1,0:T(8,128)(2,1)} async-done(((bf16[1280,256]{1,0:T(8,128)(2,1)}), bf16[1280,2048]{1,0:T(8,128)(2,1)}) %all-gather.25.cloned.1.call-update) | async-done | bytes 5242896 | tf_op jit(solution)/shard_map/all_gather | solution.py:145
  804.3 38.1 %all-gather.29.cloned.1.call-done = bf16[2048,704]{0,1:T(8,128)(2,1)} async-done(((bf16[512,704]{0,1:T(8,128)(2,1)}), bf16[2048,704]{0,1:T(8,128)(2,1)}) %all-gather.29.cloned.1.call-update) | async-done | bytes 2883600 | tf_op jit(solution)/shard_map/all_gather | solution.py:235
  851.7 34.2 %all-gather.27.cloned.1.call-done = bf16[2048,704]{0,1:T(8,128)(2,1)} async-done(((bf16[512,704]{0,1:T(8,128)(2,1)}), bf16[2048,704]{0,1:T(8,128)(2,1)}) %all-gather.27.cloned.1.call-update) | async-done | bytes 2883600 | tf_op jit(solution)/shard_map/all_gather | solution.py:234
  895.0 34.4 %all-gather.31.cloned.1.call-done = bf16[704,2048]{1,0:T(8,128)(2,1)} async-done(((bf16[704,512]{1,0:T(8,128)(2,1)}), bf16[704,2048]{1,0:T(8,128)(2,1)}) %all-gather.31.cloned.1.call-update) | async-done | bytes 2883600 | tf_op jit(solution)/shard_map/all_gather | solution.py:236
  929.4 58.0 %all-gather.33.cloned.1.call-done = bf16[1280,2048]{1,0:T(8,128)(2,1)} async-done(((bf16[1280,256]{1,0:T(8,128)(2,1)}), bf16[1280,2048]{1,0:T(8,128)(2,1)}) %all-gather.33.cloned.1.call-update) | async-done | bytes 5242896 | tf_op jit(solution)/shard_map/all_gather | solution.py:145
  987.4 11.9 multiply_convert_fusion
  1011.1 107.6 %reduce-scatter.20.cloned.1.call-done = f32[1280,256]{1,0:T(8,128)} async-done(((f32[1280,2048]{1,0:T(8,128)}), f32[1280,256]{1,0:T(8,128)}) %reduce-scatter.20.cloned.1.call-update) | async-done | bytes 1310736 | tf_op jit(solution)/shard_map/reduce_scatter | solution.py:149
  1121.5 13.9 psum.42
  1157.9 35.4 %all-gather.35.cloned.1.call-done = bf16[1280,2048]{1,0:T(8,128)(2,1)} async-done(((bf16[1280,256]{1,0:T(8,128)(2,1)}), bf16[1280,2048]{1,0:T(8,128)(2,1)}) %all-gather.35.cloned.1.call-update) | async-done | bytes 5242896 | tf_op jit(solution)/shard_map/all_gather | solution.py:145
  1214.4 264.2 %while.43 = (s32[]{:T(128)}, f32[2,128,128]{2,1,0:T(8,128)S(1)}, f32[20,2,64,128]{3,2,1,0:T(8,128)}, f32[20,2,64,128]{3,2,1,0:T(8,128)}, f32[20,2,64,128]{3,2,1,...) while((s32[]{:T(128)}, f32[2,128,128]{2,1,0:T(8,128)S(1)}, ...), condition=%wide.region_29.30_spmd.clone, body=%wide.region_28.29_spmd.clone.sunk | while | flops 176406528 | bytes 2368719 | solution.py:116
  1577.5 20.2 add_add_fusion
  1657.7 48.0 %reduce-scatter.22.cloned.1.call-done = f32[1280,256]{1,0:T(8,128)} async-done(((f32[1280,2048]{1,0:T(8,128)}), f32[1280,256]{1,0:T(8,128)}) %reduce-scatter.22.cloned.1.call-update) | async-done | bytes 1310736 | tf_op jit(solution)/shard_map/reduce_scatter | solution.py:149
  1708.9 13.9 psum.43
  1722.9 11.3 scatter_custom_fusion.1
  1741.1 14.7 reduce-scatter.34.cloned.1.call-done
  1758.2 42.2 %reduce-scatter.36.cloned.1.call-done = bf16[512,704]{0,1:T(8,128)(2,1)} async-done(((bf16[2048,704]{0,1:T(8,128)(2,1)}), bf16[512,704]{0,1:T(8,128)(2,1)}) %reduce-scatter.36.cloned.1.call-update) | async-done | bytes 720912 | tf_op jit(solution)/shard_map/reduce_scatter | solution.py:370
  1802.7 42.4 %reduce-scatter.38.cloned.1.call-done = bf16[704,512]{1,0:T(8,128)(2,1)} async-done(((bf16[704,2048]{1,0:T(8,128)(2,1)}), bf16[704,512]{1,0:T(8,128)(2,1)}) %reduce-scatter.38.cloned.1.call-update) | async-done | bytes 720912 | tf_op jit(solution)/shard_map/reduce_scatter | solution.py:373
  1847.7 25.4 %reduce-scatter.40.cloned.1.call-done = bf16[512,2]{1,0:T(8,128)(2,1)} async-done(((bf16[2048,2]{1,0:T(8,128)(2,1)}), bf16[512,2]{1,0:T(8,128)(2,1)}) %reduce-scatter.40.cloned.1.call-update) | async-done | bytes 2064
  1874.8 29.8 %reduce-scatter.24.cloned.1.call-done = bf16[512,256]{1,0:T(8,128)(2,1)} async-done(((bf16[2048,256]{1,0:T(8,128)(2,1)}), bf16[512,256]{1,0:T(8,128)(2,1)}) %reduce-scatter.24.cloned.1.call-update) | async-done | bytes 262160 | tf_op jit(solution)/shard_map/reduce_scatter | solution.py:349
  1906.4 28.9 %reduce-scatter.26.cloned.1.call-done = bf16[512,256]{1,0:T(8,128)(2,1)} async-done(((bf16[2048,256]{1,0:T(8,128)(2,1)}), bf16[512,256]{1,0:T(8,128)(2,1)}) %reduce-scatter.26.cloned.1.call-update) | async-done | bytes 262160 | tf_op jit(solution)/shard_map/reduce_scatter | solution.py:352
  1937.1 29.1 %reduce-scatter.28.cloned.1.call-done = bf16[512,256]{1,0:T(8,128)(2,1)} async-done(((bf16[2048,256]{1,0:T(8,128)(2,1)}), bf16[512,256]{1,0:T(8,128)(2,1)}) %reduce-scatter.28.cloned.1.call-update) | async-done | bytes 262160 | tf_op jit(solution)/shard_map/reduce_scatter | solution.py:355
  1968.0 28.7 %reduce-scatter.32.cloned.1.call-done = bf16[256,512]{1,0:T(8,128)(2,1)} async-done(((bf16[256,2048]{1,0:T(8,128)(2,1)}), bf16[256,512]{1,0:T(8,128)(2,1)}) %reduce-scatter.32.cloned.1.call-update) | async-done | bytes 262160 | tf_op jit(solution)/shard_map/reduce_scatter | solution.py:364
  1998.5 29.1 %reduce-scatter.30.cloned.1.call-done = bf16[512,256]{1,0:T(8,128)(2,1)} async-done(((bf16[2048,256]{1,0:T(8,128)(2,1)}), bf16[512,256]{1,0:T(8,128)(2,1)}) %reduce-scatter.30.cloned.1.call-update) | async-done | bytes 262160 | tf_op jit(solution)/shard_map/reduce_scatter | solution.py:358
  2029.6 39.8 %all-reduce.13 = (f32[2048]{0:T(1024)}, f32[128]{0:T(128)}, f32[2048]{0:T(1024)}) all-reduce(f32[2048]{0:T(1024)S(1)} %dynamic_update_slice.66, f32[128]{0:T(128)S(1)} %get-tuple-element.657, f32[2048]{0:T(1024)S(1)} %dynamic_update_slice.68), channel_id=1, replica_groups=mesh['shard'=4,'head'=4,'tensor'=2] {'shard','head','tensor'}, use_global_device_ids=true, to_apply=%region_40.41 | all-reduce | flops 4224 | bytes 33792 | tf_op jit(solution)/shard_map/psum | solution.py:345
  2078.8 75.5 %all-reduce.16.cloned.1.call-done = f32[4,3,2048]{2,0,1:T(4,128)} async-done(((f32[4,3,2048]{2,0,1:T(4,128)}), f32[4,3,2048]{2,0,1:T(4,128)}) %all-reduce.16.cloned.1.call-update) | async-done | bytes 98320 | tf_op jit(solution)/shard_map/psum | solution.py:345
  (743 shorter events, 861.2 us)
Async XLA Ops:
  20.8 14.8 all-to-all-start
  25.9 71.9 %all-gather.13.cloned.1.call-start = ((), (), s32[]{:S(2)}) async-start(), calls=%async_computation.15 | async-start | bytes 5898240 | tf_op jit(solution)/shard_map/all_gather | solution.py:145
  27.5 158.5 %copy-start.54 = (f32[1280]{0:T(1024)}, f32[1280]{0:T(1024)S(1)}, u32[]{:S(2)}) copy-start(f32[1280]{0:T(1024)S(1)} %get-tuple-element.757) | copy-start | bytes 15364
  27.5 158.5 %copy-start.56 = (f32[1280]{0:T(1024)}, f32[1280]{0:T(1024)S(1)}, u32[]{:S(2)}) copy-start(f32[1280]{0:T(1024)S(1)} %get-tuple-element.758) | copy-start | bytes 15364
  27.5 715.6 %copy-start.64 = (pred[1280]{0:T(1024)(128)(4,1)}, pred[1280]{0:T(1024)(128)(4,1)S(1)}, u32[]{:S(2)}) copy-start(pred[1280]{0:T(1024)(128)(4,1)S(1)} %get-tuple-element.761) | copy-start | bytes 3844
  40.8 83.6 %all-gather.19.cloned.1.call-start = ((), (), s32[]{:S(2)}) async-start(), calls=%async_computation.18 | async-start | bytes 1310720 | tf_op jit(solution)/shard_map/all_gather | solution.py:230
  41.6 111.4 %all-gather.17.cloned.1.call-start = ((), (), s32[]{:S(2)}) async-start(), calls=%async_computation.17 | async-start | bytes 1310720 | tf_op jit(solution)/shard_map/all_gather | solution.py:229
  42.3 139.0 %all-gather.15.cloned.1.call-start = ((), (), s32[]{:S(2)}) async-start(), calls=%async_computation.16 | async-start | bytes 1310720 | tf_op jit(solution)/shard_map/all_gather | solution.py:228
  42.9 573.2 %all-gather.21.cloned.1.call-start = ((), (), s32[]{:S(2)}) async-start(), calls=%async_computation.19 | async-start | bytes 1310720 | tf_op jit(solution)/shard_map/all_gather | solution.py:231
  43.5 583.1 %all-gather.23.cloned.1.call-start = ((), (), s32[]{:S(2)}) async-start(), calls=%async_computation.20 | async-start | bytes 1310720 | tf_op jit(solution)/shard_map/all_gather | solution.py:233
  44.1 699.1 %reduce-scatter.16.cloned.1.call-start = ((), (), s32[]{:S(2)}) async-start(), calls=%async_computation.21 | async-start | bytes 11796480 | tf_op jit(solution)/shard_map/reduce_scatter | solution.py:149
  52.7 162.6 %copy-start.62 = (bf16[2048,2]{0,1:T(2,128)(2,1)}, bf16[2048,2]{0,1:T(2,128)(2,1)S(1)}, u32[]{:S(2)}) copy-start(bf16[2048,2]{0,1:T(2,128)(2,1)S(1)} %all_gather.43) | copy-start | bytes 24580
  633.6 167.2 %all-gather.25.cloned.1.call-start = ((), (), s32[]{:S(2)}) async-start(), calls=%async_computation.22 | async-start | bytes 5898240 | tf_op jit(solution)/shard_map/all_gather | solution.py:145
  745.7 96.7 %all-gather.29.cloned.1.call-start = ((), (), s32[]{:S(2)}) async-start(), calls=%async_computation.24 | async-start | bytes 3604480 | tf_op jit(solution)/shard_map/all_gather | solution.py:235
  746.5 139.4 %all-gather.27.cloned.1.call-start = ((), (), s32[]{:S(2)}) async-start(), calls=%async_computation.23 | async-start | bytes 3604480 | tf_op jit(solution)/shard_map/all_gather | solution.py:234
  747.1 182.3 %all-gather.31.cloned.1.call-start = ((), (), s32[]{:S(2)}) async-start(), calls=%async_computation.25 | async-start | bytes 3604480 | tf_op jit(solution)/shard_map/all_gather | solution.py:236
  747.8 239.6 %all-gather.33.cloned.1.call-start = ((), (), s32[]{:S(2)}) async-start(), calls=%async_computation.27 | async-start | bytes 5898240 | tf_op jit(solution)/shard_map/all_gather | solution.py:145
  748.4 370.4 %reduce-scatter.20.cloned.1.call-start = ((), (), s32[]{:S(2)}) async-start(), calls=%async_computation.28 | async-start | bytes 11796480 | tf_op jit(solution)/shard_map/reduce_scatter | solution.py:149
  1011.0 182.3 %all-gather.35.cloned.1.call-start = ((), (), s32[]{:S(2)}) async-start(), calls=%async_computation.29 | async-start | bytes 5898240 | tf_op jit(solution)/shard_map/all_gather | solution.py:145
  1138.4 519.3 %reduce-scatter.18.cloned.1.call-start = ((), (), s32[]{:S(2)}) async-start(), calls=%async_computation.26 | async-start | bytes 11796480 | tf_op jit(solution)/shard_map/reduce_scatter | solution.py:149
  1157.8 547.8 %reduce-scatter.22.cloned.1.call-start = ((), (), s32[]{:S(2)}) async-start(), calls=%async_computation.30 | async-start | bytes 11796480 | tf_op jit(solution)/shard_map/reduce_scatter | solution.py:149
  1597.7 158.1 %reduce-scatter.34.cloned.1.call-start = ((), (), s32[]{:S(2)}) async-start(), calls=%async_computation.37 | async-start | bytes 3604480 | tf_op jit(solution)/shard_map/reduce_scatter | solution.py:367
  1606.8 193.6 %reduce-scatter.36.cloned.1.call-start = ((), (), s32[]{:S(2)}) async-start(), calls=%async_computation.38 | async-start | bytes 3604480 | tf_op jit(solution)/shard_map/reduce_scatter | solution.py:370
  1615.5 229.7 %reduce-scatter.38.cloned.1.call-start = ((), (), s32[]{:S(2)}) async-start(), calls=%async_computation.39 | async-start | bytes 3604480 | tf_op jit(solution)/shard_map/reduce_scatter | solution.py:373
  1624.2 249.0 %reduce-scatter.40.cloned.1.call-start = ((), (), s32[]{:S(2)}) async-start(), calls=%async_computation.40 | async-start | bytes 655360
  1630.0 274.6 %reduce-scatter.24.cloned.1.call-start = ((), (), s32[]{:S(2)}) async-start(), calls=%async_computation.31 | async-start | bytes 1310720 | tf_op jit(solution)/shard_map/reduce_scatter | solution.py:349
  1635.7 299.6 %reduce-scatter.26.cloned.1.call-start = ((), (), s32[]{:S(2)}) async-start(), calls=%async_computation.32 | async-start | bytes 1310720 | tf_op jit(solution)/shard_map/reduce_scatter | solution.py:352
  1640.8 325.4 %reduce-scatter.28.cloned.1.call-start = ((), (), s32[]{:S(2)}) async-start(), calls=%async_computation.33 | async-start | bytes 1310720 | tf_op jit(solution)/shard_map/reduce_scatter | solution.py:355
  1646.2 350.6 %reduce-scatter.32.cloned.1.call-start = ((), (), s32[]{:S(2)}) async-start(), calls=%async_computation.36 | async-start | bytes 1310720 | tf_op jit(solution)/shard_map/reduce_scatter | solution.py:364
  1651.5 376.1 %reduce-scatter.30.cloned.1.call-start = ((), (), s32[]{:S(2)}) async-start(), calls=%async_computation.34 | async-start | bytes 1310720 | tf_op jit(solution)/shard_map/reduce_scatter | solution.py:358
  1736.5 332.8 %all-to-all-start.1 = ((bf16[4,324,256]{2,1,0:T(8,128)(2,1)}), bf16[4,324,256]{2,1,0:T(8,128)(2,1)S(1)}, u32[]{:S(2)}, u32[]{:S(2)}) async-start(bf16[4,324,256]{2,1,0:T(8,128)(2,1)} %convert_element_type.202), calls=%async_computation.5 | async-start | bytes 1343488 | tf_op jit(solution)/shard_map/all_to_all | solution.py:326
  1740.3 413.9 %all-reduce.16.cloned.1.call-start = ((), (), s32[]{:S(2)}) async-start(), calls=%async_computation.35 | async-start | bytes 196608 | tf_op jit(solution)/shard_map/psum | solution.py:345
  (88 other events, 1762.8 us)
Sparse Core Ops, SparseCore 0:
  41.0 56.7 all-gather.12
  99.6 24.8 all-gather.18
  126.3 26.6 all-gather.16
  154.7 26.6 all-gather.14
  183.0 26.6 all-gather.20
  211.4 27.2 all-gather.22
  633.7 109.3 reduce-scatter.15
  745.9 54.8 all-gather.24
  802.6 39.8 all-gather.28
  844.1 41.6 all-gather.26
  887.7 41.6 all-gather.30
  930.8 56.5 all-gather.32
  1011.1 107.5 reduce-scatter.19
  1138.5 54.7 all-gather.34
  1195.4 107.5 reduce-scatter.17
  1597.8 107.7 reduce-scatter.21
  1708.5 47.2 reduce-scatter.33
  1758.7 41.6 reduce-scatter.35
  1803.4 41.7 reduce-scatter.37
  1848.4 24.7 reduce-scatter.39
  1876.9 27.6 reduce-scatter.23
  1907.5 27.7 reduce-scatter.25
  1938.5 27.7 reduce-scatter.27
  1969.0 27.7 reduce-scatter.31
  1999.9 27.7 reduce-scatter.29
  2033.6 120.5 all-reduce.15
where the time goes:
time: 2180 us; the launch traced here: 2160 us
  waiting for transfers between devices  989 us (45%)
  matrix products  617 us (28%)
  other arithmetic  321 us (15%)
  local copies, waits for them, and re-layouts  132 us (6%)
  blocking collectives  75.9 us (3%)
    reduce_scatter x4, waiting for transfers between devices, shares(): lax.psum_scatter(partial_sum, ('head', 'tensor'), scatter_dimension=1, ti...  265 us
    another operation x5, other arithmetic, delta_rule(): lax.linalg.triangular_solve(system, jnp.broadcast_to(identity, system.sha...  200 us
    all_gather x4, waiting for transfers between devices, full_rows(): return lax.all_gather(piece_in, ('head', 'tensor'), axis=1, tiled=True)  190 us
    dot_general x60, matrix products, advance(): jnp.einsum('hid,hde->hie', w_part, memory, precision=HIGHEST)  123 us
    dot_general x60, matrix products, advance(): jnp.einsum('hij,hje->hie', s_part, fresh_vals, precision=HIGHEST)  104 us
    dot_general x60, matrix products, advance(): jnp.einsum('hid,hde->hie', q_part, memory, precision=HIGHEST)  98.7 us
    psum x1, waiting for transfers between devices, body(): lax.psum((mixer_gain_full, conv_full, d_gain_heads_part, ffn_gain_full),...  75.5 us
    dot_general x60, matrix products, advance(): jnp.einsum('hid,hie->hde', k_part, fresh_vals, precision=HIGHEST)  62.3 us
  transfers between devices with their start and end apart: 28, of which 24 were waited for; matrix products, arithmetic and copies ran while one was open for 46% of the time, Pallas kernels for 0%

commit v1 on v0

v1 whole, which is shorter than its diff:
```python
import functools
import jax
import jax.numpy as jnp
from jax import lax
from jax.experimental import pallas as pl
from jax.experimental.pallas import tpu as pltpu

from jax.sharding import PartitionSpec as P

D = 2048
HD = 128
CONV = 4
BLOCK = 64
SEQ_DEV = 4
REAL_DEV = 1152
CAP = 1280
NB = CAP // BLOCK
EPSILON = 1e-06
HEAD_FLOOR = 0.01
F32 = jnp.float32
BF = jnp.bfloat16

def split(x):
    hi = x.astype(BF)
    return hi, (x - hi.astype(F32)).astype(BF)

NN=(((1,),(0,)),((),())); NT=(((1,),(1,)),((),())); TN=(((0,),(0,)),((),()))

def dg(a, b, dims):
    return lax.dot_general(a, b, dims, preferred_element_type=F32)

def d3(a, b, dims=NN):
    ah, al = split(a); bh, bl = split(b)
    return dg(ah, bh, dims) + (dg(ah, bl, dims) + dg(al, bh, dims))

def masks():
    ri = lax.broadcasted_iota(jnp.int32, (BLOCK, BLOCK), 0)
    ci = lax.broadcasted_iota(jnp.int32, (BLOCK, BLOCK), 1)
    return ri, ci

def sigmoid(x):
    return 1.0 / (1.0 + jnp.exp(-x))

def conv_rows(cur, tail, wt, pos):
    ext = jnp.concatenate([tail, cur], axis=0)
    out = wt[0] * cur
    for j in range(1, CONV):
        sh = pltpu.roll(ext, j, axis=0)[8:]
        out = out + wt[j] * jnp.where(pos >= j, sh, 0.0)
    return out

def inverses(lmats, ri, ci):
    apart = ri ^ ci
    xs = [jnp.where(apart == 0, 1.0, 0.0) - jnp.where(apart == 1, m, 0.0) for m in lmats]
    s = 2
    while s < BLOCK:
        at = (apart >= s) & (apart < 2 * s)
        ys = [d3(x, jnp.where(at, m, 0.0)) for x, m in zip(xs, lmats)]
        xs = [x - d3(y, x) for x, y in zip(xs, ys)]
        s *= 2
    return xs

def fwd_kernel(persist, pre, pos_ref, fill_ref, cw, gain, mixed, c_out, qk, w_out, u_out, u2_out, o_out, p_out, t_out, m_out, s_out, b_s):
    ri, ci = masks()
    heads = 2
    def phase_a(n, tails):
        r = pl.ds(pl.multiple_of(n * BLOCK, BLOCK), BLOCK)
        pos = pos_ref[r, :]; fil = fill_ref[r, :]
        new_tails = []
        acts = []
        for i in range(3):
            cur = pre[r, i*256:(i+1)*256]
            wt = [cw[j*3+i:j*3+i+1, :] for j in range(CONV)]
            cc = conv_rows(cur, tails[i], wt, pos)
            c_out[r, i*256:(i+1)*256] = cc
            acts.append(cc * sigmoid(cc) * fil)
            new_tails.append(cur[BLOCK-8:])
        beta = sigmoid(pre[r, 1024:1152])
        for h in range(heads):
            hs = slice(h*HD, (h+1)*HD)
            yq = acts[0][:, hs]; yk = acts[1][:, hs]; v = acts[2][:, hs]
            q = yq * lax.rsqrt(jnp.sum(yq*yq, axis=1, keepdims=True) + EPSILON)
            k = yk * lax.rsqrt(jnp.sum(yk*yk, axis=1, keepdims=True) + EPSILON)
            b = beta[:, h:h+1]
            qk[r, h*HD:(h+1)*HD] = q
            qk[r, 256+h*HD:256+(h+1)*HD] = k
            lmat = jnp.where(ri > ci, b * d3(k, k, NT), 0.0)
            p_out[n*2+h] = jnp.where(ri >= ci, d3(q, k, NT), 0.0)
            t_out[n*2+h] = lmat
            u_out[r, hs] = b*v
            w_out[r, hs] = b*k
        return tuple(new_tails)
    z8 = jnp.zeros((8, 256), F32)
    lax.fori_loop(0, NB, phase_a, (z8, z8, z8))
    GRP = 8
    def phase_t(i, _):
        ts = inverses([t_out[i*GRP+j] for j in range(GRP)], ri, ci)
        for j in range(GRP):
            t_out[i*GRP+j] = ts[j]
        return 0
    lax.fori_loop(0, 2*NB//GRP, phase_t, 0)
    def phase_w(i, _):
        for jj in range(2):
            n = i*2+jj
            r = pl.ds(pl.multiple_of(n * BLOCK, BLOCK), BLOCK)
            for h in range(heads):
                hs = slice(h*HD, (h+1)*HD)
                e = n*2+h
                wu = d3(t_out[e], jnp.concatenate([w_out[r, hs], u_out[r, hs]], axis=1))
                mb = d3(qk[r, 256+h*HD:256+(h+1)*HD], wu, TN)
                w_out[r, hs] = wu[:, :HD]; u_out[r, hs] = wu[:, HD:]
                m_out[e] = mb[:, :HD]; b_s[e] = mb[:, HD:]
        return 0
    lax.fori_loop(0, NB//2, phase_w, 0)
    def phase_b(n, ss):
        out = []
        for h in range(heads):
            e = n*2+h
            s = ss[h] * persist[n]
            s_out[e] = s
            out.append(s - d3(m_out[e], s) + b_s[e])
        return tuple(out)
    zs = jnp.zeros((HD, HD), F32)
    lax.fori_loop(0, NB, phase_b, (zs, zs))
    def phase_c(n, _):
        r = pl.ds(pl.multiple_of(n * BLOCK, BLOCK), BLOCK)
        for h in range(heads):
            hs = slice(h*HD, (h+1)*HD)
            e = n*2+h
            wq = jnp.concatenate([w_out[r, hs], qk[r, hs]], axis=0)
            rr = d3(wq, s_out[e])
            u2 = u_out[r, hs] - rr[:BLOCK]
            o = rr[BLOCK:] + d3(p_out[e], u2)
            u2_out[r, hs] = u2
            o_out[r, hs] = o
            ms = jnp.mean(o*o, axis=1, keepdims=True)
            sc = lax.rsqrt(jnp.maximum(ms, HEAD_FLOOR))
            gg = pre[r, 768+h*HD:768+(h+1)*HD]
            mixed[r, hs] = (o * sc * gain[...] * (gg * sigmoid(gg))).astype(BF)
        return 0
    lax.fori_loop(0, NB, phase_c, 0)

def sds(*s, dt=F32): return jax.ShapeDtypeStruct(s, dt)
VM = pl.BlockSpec(memory_space=pltpu.VMEM)
SM = pl.BlockSpec(memory_space=pltpu.SMEM)

def mixer_fwd(persist, pre, pos, fil, cw, gain):
    outs = (sds(CAP,256,dt=BF), sds(CAP,768), sds(CAP,512), sds(CAP,256), sds(CAP,256), sds(CAP,256), sds(CAP,256),
            sds(2*NB,BLOCK,BLOCK), sds(2*NB,BLOCK,BLOCK), sds(2*NB,HD,HD), sds(2*NB,HD,HD))
    return pl.pallas_call(fwd_kernel, out_shape=outs, in_specs=[SM]+[VM]*5, out_specs=[VM]*len(outs),
        scratch_shapes=[pltpu.VMEM((2*NB,HD,HD),F32)],
        compiler_params=pltpu.CompilerParams(vmem_limit_bytes=56*2**20), cost_estimate=pl.CostEstimate(flops=0, bytes_accessed=140 * 2**20, transcendentals=0),
        name="mixer_forward")(persist, pre, pos, fil, cw, gain)

def bwd_kernel(persist, dmix, pre, pos_ref, fill_ref, cw, gain, c_in, qk, w_in, u_in, u2_in, o_in, p_in, t_in, m_in, s_in,
               dpre, dcw, dgain, e_s, do_s):
    ri, ci = masks()
    heads = 2
    lane = lax.broadcasted_iota(jnp.int32, (BLOCK, HD), 1)
    dgain[...] = jnp.zeros_like(dgain)
    dcw[...] = jnp.zeros_like(dcw)
    def phase_a(n, _):
        r = pl.ds(pl.multiple_of(n * BLOCK, BLOCK), BLOCK)
        for h in range(heads):
            hs = slice(h*HD, (h+1)*HD)
            e = n*2+h
            o = o_in[r, hs]; dm = dmix[r, hs]
            gg = pre[r, 768+h*HD:768+(h+1)*HD]
            sg = sigmoid(gg); si = gg*sg
            ms = jnp.mean(o*o, axis=1, keepdims=True)
            sc = lax.rsqrt(jnp.maximum(ms, HEAD_FLOOR))
            on = o*sc
            gn = gain[...]
            dpre[r, 768+h*HD:768+(h+1)*HD] = (dm * on * gn * (sg * (1.0 + gg*(1.0-sg)))).astype(BF)
            dgs = dm * on * si
            dgain[...] += jnp.sum(dgs.reshape(8, 8, HD), axis=0)
            dn = dm * gn * si
            corr = jnp.where(ms > HEAD_FLOOR, jnp.mean(dn*on, axis=1, keepdims=True), 0.0)
            do = sc * (dn - on*corr)
            do_s[r, hs] = do
            pdo = d3(p_in[e], do, TN)
            qw = jnp.concatenate([qk[r, hs], w_in[r, hs]], axis=0)
            dd = jnp.concatenate([do, -pdo], axis=0)
            e_s[e] = d3(qw, dd, TN)
        return 0
    lax.fori_loop(0, NB, phase_a, 0)
    def phase_b(i, ds):
        n = NB-1-i
        out = []
        for h in range(heads):
            e = n*2+h
            d = ds[h]
            ee = e_s[e]
            e_s[e] = d
            out.append((d - d3(m_in[e], d, TN) + ee) * persist[n])
        return tuple(out)
    zs = jnp.zeros((HD, HD), F32)
    lax.fori_loop(0, NB, phase_b, (zs, zs))
    def phase_c(i, heads_dc):
        n = NB-1-i
        r = pl.ds(pl.multiple_of(n * BLOCK, BLOCK), BLOCK)
        pos = pos_ref[r, :]; fil = fill_ref[r, :]
        beta_t = sigmoid(pre[r, 1024:1152])
        dacts = [[], [], []]
        dbt = jnp.zeros((BLOCK, HD), F32)
        for h in range(heads):
            hs = slice(h*HD, (h+1)*HD)
            e = n*2+h
            q = qk[r, hs]; k = qk[r, 256+h*HD:256+(h+1)*HD]
            w = w_in[r, hs]; u = u_in[r, hs]; u2 = u2_in[r, hs]
            do = do_s[r, hs]; p = p_in[e]; t = t_in[e]; s = s_in[e]; ds = e_s[e]
            cv = c_in[r, 512+h*HD:512+(h+1)*HD]
            v = cv * sigmoid(cv) * fil
            b = beta_t[:, h:h+1]
            du2 = d3(p, do, TN) + d3(k, ds)
            dp = jnp.where(ri >= ci, d3(do, u2, NT), 0.0)
            xs = d3(jnp.concatenate([do, -du2], axis=0), s, NT)
            dq = xs[:BLOCK] + d3(dp, k)
            dw = xs[BLOCK:]
            dk = d3(dp, q, TN) + d3(u2, ds, NT)
            xx = d3(t, jnp.concatenate([dw, du2], axis=1), TN)
            xw = xx[:, :HD]; xu = xx[:, HD:]
            wu = jnp.concatenate([w, u], axis=1)
            mm = jnp.where(ri > ci, -d3(xx, wu, NT), 0.0)
            g = d3(k, k, NT)
            db = jnp.sum(mm*g, axis=1, keepdims=True)
            bm = b*mm
            dk = dk + d3(bm + bm.T, k) + b*xw
            db = db + jnp.sum(xw*k + xu*v, axis=1, keepdims=True)
            dv = b*xu
            dbt = jnp.where(lane == h, db, dbt)
            cq = c_in[r, hs]; ck = c_in[r, 256+h*HD:256+(h+1)*HD]
            sq = sigmoid(cq); sk = sigmoid(ck); sv = sigmoid(cv)
            yq = cq*sq*fil; yk = ck*sk*fil
            rq = lax.rsqrt(jnp.sum(yq*yq, axis=1, keepdims=True) + EPSILON)
            rk = lax.rsqrt(jnp.sum(yk*yk, axis=1, keepdims=True) + EPSILON)
            dyq = rq*(dq - q*jnp.sum(dq*q, axis=1, keepdims=True))
            dyk = rk*(dk - k*jnp.sum(dk*k, axis=1, keepdims=True))
            dacts[0].append(dyq*fil*(sq*(1.0+cq*(1.0-sq))))
            dacts[1].append(dyk*fil*(sk*(1.0+ck*(1.0-sk))))
            dacts[2].append(dv*fil*(sv*(1.0+cv*(1.0-sv))))
        dpre[r, 1024:1152] = (dbt*beta_t*(1.0-beta_t)).astype(BF)
        nxt = jnp.minimum(n+1, NB-1)
        posx = jnp.concatenate([pos, pos_ref[pl.ds(pl.multiple_of(nxt*BLOCK, BLOCK), 8), :]], axis=0)
        prv = jnp.maximum(n*BLOCK-8, 0)
        new = []
        for i in range(3):
            dc = jnp.concatenate(dacts[i], axis=1)
            ext = jnp.concatenate([dc, heads_dc[i]], axis=0)
            cur = pre[r, i*256:(i+1)*256]
            tail = pre[pl.ds(pl.multiple_of(prv, 8), 8), i*256:(i+1)*256]
            xext = jnp.concatenate([tail, cur], axis=0)
            dx = cw[i:i+1, :]*dc
            dcw[i] += jnp.sum((dc*cur).reshape(8, 8, 256), axis=0)
            for j in range(1, CONV):
                z = jnp.where(posx >= j, ext, 0.0)
                dx = dx + cw[j*3+i:j*3+i+1, :]*pltpu.roll(z, BLOCK+8-j, axis=0)[:BLOCK]
                sh = pltpu.roll(xext, j, axis=0)[8:]
                dcw[j*3+i] += jnp.sum(jnp.where(pos >= j, dc*sh, 0.0).reshape(8, 8, 256), axis=0)
            dpre[r, i*256:(i+1)*256] = dx.astype(BF)
            new.append(dc[:8])
        return tuple(new)
    z8 = jnp.zeros((8, 256), F32)
    lax.fori_loop(0, NB, phase_c, (z8, z8, z8))

def mixer_bwd(persist, dmix, pre, pos, fil, cw, gain, saved):
    outs = (sds(CAP,1152,dt=BF), sds(12,8,256), sds(8,HD))
    return pl.pallas_call(bwd_kernel, out_shape=outs, in_specs=[SM]+[VM]*(6+len(saved)), out_specs=[VM]*3,
        scratch_shapes=[pltpu.VMEM((2*NB,HD,HD),F32), pltpu.VMEM((CAP,256),F32)],
        compiler_params=pltpu.CompilerParams(vmem_limit_bytes=58*2**20), cost_estimate=pl.CostEstimate(flops=0, bytes_accessed=200 * 2**20, transcendentals=0),
        name="mixer_backward")(persist, dmix, pre, pos, fil, cw, gain, *saved)


MESH = pl.DeviceIdType.MESH
LINK_COST = 150 * 2**20
HBM = pl.BlockSpec(memory_space=pltpu.HBM)


def places():
    s, h, t = lax.axis_index("shard"), lax.axis_index("head"), lax.axis_index("tensor")
    return h, t, (s, h + 1, t), (s, h - 1, t), (s, h, 1 - t)


def shard_peers(m):
    s, h, t = lax.axis_index("shard"), lax.axis_index("head"), lax.axis_index("tensor")
    return [((lax.rem(s + i, m), h, t), lax.rem(s + i, m)) for i in range(1, m)]


class Carry:
    def __init__(self, kinds, m, ins, outs, send, recv, here):
        self.kinds, self.m, self.ins, self.outs = kinds, m, ins, outs
        self.send, self.recv, self.here = send, recv, here
        self.me = lax.axis_index("shard")

    def part(self, e, src):
        if self.kinds[e] == "gather":
            rows = self.ins[e].shape[0]
            return self.outs[e].at[pl.ds(pl.multiple_of(src * rows, rows), rows)]
        return self.outs[e].at[src]

    def given(self, e, dst):
        if self.kinds[e] == "columns":
            w = self.ins[e].shape[1] // self.m
            return self.ins[e].at[:, pl.ds(pl.multiple_of(dst * w, w), w)]
        return self.ins[e] if self.kinds[e] == "gather" else self.ins[e].at[dst]

    def copy(self, e, i, p):
        return pltpu.make_async_remote_copy(src_ref=self.given(e, p[1]), dst_ref=self.part(e, self.me), send_sem=self.send.at[e, i],
                                            recv_sem=self.recv.at[e, self.me], device_id=p[0], device_id_type=MESH)

    def local(self, e):
        return pltpu.make_async_copy(self.given(e, self.me), self.part(e, self.me), self.here.at[e])

    def greet(self):
        barrier = pltpu.get_barrier_semaphore()
        if self.kinds:
            for p, _ in shard_peers(self.m):
                pl.semaphore_signal(barrier, inc=1, device_id=p, device_id_type=MESH)
        return self.m - 1 if self.kinds else 0

    def start(self):
        for e in range(len(self.kinds)):
            for i, p in enumerate(shard_peers(self.m)):
                self.copy(e, i, p).start()
            self.local(e).start()

    def wait(self):
        for e in range(len(self.kinds)):
            self.local(e).wait()
            for i, p in enumerate(shard_peers(self.m)):
                self.copy(e, i, p).wait_send()
                pltpu.make_async_remote_copy(src_ref=self.given(e, p[1]), dst_ref=self.part(e, p[1]), send_sem=self.send.at[e, i],
                                             recv_sem=self.recv.at[e, p[1]], device_id=p[0], device_id_type=MESH).wait_recv()


def carried(kinds, m, arrays):
    dma = pltpu.SemaphoreType.DMA
    give = {"gather": lambda a: (m * a.shape[0], a.shape[1]), "swap": lambda a: a.shape,
            "columns": lambda a: (m, a.shape[0], a.shape[1] // m)}
    shapes = [jax.ShapeDtypeStruct(give[k](a), a.dtype) for k, a in zip(kinds, arrays)]
    e = len(kinds)
    return shapes, ([dma((e, m)), dma((e, m)), dma((e,))] if e else [])


def carry_of(kinds, m, refs, n_in, n_out):
    e = len(kinds)
    ins, refs = refs[:n_in], refs[n_in:]
    c_in, refs = refs[:e], refs[e:]
    outs, refs = refs[:n_out], refs[n_out:]
    c_out, refs = refs[:e], refs[e:]
    sems = (refs[-3:] if e else (None,) * 3)
    scratch = refs[:-3] if e else refs
    return ins, outs, scratch, Carry(kinds, m, c_in, c_out, *sems)


def greet(n, h, up, down, across, more=0):
    barrier = pltpu.get_barrier_semaphore()
    pl.semaphore_signal(barrier, inc=1, device_id=across, device_id_type=MESH)

    @pl.when(h < n - 1)
    def _():
        pl.semaphore_signal(barrier, inc=1, device_id=up, device_id_type=MESH)

    @pl.when(h > 0)
    def _():
        pl.semaphore_signal(barrier, inc=1, device_id=down, device_id_type=MESH)

    pl.semaphore_wait(barrier, 1 + more + (h < n - 1).astype(jnp.int32) + (h > 0).astype(jnp.int32))


def gather_kernel(n, width, m, kinds, *refs):
    (x,), (out,), (here, up_s, up_r, down_s, down_r, core_s, core_r), carry = carry_of(kinds, m, refs, 1, 1)
    h, t, up, down, across = places()

    def cols(j):
        return out.at[:, pl.ds(pl.multiple_of((j * 2 + t) * width, width), width)]

    def other(j):
        return out.at[:, pl.ds(pl.multiple_of((j * 2 + 1 - t) * width, width), width)]

    def send(j, src, ss, rs, to):
        return pltpu.make_async_remote_copy(src_ref=src, dst_ref=cols(j), send_sem=ss.at[j], recv_sem=rs.at[j],
                                            device_id=to, device_id_type=MESH)

    greet(n, h, up, down, across, carry.greet())
    local = pltpu.make_async_copy(x, cols(h), here)
    local.start()

    @pl.when(h < n - 1)
    def _():
        send(h, x, up_s, up_r, up).start()

    @pl.when(h > 0)
    def _():
        send(h, x, down_s, down_r, down).start()

    send(h, x, core_s, core_r, across).start()
    carry.start()
    for k in range(1, n):
        below, above = h - k, h + k

        @pl.when(below >= 0)
        def _():
            send(below, cols(below), up_s, up_r, up).wait_recv()

            @pl.when(h < n - 1)
            def _():
                send(below, cols(below), up_s, up_r, up).start()

            send(below, cols(below), core_s, core_r, across).start()

        @pl.when(above < n)
        def _():
            send(above, cols(above), down_s, down_r, down).wait_recv()

            @pl.when(h > 0)
            def _():
                send(above, cols(above), down_s, down_r, down).start()

            send(above, cols(above), core_s, core_r, across).start()

    for j in range(n):
        back = pltpu.make_async_remote_copy(src_ref=cols(j), dst_ref=other(j), send_sem=core_s.at[j], recv_sem=core_r.at[j],
                                            device_id=across, device_id_type=MESH)
        back.wait_recv()
        back.wait_send()

        @pl.when((j <= h) & (h < n - 1))
        def _():
            send(j, cols(j), up_s, up_r, up).wait_send()

        @pl.when((j >= h) & (h > 0))
        def _():
            send(j, cols(j), down_s, down_r, down).wait_send()

    local.wait()
    carry.wait()


def z_gather(n, piece, collective_id, name, m=1, kinds=(), arrays=()):
    rows, width = piece.shape
    dma = pltpu.SemaphoreType.DMA
    shapes, sems = carried(kinds, m, arrays)
    out = pl.pallas_call(
        functools.partial(gather_kernel, n, width, m, kinds),
        out_shape=[jax.ShapeDtypeStruct((rows, 2 * n * width), piece.dtype)] + shapes,
        in_specs=[HBM] * (1 + len(shapes)), out_specs=[HBM] * (1 + len(shapes)),
        scratch_shapes=[dma] + [dma((n,))] * 6 + sems,
        compiler_params=pltpu.CompilerParams(collective_id=collective_id, has_side_effects=True),
        cost_estimate=pl.CostEstimate(flops=0, bytes_accessed=LINK_COST, transcendentals=0),
        name=name,
    )(piece, *arrays)
    return out if kinds else out[0]


STEP = 128


def group_peers(n):
    s, h, t = lax.axis_index("shard"), lax.axis_index("head"), lax.axis_index("tensor")
    peers = []
    for i in range(1, 2 * n):
        hh, tt = lax.rem(h + i // 2, n), lax.rem(t + i % 2, 2)
        peers.append(((s, hh, tt), hh * 2 + tt))
    return peers


def greet_group(n, more=0):
    barrier = pltpu.get_barrier_semaphore()
    for p, _ in group_peers(n):
        pl.semaphore_signal(barrier, inc=1, device_id=p, device_id_type=MESH)
    pl.semaphore_wait(barrier, 2 * n - 1 + more)


def scatter_kernel(n, width, m, kinds, *refs):
    (part,), (out,), scratch, carry = carry_of(kinds, m, refs, 1, 1)
    mine, theirs, from_below, from_above, here, core_s, core_r, up_s, up_r, down_s, down_r = scratch
    h, t, up, down, across = places()

    def cols(j, c):
        return part.at[:, pl.ds(pl.multiple_of((j * 2 + c) * width, width), width)]

    def swap(j):
        return pltpu.make_async_remote_copy(src_ref=cols(j, 1 - t), dst_ref=theirs.at[j], send_sem=core_s.at[j],
                                            recv_sem=core_r.at[j], device_id=across, device_id_type=MESH)

    def own(j):
        return pltpu.make_async_copy(cols(j, t), mine.at[j], here.at[j])

    def rise(k):
        return pltpu.make_async_remote_copy(src_ref=mine.at[n - 1 - k], dst_ref=from_below.at[k], send_sem=up_s.at[k],
                                            recv_sem=up_r.at[k], device_id=up, device_id_type=MESH)

    def fall(k):
        return pltpu.make_async_remote_copy(src_ref=mine.at[k], dst_ref=from_above.at[k], send_sem=down_s.at[k],
                                            recv_sem=down_r.at[k], device_id=down, device_id_type=MESH)

    def total(j, extra):
        def step(i, c):
            r = pl.ds(pl.multiple_of(i * STEP, STEP), STEP)
            v = mine[j, r, :].astype(F32) + theirs[j, r, :].astype(F32)
            if extra is not None:
                v = v + extra(r).astype(F32)
            mine[j, r, :] = v.astype(BF)
            return c
        lax.fori_loop(0, CAP // STEP, step, 0)

    order = [j for i in range(n // 2) for j in (n - 1 - i, i)]
    for j in order:
        own(j).start()
    greet(n, h, up, down, across, carry.greet())
    for j in order:
        swap(j).start()
    carry.start()

    def arrive(j):
        own(j).wait()
        swap(j).wait_recv()

    for tick in range(2 * n - 2):
        ku = tick - h
        tu = n - 1 - ku

        @pl.when((ku >= 0) & (tu > h))
        def _():
            arrive(tu)

            @pl.when(h == 0)
            def _():
                total(tu, None)

            @pl.when(h > 0)
            def _():
                rise(ku).wait_recv()
                total(tu, lambda r: from_below[ku, r, :])

            rise(ku).start()

        kd = tick - (n - 1 - h)

        @pl.when((kd >= 0) & (kd < h))
        def _():
            arrive(kd)

            @pl.when(h == n - 1)
            def _():
                total(kd, None)

            @pl.when(h < n - 1)
            def _():
                fall(kd).wait_recv()
                total(kd, lambda r: from_above[kd, r, :])

            fall(kd).start()

    arrive(h)

    def final(get):
        def step(i, c):
            r = pl.ds(pl.multiple_of(i * STEP, STEP), STEP)
            out[r, :] = get(r)
            return c
        lax.fori_loop(0, CAP // STEP, step, 0)

    final(lambda r: mine[h, r, :].astype(F32) + theirs[h, r, :].astype(F32))

    @pl.when(h > 0)
    def _():
        rise(n - 1 - h).wait_recv()
        final(lambda r: out[r, :] + from_below[n - 1 - h, r, :].astype(F32))

    @pl.when(h < n - 1)
    def _():
        fall(h).wait_recv()
        final(lambda r: out[r, :] + from_above[h, r, :].astype(F32))

    for j in range(n):
        swap(j).wait_send()
    for k in range(n - 1):
        @pl.when(n - 1 - k > h)
        def _():
            rise(k).wait_send()

        @pl.when(k < h)
        def _():
            fall(k).wait_send()
    carry.wait()


def z_scatter(n, part, collective_id, name, m=1, kinds=(), arrays=()):
    rows, width = part.shape[0], part.shape[1] // (2 * n)
    dma = pltpu.SemaphoreType.DMA
    shapes, sems = carried(kinds, m, arrays)
    out = pl.pallas_call(
        functools.partial(scatter_kernel, n, width, m, kinds),
        out_shape=[jax.ShapeDtypeStruct((rows, width), F32)] + shapes,
        in_specs=[HBM] * (1 + len(shapes)), out_specs=[VM] + [HBM] * len(shapes),
        scratch_shapes=[pltpu.VMEM((n, rows, width), BF)] * 2 + [pltpu.VMEM((n - 1, rows, width), BF)] * 2
        + [dma((n,))] * 3 + [dma((n - 1,))] * 4 + sems,
        compiler_params=pltpu.CompilerParams(collective_id=collective_id, has_side_effects=True, vmem_limit_bytes=32 * 2**20),
        cost_estimate=pl.CostEstimate(flops=0, bytes_accessed=LINK_COST, transcendentals=0),
        name=name,
    )(part, *arrays)
    return out if kinds else out[0]


def scatter_norm_kernel(n, width, m, kinds, *refs):
    (part, kept, scale, base, gain), (out, low, dgain), scratch, carry = carry_of(kinds, m, refs, 5, 3)
    (acc, tots, tot_s, tot_r, mine, theirs, from_below, from_above,
     here, core_s, core_r, up_s, up_r, down_s, down_r) = scratch
    h, t, up, down, across = places()

    def cols(j, c):
        return part.at[:, pl.ds(pl.multiple_of((j * 2 + c) * width, width), width)]

    def swap(j):
        return pltpu.make_async_remote_copy(src_ref=cols(j, 1 - t), dst_ref=theirs.at[j], send_sem=core_s.at[j],
                                            recv_sem=core_r.at[j], device_id=across, device_id_type=MESH)

    def own(j):
        return pltpu.make_async_copy(cols(j, t), mine.at[j], here.at[j])

    def rise(k):
        return pltpu.make_async_remote_copy(src_ref=mine.at[n - 1 - k], dst_ref=from_below.at[k], send_sem=up_s.at[k],
                                            recv_sem=up_r.at[k], device_id=up, device_id_type=MESH)

    def fall(k):
        return pltpu.make_async_remote_copy(src_ref=mine.at[k], dst_ref=from_above.at[k], send_sem=down_s.at[k],
                                            recv_sem=down_r.at[k], device_id=down, device_id_type=MESH)

    def total(j, extra):
        def step(i, c):
            r = pl.ds(pl.multiple_of(i * STEP, STEP), STEP)
            v = mine[j, r, :].astype(F32) + theirs[j, r, :].astype(F32)
            if extra is not None:
                v = v + extra(r).astype(F32)
            mine[j, r, :] = v.astype(BF)
            return c
        lax.fori_loop(0, CAP // STEP, step, 0)

    order = [j for i in range(n // 2) for j in (n - 1 - i, i)]
    for j in order:
        own(j).start()
    greet_group(n, carry.greet())
    for j in order:
        swap(j).start()
    carry.start()

    def arrive(j):
        own(j).wait()
        swap(j).wait_recv()

    for tick in range(2 * n - 2):
        ku = tick - h
        tu = n - 1 - ku

        @pl.when((ku >= 0) & (tu > h))
        def _():
            arrive(tu)

            @pl.when(h == 0)
            def _():
                total(tu, None)

            @pl.when(h > 0)
            def _():
                rise(ku).wait_recv()
                total(tu, lambda r: from_below[ku, r, :])

            rise(ku).start()

        kd = tick - (n - 1 - h)

        @pl.when((kd >= 0) & (kd < h))
        def _():
            arrive(kd)

            @pl.when(h == n - 1)
            def _():
                total(kd, None)

            @pl.when(h < n - 1)
            def _():
                fall(kd).wait_recv()
                total(kd, lambda r: from_above[kd, r, :])

            fall(kd).start()

    arrive(h)

    def final(get):
        def step(i, c):
            r = pl.ds(pl.multiple_of(i * STEP, STEP), STEP)
            acc[r, :] = get(r)
            return c
        lax.fori_loop(0, CAP // STEP, step, 0)

    final(lambda r: mine[h, r, :].astype(F32) + theirs[h, r, :].astype(F32))

    @pl.when(h > 0)
    def _():
        rise(n - 1 - h).wait_recv()
        final(lambda r: acc[r, :] + from_below[n - 1 - h, r, :].astype(F32))

    @pl.when(h < n - 1)
    def _():
        fall(h).wait_recv()
        final(lambda r: acc[r, :] + from_above[h, r, :].astype(F32))

    me = h * 2 + t
    gains = gain[...]
    ones = jnp.ones((8, width), BF)

    def share(i, c):
        r = pl.ds(pl.multiple_of(i * STEP, STEP), STEP)
        hi, lo = split(acc[r, :] * gains * kept[r, :].astype(F32))
        tots[me, :, r] = dg(ones, hi, NT) + dg(ones, lo, NT)
        return c
    lax.fori_loop(0, CAP // STEP, share, 0)
    peers = group_peers(n)
    sends = [pltpu.make_async_remote_copy(src_ref=tots.at[me], dst_ref=tots.at[me], send_sem=tot_s.at[i], recv_sem=tot_r.at[me],
                                          device_id=p[0], device_id_type=MESH) for i, p in enumerate(peers)]
    for c in sends:
        c.start()
    for i, p in enumerate(peers):
        pltpu.make_async_remote_copy(src_ref=tots.at[me], dst_ref=tots.at[p[1]], send_sem=tot_s.at[i], recv_sem=tot_r.at[p[1]],
                                     device_id=p[0], device_id_type=MESH).wait_recv()
    dgain[...] = jnp.zeros_like(dgain)
    eighth = jnp.full((8, 128), 0.125, BF)

    def close(i, c):
        r = pl.ds(pl.multiple_of(i * STEP, STEP), STEP)
        row = tots[0, :, r]
        for d in range(1, 2 * n):
            row = row + tots[d, :, r]
        hi, lo = split(row)
        total_r = dg(hi, eighth, TN) + dg(lo, eighth, TN)
        sc = scale[r, :]
        kp = kept[r, :].astype(F32)
        dn = acc[r, :]
        back = base[r, :].astype(F32) + sc * (gains * dn) - kp * jnp.tile((sc * sc * sc) * (total_r * (1.0 / D)), (1, width // 128))
        out[r, :] = back
        low[r, :] = back.astype(BF)
        dgain[...] += jnp.sum((dn * kp * sc).reshape(STEP // 8, 8, width), axis=0)
        return c
    lax.fori_loop(0, CAP // STEP, close, 0)
    for c in sends:
        c.wait_send()

    for j in range(n):
        swap(j).wait_send()
    for k in range(n - 1):
        @pl.when(n - 1 - k > h)
        def _():
            rise(k).wait_send()

        @pl.when(k < h)
        def _():
            fall(k).wait_send()
    carry.wait()


def z_scatter_norm(n, part, kept, scale, base, gain, collective_id, name, m=1, kinds=(), arrays=()):
    rows, width = part.shape[0], part.shape[1] // (2 * n)
    dma = pltpu.SemaphoreType.DMA
    shapes, sems = carried(kinds, m, arrays)
    return pl.pallas_call(
        functools.partial(scatter_norm_kernel, n, width, m, kinds),
        out_shape=[jax.ShapeDtypeStruct((rows, width), F32), jax.ShapeDtypeStruct((rows, width), BF),
                   jax.ShapeDtypeStruct((8, width), F32)] + shapes,
        in_specs=[HBM] + [VM] * 4 + [HBM] * len(shapes), out_specs=[VM] * 3 + [HBM] * len(shapes),
        scratch_shapes=[pltpu.VMEM((rows, width), F32), pltpu.VMEM((2 * n, 8, rows), F32), dma((2 * n,)), dma((2 * n,))]
        + [pltpu.VMEM((n, rows, width), BF)] * 2 + [pltpu.VMEM((n - 1, rows, width), BF)] * 2
        + [dma((n,))] * 3 + [dma((n - 1,))] * 4 + sems,
        compiler_params=pltpu.CompilerParams(collective_id=collective_id, has_side_effects=True, vmem_limit_bytes=40 * 2**20),
        cost_estimate=pl.CostEstimate(flops=0, bytes_accessed=LINK_COST, transcendentals=0),
        name=name,
    )(part, kept, scale, base, gain, *arrays)


def small_kernel(n, m, x, out, held, total, shard_s, shard_r, group_s, group_r):
    s, h, t = lax.axis_index("shard"), lax.axis_index("head"), lax.axis_index("tensor")
    barrier = pltpu.get_barrier_semaphore()
    others = [lax.rem(s + i, m) for i in range(1, m)]
    peers = group_peers(n)
    for o in others:
        pl.semaphore_signal(barrier, inc=1, device_id=(o, h, t), device_id_type=MESH)
    for p, _ in peers:
        pl.semaphore_signal(barrier, inc=1, device_id=p, device_id_type=MESH)
    pl.semaphore_wait(barrier, m - 1 + 2 * n - 1)

    def over(i, o):
        return pltpu.make_async_remote_copy(src_ref=x, dst_ref=held.at[i], send_sem=shard_s.at[i], recv_sem=shard_r.at[i],
                                            device_id=(o, h, t), device_id_type=MESH)

    def along(i, p):
        return pltpu.make_async_remote_copy(src_ref=total, dst_ref=out.at[h * 2 + t], send_sem=group_s.at[i],
                                            recv_sem=group_r.at[h * 2 + t], device_id=p[0], device_id_type=MESH)

    for i, o in enumerate(others):
        over(i, o).start()
    for i, o in enumerate(others):
        over(i, o).wait_recv()
    v = x[...]
    for i in range(m - 1):
        v = v + held[i]
    total[...] = v
    out[h * 2 + t] = v
    for i, p in enumerate(peers):
        along(i, p).start()
    for i, p in enumerate(peers):
        pltpu.make_async_remote_copy(src_ref=total, dst_ref=out.at[p[1]], send_sem=group_s.at[i], recv_sem=group_r.at[p[1]],
                                     device_id=p[0], device_id_type=MESH).wait_recv()
    for i, o in enumerate(others):
        over(i, o).wait_send()
    for i, p in enumerate(peers):
        along(i, p).wait_send()


def sum_small(n, m, x, collective_id):
    dma = pltpu.SemaphoreType.DMA
    return pl.pallas_call(
        functools.partial(small_kernel, n, m),
        out_shape=jax.ShapeDtypeStruct((2 * n,) + x.shape, F32),
        in_specs=[VM], out_specs=VM,
        scratch_shapes=[pltpu.VMEM((m - 1,) + x.shape, F32), pltpu.VMEM(x.shape, F32), dma((m - 1,)), dma((m - 1,)),
                        dma((2 * n,)), dma((2 * n,))],
        compiler_params=pltpu.CompilerParams(collective_id=collective_id, has_side_effects=True),
        name="sum_small",
    )(x)


PRE = 1152
GROUP = ("head", "tensor")


def int_sum(values, along_axis):
    return jnp.sum(values, axis=along_axis)


def before(values):
    at = jnp.arange(values.shape[0], dtype=jnp.int32)
    return int_sum(jnp.where(at[None, :] < at[:, None], values[None, :], 0), 1)


def layout(seq_lengths, starts, dealing, group_idx):
    total_seqs = seq_lengths.shape[0]
    chosen = lax.dynamic_slice_in_dim(dealing, group_idx * SEQ_DEV, SEQ_DEV)
    picked = (chosen[:, None] == jnp.arange(total_seqs, dtype=jnp.int32)[None, :]).astype(jnp.int32)
    own_length = int_sum(picked * seq_lengths[None, :], 1)
    own_start = int_sum(picked * starts[None, :], 1)
    padded = (own_length + BLOCK - 1) // BLOCK * BLOCK
    buffer_start = before(padded)
    row_ids = jnp.arange(CAP, dtype=jnp.int32)
    member = int_sum((row_ids[:, None] >= buffer_start[None, :]).astype(jnp.int32), 1) - 1
    owned_by = (member[:, None] == jnp.arange(SEQ_DEV, dtype=jnp.int32)[None, :]).astype(jnp.int32)
    position = row_ids - int_sum(owned_by * buffer_start[None, :], 1)
    row_length = int_sum(owned_by * own_length[None, :], 1)
    seq_first = int_sum(owned_by * own_start[None, :], 1)
    filled = position < row_length
    return (seq_first + position, position, filled, seq_first, own_start, own_length)


def congruent(lower_end, upper_end, residue, modulus):
    return (upper_end - 1 - residue) // modulus - (lower_end - 1 - residue) // modulus


def mm(left, right, dims=NN):
    return lax.dot_general(left, right, dims, preferred_element_type=F32)


def full_rows(piece_in):
    return lax.all_gather(piece_in, GROUP, axis=1, tiled=True)


def shares(partial_sum):
    return lax.psum_scatter(partial_sum.astype(BF), GROUP, scatter_dimension=1, tiled=True).astype(F32)


def column_blocks(grad, m):
    rows, wide = grad.shape[0], grad.shape[1] // m
    if wide % 128 == 0:
        return "columns", grad
    return "swap", grad.reshape(rows, m, wide).transpose(1, 0, 2)


def sum_blocks(blocks):
    return jnp.sum(blocks.astype(F32), axis=0)


def body(tokens, seq_lengths, dealing, gain_mixer, w_query, w_key, w_value, w_gate, w_beta, conv_weight,
         gain_heads, w_out, gain_ffn, w_up_gate, w_up, w_down, cotangent):
    shards = lax.axis_size("shard")
    device = lax.axis_index("shard")
    width = tokens.shape[2]
    col_start = lax.axis_index(GROUP) * width
    ff = w_up.shape[1]
    per_peer = CAP // shards + SEQ_DEV
    slots = shards * per_peer
    total_seqs = seq_lengths.shape[0]

    w_piece = jnp.concatenate(
        [w_query, w_key, w_value, w_gate, w_beta, jnp.zeros((w_beta.shape[0], PRE - 4 * width - w_beta.shape[1]), BF)], axis=1)

    starts = before(seq_lengths)
    finish = starts + seq_lengths
    own_rows = tokens.reshape(REAL_DEV, width)
    own_ids = jnp.arange(REAL_DEV, dtype=jnp.int32)
    packed_ids = own_ids * shards + device
    inside = ((packed_ids[:, None] >= starts[None, :]) & (packed_ids[:, None] < finish[None, :])).astype(jnp.int32)
    seq_ids = jnp.arange(total_seqs, dtype=jnp.int32)
    matches = (dealing[:, None] == seq_ids[None, :]).astype(jnp.int32)
    seq_home = int_sum(matches * (seq_ids // SEQ_DEV)[:, None], 0)
    held = congruent(starts, finish, device, shards)
    ahead = (seq_home[:, None] == seq_home[None, :]) & (seq_ids[None, :] < seq_ids[:, None])
    seq_slot = (seq_home * per_peer + int_sum(jnp.where(ahead, held[None, :], 0), 1)
                - 1 - (starts - 1 - device) // shards)
    sent_slot = int_sum(inside * seq_slot[None, :], 1) + own_ids
    slot_ids = jnp.arange(slots, dtype=jnp.int32)
    send_pick = (slot_ids[:, None] == sent_slot[None, :]).astype(BF)
    outbox = mm(send_pick, own_rows).astype(BF)
    arrived = lax.all_to_all(outbox.reshape(shards, per_peer, width), "shard", split_axis=0, concat_axis=0, tiled=True)
    natural, position, filled, seq_first, own_start, own_length = layout(seq_lengths, starts, dealing, device)
    source = natural % shards
    earlier = own_start[None, :] < seq_first[:, None]
    span_counts = congruent(own_start[None, :], (own_start + own_length)[None, :], source[:, None], shards)
    arrival = int_sum(jnp.where(earlier, span_counts, 0), 1) + congruent(seq_first, natural, source, shards)
    recv_slot = jnp.where(filled, source * per_peer + arrival, -1)
    recv_pick = (recv_slot[:, None] == slot_ids[None, :]).astype(BF)
    x_rows = mm(recv_pick, arrived.reshape(slots, width)).astype(BF)
    filled_f = filled.astype(F32)[:, None]
    persist = (position.reshape(-1, BLOCK)[:, 0] != 0).astype(F32)
    pos = position[:, None]
    taps = conv_weight.reshape(3 * CONV, width)
    head_gain = gain_heads[None, :]

    n = lax.axis_size("head")
    rows_full, w_in = z_gather(n, x_rows, 1, "gather_rows", shards, ("gather",), (w_piece,))
    rows_full, cot_piece, w_down, w_out = lax.optimization_barrier((rows_full, cotangent, w_down, w_out))
    w_o = lax.all_gather(w_out, "shard", axis=1, tiled=True)
    cot_full = full_rows(cot_piece)
    w_d = lax.all_gather(w_down, "shard", axis=1, tiled=True)
    rows_full = rows_full.astype(F32)
    scale_one = lax.rsqrt(jnp.mean(rows_full * rows_full, axis=1) + EPSILON)
    normed = (rows_full * scale_one[:, None] * gain_mixer[None, :]).astype(BF)
    pre = mm(normed, w_in)
    mixed, *saved = mixer_fwd(persist, pre, pos, filled_f, taps, head_gain)
    branch_part, cot_full = lax.optimization_barrier((mm(mixed, w_o).astype(BF), cot_full))
    branch, w_ug = z_scatter(n, branch_part, 2, "scatter_branch", shards, ("gather",), (w_up_gate,))
    dealt_f32 = x_rows.astype(F32)
    hidden = dealt_f32 + branch
    held_low = hidden.astype(BF)
    held_full, w_u = z_gather(n, held_low, 3, "gather_held", shards, ("gather",), (w_up,))
    held_full = held_full.astype(F32)
    scale_two = lax.rsqrt(jnp.mean(held_full * held_full, axis=1) + EPSILON)
    normed_two = (held_full * scale_two[:, None] * gain_ffn[None, :]).astype(BF)
    gate_act = mm(normed_two, w_ug)
    up_act = mm(normed_two, w_u)
    sig = jax.nn.sigmoid(gate_act)
    product = (gate_act * sig * up_act).astype(BF)
    d_product = mm(cot_full, w_d, NT)
    d_gate = (d_product * up_act * sig * (1.0 + gate_act * (1.0 - sig))).astype(BF)
    d_up = (d_product * gate_act * sig).astype(BF)
    d_normed_two = (mm(d_gate, w_ug, NT) + mm(d_up, w_u, NT)).astype(BF)
    down_kind, d_w_down = column_blocks(mm(product, cot_full, TN).astype(BF), shards)
    blocks = (shards, w_up.shape[0], ff)
    d_w_ug = mm(normed_two, d_gate, TN).astype(BF).reshape(blocks)
    ffn_gain_part = lax.dynamic_slice_in_dim(gain_ffn, col_start, width)[None, :]
    d_hidden, d_hidden_low, ffn_gain_grad, d_w_ug, d_w_down = z_scatter_norm(
        n, d_normed_two, held_low, scale_two[:, None], cotangent, ffn_gain_part, 4, "scatter_normed_two", shards,
        ("swap", down_kind), (d_w_ug, d_w_down))
    d_w_u = mm(normed_two, d_up, TN).astype(BF).reshape(blocks)
    d_branch_full, d_w_u = z_gather(n, d_hidden_low, 5, "gather_branch", shards, ("swap",), (d_w_u,))
    out_part = mm(product, w_d).astype(BF)
    out_part, d_branch_full = lax.optimization_barrier((out_part, d_branch_full))
    out_sum = shares(out_part)
    d_mixed = mm(d_branch_full, w_o, NT)
    out_kind, d_w_out = column_blocks(mm(mixed, d_branch_full, TN).astype(BF), shards)
    d_pre, d_taps, d_head_gain = mixer_bwd(persist, d_mixed, pre, pos, filled_f, taps, head_gain, saved)
    d_normed = mm(d_pre, w_in, NT).astype(BF)
    d_w_in = mm(normed, d_pre, TN).astype(BF).reshape(shards, w_piece.shape[0], PRE)
    d_normed, out_sum = lax.optimization_barrier((d_normed, out_sum))
    block_out = (hidden + out_sum).astype(BF)
    mixer_gain_part = lax.dynamic_slice_in_dim(gain_mixer, col_start, width)[None, :]
    _, d_dealt, mixer_gain_grad, d_w_in, d_w_out = z_scatter_norm(
        n, d_normed, x_rows, scale_one[:, None], d_hidden, mixer_gain_part, 6, "scatter_normed", shards,
        ("swap", out_kind), (d_w_in, d_w_out))
    d_w_out = sum_blocks(d_w_out)
    d_w_in = sum_blocks(d_w_in)
    outbox_back = mm(recv_pick, d_dealt, TN).astype(BF)
    arrived_back = lax.all_to_all(outbox_back.reshape(shards, per_peer, width), "shard", split_axis=0, concat_axis=0, tiled=True)
    d_tokens = mm(send_pick, arrived_back.reshape(slots, width), TN).reshape(REAL_DEV, 1, width)

    small = jnp.concatenate([
        jnp.sum(d_taps, axis=1), jnp.sum(mixer_gain_grad, axis=0)[None, :], jnp.sum(ffn_gain_grad, axis=0)[None, :],
        jnp.pad(jnp.sum(d_head_gain, axis=0), (0, width - HD))[None, :],
        jnp.zeros((1, width), F32)], axis=0)
    summed = sum_small(n, shards, small, 7)
    by_row = summed.transpose(1, 0, 2).reshape(16, D)
    d_conv = by_row[:12].reshape(CONV, 3, D)
    d_gain_heads = jnp.sum(summed[:, 14, :HD], axis=0)
    cut = [0, width, 2 * width, 3 * width, 4 * width]
    return (
        block_out, d_tokens, by_row[12],
        d_w_in[:, cut[0]:cut[1]], d_w_in[:, cut[1]:cut[2]], d_w_in[:, cut[2]:cut[3]], d_w_in[:, cut[3]:cut[4]],
        d_w_in[:, 4 * width:4 * width + w_beta.shape[1]],
        d_conv, d_gain_heads, d_w_out, by_row[13],
        sum_blocks(d_w_ug), sum_blocks(d_w_u), sum_blocks(d_w_down),
    )


def solution(mesh):
    feat = ("head", "tensor")
    placed = (
        P(None, "shard", feat), P(), P(), P(),
        P("shard", feat), P("shard", feat), P("shard", feat), P("shard", feat), P("shard", feat),
        P(None, None, feat), P(), P(feat, "shard"), P(),
        P("shard", feat), P("shard", feat), P(feat, "shard"), P("shard", feat),
    )
    given = (
        P("shard", feat), P(None, "shard", feat), P(),
        P("shard", feat), P("shard", feat), P("shard", feat), P("shard", feat), P("shard", feat),
        P(), P(), P(feat, "shard"), P(),
        P("shard", feat), P("shard", feat), P(feat, "shard"),
    )
    return jax.shard_map(body, mesh=mesh, in_specs=placed, out_specs=given, check_vma=False)
```

time: 2180 us -> 743 us (0.34)
  waiting for transfers between devices: 989 us -> 22.1 us
  matrix products: 617 us -> 134 us
  Pallas kernels: 0 us -> 472 us
  other arithmetic: 321 us -> 34.9 us
  local copies, waits for them, and re-layouts: 132 us -> 50.2 us
  blocking collectives: 75.9 us -> 0 us
    reduce_scatter x12 -> x1, waiting for transfers between devices: 510 us -> 0.01 us  [shares(): lax.psum_scatter(partial_sum.astype(BF), GROUP, scatter_dimension=1, tile...]
    dot_general x280 -> x19, matrix products: 610 us -> 134 us  [mm(): return lax.dot_general(left, right, dims, preferred_element_type=F32)]
    pallas_call x0 -> x9, Pallas kernels: none -> 472 us  [the longest x3 159 us: z_gather(): pl.pallas_call(functools.partial(gather_kernel, n, width, m, kinds), out_...]
    all_gather x12 -> x3, waiting for transfers between devices: 364 us -> 10.3 us  [the longest x1 10.3 us: full_rows(): return lax.all_gather(piece_in, GROUP, axis=1, tiled=True)]
    another operation x11 -> x0, other arithmetic: 202 us -> none  [the longest x5 200 us: delta_rule(): lax.linalg.triangular_solve(system, jnp.broadcast_to(identity, system.sha...]
    psum x1 -> x0, waiting for transfers between devices: 75.5 us -> none  [body(): lax.psum((mixer_gain_full, conv_full, d_gain_heads_part, ffn_gain_full),...]
    psum x3 -> x0, blocking collectives: 67.6 us -> none  [the longest x1 39.8 us: body(): lax.psum((mixer_gain_full, conv_full, d_gain_heads_part, ffn_gain_full),...]
    unnamed x27 -> x4, waiting for transfers between devices: 31.1 us -> 0.75 us
  transfers between devices with their start and end apart: 28 -> 6, of which waited for: 24 -> 3; matrix products, arithmetic and copies ran while one was open for 46% -> 14% of each run, Pallas kernels for 0% -> 29%
where the time goes in v1:
time: 743 us; the launch traced here: 737 us
  Pallas kernels  472 us (64%)
  matrix products  134 us (18%)
  local copies, waits for them, and re-layouts  50.2 us (7%)
  other arithmetic  34.9 us (5%)
  waiting for transfers between devices  22.1 us (3%)
  between operations  14.8 us (2%)
  starting transfers between devices  8.94 us (1%)
    pallas_call x3, Pallas kernels, z_gather(): pl.pallas_call(functools.partial(gather_kernel, n, width, m, kinds), out_...  159 us
    pallas_call x2, Pallas kernels, z_scatter_norm(): pl.pallas_call(functools.partial(scatter_norm_kernel, n, width, m, kinds)...  137 us
    dot_general x19, matrix products, mm(): return lax.dot_general(left, right, dims, preferred_element_type=F32)  134 us
    pallas_call x1, Pallas kernels, mixer_bwd(): pl.pallas_call(bwd_kernel, out_shape=outs, in_specs=[SM] + [VM] * (6 + le...  65.9 us
    pallas_call x1, Pallas kernels, z_scatter(): pl.pallas_call(functools.partial(scatter_kernel, n, width, m, kinds), out...  53 us
    pallas_call x1, Pallas kernels, mixer_fwd(): pl.pallas_call(fwd_kernel, out_shape=outs, in_specs=[SM] + [VM] * 5, out_...  47 us
    unnamed x95, local copies, waits for them, and re-layouts  28.9 us
  transfers between devices with their start and end apart: 6, of which 3 were waited for; matrix products, arithmetic and copies ran while one was open for 14% of the time, Pallas kernels for 29%

profile of v1, /device:TPU:0, one launch (start us, length us, event | category | flops | bytes accessed | tf_op | source)
XLA Modules:
  0.0 736.6 jit_solution(17649971409979960577)
XLA Ops:
  12.0 5.2 all-to-all-start
  20.4 6.4 all-to-all-done
  29.2 58.6 %gather_rows.1 = (bf16[1280,2048]{1,0:T(8,128)(2,1)}, bf16[2048,1152]{1,0:T(8,128)(2,1)}) custom-call(bf16[1280,256]{1,0:T(8,128)(2,1)} %fusion.16.refs_0_.refs_1_, bf16[512,1152]{1,0:T(8,128)(2,1)} %concatenate.6.refs_1_), custom_call_target="tpu_custom_call" | custom-call | bytes 157286400 | tf_op jit(solution)/shard_map/gather_rows/pallas_call | solution.py:444
  98.0 12.1 %fusion.19.pre = f32[1280,1152]{1,0:T(8,128)} fusion(bf16[2048,1152]{1,0:T(8,128)(2,1)} %get-tuple-element.58, bf16[1280,2048]{1,0:T(8,128)(2,1)} %get-tuple-element.57, f32[2048]{0:T(1024)S(1)} %copy-done.35, f32[1280]{0:T(1024)S(1)} %add_rsqrt_fusion.1), kind=kOutput, calls=%fused_computation.42 | convolution fusion | flops 6050283520 | bytes 15873024 | tf_op jit(solution)/shard_map/dot_general | solution.py:869
  110.2 47.0 %mixer_forward.1 = (bf16[1280,256]{1,0:T(8,128)(2,1)}, f32[1280,768]{1,0:T(8,128)}, f32[1280,512]{1,0:T(8,128)}, f32[1280,256]{1,0:T(8,128)}, f32[1280,256]{1,0:...) custom-call(f32[20]{0:T(128)} %convert_reduce_fusion.6.persist, ...), custom_call_target="tpu_custom_call" | custom-call | bytes 146800640 | tf_op jit(solution)/shard_map/mixer_forward/pallas_call | solution.py:150
  157.2 5.3 convolution_convert_fusion.3.refs_0_
  162.5 10.3 %all-gather.6.cloned.1.call-done = bf16[1280,2048]{1,0:T(8,128)(2,1)} async-done(((bf16[1280,256]{1,0:T(8,128)(2,1)}), bf16[1280,2048]{1,0:T(8,128)(2,1)}) %all-gather.6.cloned.1.call-update) | async-done | bytes 5242896 | tf_op jit(solution)/shard_map/all_gather | solution.py:873
  175.2 53.0 %scatter_branch.1 = (f32[1280,256]{1,0:T(8,128)S(1)}, bf16[2048,704]{1,0:T(8,128)(2,1)S(1)}) custom-call(bf16[1280,2048]{1,0:T(8,128)(2,1)S(1)} %copy-done.2, bf16[512,704]{1,0:T(8,128)(2,1)S(1)} %copy.114.refs_1_), custom_call_target="tpu_custom_call" | custom-call | bytes 157286400 | tf_op jit(solution)/shard_map/scatter_branch/pallas_call | solution.py:594
  230.9 49.8 %gather_held.1 = (bf16[1280,2048]{1,0:T(8,128)(2,1)}, bf16[2048,704]{1,0:T(8,128)(2,1)}) custom-call(bf16[1280,256]{1,0:T(8,128)(2,1)} %fusion.21.refs_0_.refs_1_, bf16[512,704]{1,0:T(8,128)(2,1)} %copy.115.refs_1_), custom_call_target="tpu_custom_call" | custom-call | bytes 157286400 | tf_op jit(solution)/shard_map/gather_held/pallas_call | solution.py:444
  284.8 8.0 %fusion.49 = f32[1280,704]{0,1:T(8,128)} fusion(bf16[2048,704]{1,0:T(8,128)(2,1)} %get-tuple-element.66, bf16[1280,2048]{1,0:T(8,128)(2,1)S(1)} %copy-done.20, f32[2048]{0:T(1024)S(1)} %copy-done.34, f32[1280]{0:T(1024)S(1)} %add_rsqrt_fusion), kind=kOutput, calls=%fused_computation.149 | convolution fusion | flops 3701473280 | bytes 11744256 | tf_op jit(solution)/shard_map/dot_general | solution.py:869
  292.9 6.0 fusion.51
  298.8 12.2 %multiply_convert_fusion = (bf16[1280,704]{0,1:T(8,128)(2,1)S(1)}, bf16[1280,704]{0,1:T(8,128)(2,1)S(1)}, bf16[1280,704]{0,1:T(8,128)(2,1)}) fusion(f32[1280,704]{0,1:T(8,128)} %fusion.51, f32[1280,704]{0,1:T(8,128)} %fusion.49, bf16[1280,2048]{1,0:T(8,128)(2,1)} %all-gather.6.cloned.1.call-done, bf16[704,2048]{1,0:T(8,128)(2,1)} %all-gather.8.cloned.1.call-done), kind=kOutput, calls=%fused_computation.25 | convolution fusion | flops 3705405440 | bytes 20742144 | tf_op jit(solution)/shard_map/dot_general | solution.py:869
  311.0 8.8 %convolution_convert_fusion.5 = bf16[2048,704]{0,1:T(8,128)(2,1)} fusion(bf16[1280,704]{0,1:T(8,128)(2,1)S(1)} %get-tuple-element.196, bf16[1280,2048]{1,0:T(8,128)(2,1)} %get-tuple-element.64, f32[2048]{0:T(1024)S(1)} %copy-done.34, f32[1280]{0:T(1024)S(1)} %add_rsqrt_fusion), kind=kOutput, calls=%fused_computation.32 | convolution fusion | flops 3702915072 | bytes 9942016 | tf_op jit(solution)/shard_map/dot_general | solution.py:869
  319.8 7.0 fusion.55
  327.1 5.5 convolution_convert_fusion.4
  332.6 4.6 copy.118
  337.2 8.5 %convolution_convert_fusion.6.refs_6_ = bf16[704,2048]{1,0:T(8,128)(2,1)} fusion(bf16[1280,704]{0,1:T(8,128)(2,1)} %get-tuple-element.197, bf16[1280,2048]{1,0:T(8,128)(2,1)} %all-gather.6.cloned.1.call-done), kind=kOutput, calls=%fused_computation.33 | convolution fusion | flops 3692429312 | bytes 9928704 | tf_op jit(solution)/shard_map/dot_general | solution.py:869
  345.8 4.7 copy.116
  350.5 12.3 %add_convert_fusion.refs_0_ = bf16[1280,2048]{1,0:T(8,128)(2,1)} fusion(f32[1280,2048]{1,0:T(8,128)} %fusion.55, bf16[1280,704]{0,1:T(8,128)(2,1)} %copy-done.38, bf16[2048,704]{1,0:T(8,128)(2,1)} %get-tuple-element.66), kind=kOutput, calls=%fused_computation.10 | convolution fusion | flops 3696230400 | bytes 20414464 | tf_op jit(solution)/shard_map/dot_general | solution.py:869
  362.8 68.5 %scatter_normed_two.1 = (f32[1280,256]{1,0:T(8,128)S(1)}, bf16[1280,256]{1,0:T(8,128)(2,1)S(1)}, f32[8,256]{1,0:T(8,128)S(1)}, bf16[4,512,704]{2,1,0:T(8,128)(2,1)S(1)}, bf16[4,704,512]{2,1,0:T(8,128)(2,1)S(1)}) custom-call(bf16[1280,2048]{1,0:T(8,128)(2,1)} %add_convert_fusion.refs_0_, bf16[1280,256]{1,0:T(8,128)(2,1)S(1)} %copy-done.4, ...), custom_call_target="tpu_custom_call" | custom-call | bytes 157286400 | tf_op jit(solution)/shard_map/scatter_normed_two/pallas_call | solution.py:767
  436.4 50.1 %gather_branch.1 = (bf16[1280,2048]{1,0:T(8,128)(2,1)}, bf16[4,512,704]{2,1,0:T(8,128)(2,1)}) custom-call(bf16[1280,256]{1,0:T(8,128)(2,1)} %copy-done.13, bf16[4,512,704]{2,1,0:T(8,128)(2,1)} %bitcast.47), custom_call_target="tpu_custom_call" | custom-call | bytes 157286400 | tf_op jit(solution)/shard_map/gather_branch/pallas_call | solution.py:444
  486.5 9.0 %convolution_convert_fusion.2 = bf16[1280,2048]{1,0:T(8,128)(2,1)} fusion(bf16[1280,704]{0,1:T(8,128)(2,1)} %get-tuple-element.197, bf16[704,2048]{1,0:T(8,128)(2,1)} %all-gather.8.cloned.1.call-done), kind=kOutput, calls=%fused_computation.14 | convolution fusion | flops 3693608960 | bytes 9928704 | tf_op jit(solution)/shard_map/dot_general | solution.py:869
  495.8 5.4 fusion.56.dmix
  501.3 65.9 %mixer_backward.1 = (bf16[1280,1152]{1,0:T(8,128)(2,1)}, f32[12,8,256]{2,1,0:T(8,128)}, f32[8,128]{1,0:T(8,128)}) custom-call(f32[20]{0:T(128)} %convert_reduce_fusion.6.persist, f32[1280,256]{1,0:T(8,128)} %fusion.56.dmix, f32[1280,1152]{1,0:T(8,128)} %fusion.19.pre, s32[1280,1]{1,0:T(8,128)} %copy-done.18, f32[1280,1]{1,0:T(8,128)} %fusion.22.fill_ref, ...), custom_call_target="tpu_custom_call" | custom-call | bytes 209715200 | tf_op jit(solution)/shard_map/mixer_backward/pallas_call | solution.py:268
  575.5 3.8 convert_reduce_fusion.2
  585.7 5.2 convolution_convert_fusion.7.refs_6_
  590.9 10.9 %convolution_convert_fusion = bf16[2048,1152]{1,0:T(8,128)(2,1)} fusion(bf16[1280,1152]{1,0:T(8,128)(2,1)S(1)} %copy-done.36, bf16[1280,2048]{1,0:T(8,128)(2,1)} %get-tuple-element.57, f32[2048]{0:T(1024)S(1)} %copy-done.35, f32[1280]{0:T(1024)S(1)} %add_rsqrt_fusion.1), kind=kOutput, calls=%fused_computation.12 | convolution fusion | flops 6052642816 | bytes 12923904 | tf_op jit(solution)/shard_map/dot_general | solution.py:869
  601.8 8.7 %convolution_convert_fusion.1.refs_0_ = bf16[1280,2048]{1,0:T(8,128)(2,1)} fusion(bf16[1280,1152]{1,0:T(8,128)(2,1)S(1)} %copy-done.36, bf16[2048,1152]{1,0:T(8,128)(2,1)S(1)} %bitcast.62), kind=kOutput, calls=%fused_computation.13 | convolution fusion | flops 6042419200 | bytes 12910592 | tf_op jit(solution)/shard_map/dot_general | solution.py:869
  615.3 68.3 %scatter_normed.1 = (f32[1280,256]{1,0:T(8,128)}, bf16[1280,256]{1,0:T(8,128)(2,1)S(1)}, f32[8,256]{1,0:T(8,128)S(1)}, bf16[4,512,1152]{2,1,0:T(8,128)(2,1)S(1)}, bf16[4,256,512]{2,1,0:T(8,128)(2,1)S(1)}) custom-call(bf16[1280,2048]{1,0:T(8,128)(2,1)} %convolution_convert_fusion.1.refs_0_, bf16[1280,256]{1,0:T(8,128)(2,1)S(1)} %copy-done.3, ...), custom_call_target="tpu_custom_call" | custom-call | bytes 157286400 | tf_op jit(solution)/shard_map/scatter_normed/pallas_call | solution.py:767
  688.3 11.0 %sum_small.1 = f32[8,16,256]{2,1,0:T(8,128)} custom-call(f32[16,256]{1,0:T(8,128)} %concatenate.7.x), custom_call_target="tpu_custom_call" | custom-call | tf_op jit(solution)/shard_map/sum_small/pallas_call | solution.py:822
  717.0 4.7 all-to-all-done.1
  723.7 6.0 copy.122
  (172 shorter events, 79.1 us)
Async XLA Ops:
  9.8 7.4 %copy-start.37 = (s32[16]{0:T(128)S(1)}, s32[16]{0:T(128)}, u32[]{:S(2)}) copy-start(s32[16]{0:T(128)} %param.19) | copy-start | bytes 196
  9.8 7.4 %copy-start.33 = (s32[16]{0:T(128)S(1)}, s32[16]{0:T(128)}, u32[]{:S(2)}) copy-start(s32[16]{0:T(128)} %param.18) | copy-start | bytes 196
  9.8 8.0 %copy-start.32 = (bf16[512,2]{0,1:T(2,128)(2,1)S(1)}, bf16[512,2]{0,1:T(2,128)(2,1)}, u32[]{:S(2)}) copy-start(bf16[512,2]{0,1:T(2,128)(2,1)} %param.25) | copy-start | bytes 6148
  9.8 8.2 %copy-start.23 = (bf16[512,256]{1,0:T(8,128)(2,1)S(1)}, bf16[512,256]{1,0:T(8,128)(2,1)}, u32[]{:S(2)}) copy-start(bf16[512,256]{1,0:T(8,128)(2,1)} %param.21) | copy-start | bytes 786436
  9.8 8.2 %copy-start.24 = (bf16[512,256]{1,0:T(8,128)(2,1)S(1)}, bf16[512,256]{1,0:T(8,128)(2,1)}, u32[]{:S(2)}) copy-start(bf16[512,256]{1,0:T(8,128)(2,1)} %param.22) | copy-start | bytes 786436
  9.9 8.2 %copy-start.25 = (bf16[512,256]{1,0:T(8,128)(2,1)S(1)}, bf16[512,256]{1,0:T(8,128)(2,1)}, u32[]{:S(2)}) copy-start(bf16[512,256]{1,0:T(8,128)(2,1)} %param.23) | copy-start | bytes 786436
  9.9 8.2 %copy-start.26 = (bf16[512,256]{1,0:T(8,128)(2,1)S(1)}, bf16[512,256]{1,0:T(8,128)(2,1)}, u32[]{:S(2)}) copy-start(bf16[512,256]{1,0:T(8,128)(2,1)} %param.24) | copy-start | bytes 786436
  12.0 14.8 %all-to-all-start = ((bf16[4,324,256]{2,1,0:T(8,128)(2,1)}), bf16[4,324,256]{2,1,0:T(8,128)(2,1)S(1)}, u32[]{:S(2)}, u32[]{:S(2)}) async-start(bf16[4,324,256]{2,1,0:T(8,128)(2,1)} %reshape.305), calls=%async_computation | async-start | bytes 1343488 | tf_op jit(solution)/shard_map/all_to_all | solution.py:922
  17.2 140.1 %all-gather.4.cloned.1.call-start = ((), (), s32[]{:S(2)}) async-start(), calls=%async_computation.3 | async-start | bytes 1310720 | tf_op jit(solution)/shard_map/all_gather | solution.py:940
  20.4 8.8 %copy-start.28 = (s32[1280]{0:T(1024)}, s32[1280]{0:T(1024)S(1)}, u32[]{:S(2)}) copy-start(s32[1280]{0:T(1024)S(1)} %fusion.39) | copy-start | bytes 15364
  26.9 62.1 %copy-start.27 = (f32[4,3,256]{2,0,1:T(4,128)S(1)}, f32[4,3,256]{2,0,1:T(4,128)}, u32[]{:S(2)}) copy-start(f32[4,3,256]{2,0,1:T(4,128)} %param.26) | copy-start | bytes 36868
  29.2 60.5 %copy-start.22 = (bf16[512,704]{0,1:T(8,128)(2,1)S(1)}, bf16[512,704]{0,1:T(8,128)(2,1)}, u32[]{:S(2)}) copy-start(bf16[512,704]{0,1:T(8,128)(2,1)} %param.30) | copy-start | bytes 2162692
  29.2 63.1 %copy-start.34 = (f32[2048]{0:T(1024)S(1)}, f32[2048]{0:T(1024)}, u32[]{:S(2)}) copy-start(f32[2048]{0:T(1024)} %param.29) | copy-start | bytes 24580
  87.8 84.9 %all-gather.6.cloned.1.call-start = ((), (), s32[]{:S(2)}) async-start(), calls=%async_computation.4 | async-start | bytes 5898240 | tf_op jit(solution)/shard_map/all_gather | solution.py:873
  88.6 210.2 %all-gather.8.cloned.1.call-start = ((), (), s32[]{:S(2)}) async-start(), calls=%async_computation.5 | async-start | bytes 3604480 | tf_op jit(solution)/shard_map/all_gather | solution.py:942
  89.0 8.8 %copy-start.18 = (s32[1280,1]{1,0:T(8,128)}, s32[1280,1]{1,0:T(8,128)S(1)}, u32[]{:S(2)}) copy-start(s32[1280,1]{1,0:T(8,128)S(1)} %copy.113.pos_ref) | copy-start | bytes 15364
  97.8 512.7 %reduce-scatter.2.cloned.1.call-start = ((), (), s32[]{:S(2)}) async-start(), calls=%async_computation.6 | async-start | bytes 5898240 | tf_op jit(solution)/shard_map/reduce_scatter | solution.py:877
  175.2 54.7 %copy-start.3 = (bf16[1280,256]{1,0:T(8,128)(2,1)S(1)}, bf16[1280,256]{1,0:T(8,128)(2,1)}, u32[]{:S(2)}) copy-start(bf16[1280,256]{1,0:T(8,128)(2,1)} %fusion.16.refs_0_.refs_1_) | copy-start | bytes 1966084
  284.8 8.1 %copy-start.15 = (bf16[2048,704]{1,0:T(8,128)(2,1)S(1)}, bf16[2048,704]{1,0:T(8,128)(2,1)}, u32[]{:S(2)}) copy-start(bf16[2048,704]{1,0:T(8,128)(2,1)} %copy-done.14) | copy-start | bytes 8650756
  311.0 16.0 %copy-start.38 = (bf16[1280,704]{0,1:T(8,128)(2,1)}, bf16[1280,704]{0,1:T(8,128)(2,1)S(1)}, u32[]{:S(2)}) copy-start(bf16[1280,704]{0,1:T(8,128)(2,1)S(1)} %get-tuple-element.195) | copy-start | bytes 5406724
  311.0 8.8 %copy-start.16 = (bf16[2048,704]{1,0:T(8,128)(2,1)S(1)}, bf16[2048,704]{1,0:T(8,128)(2,1)}, u32[]{:S(2)}) copy-start(bf16[2048,704]{1,0:T(8,128)(2,1)} %copy-done.14) | copy-start | bytes 8650756
  311.0 16.0 %slice-start.1 = ((s8[5242880]{0:T(1024)(128)(4,1)}), s8[4194304]{0:T(1024)(128)(4,1)S(1)}, s32[]{:S(2)}) async-start(s8[5242880]{0:T(1024)(128)(4,1)} %bitcast.49), calls=%async_computation.8 | async-start | bytes 8388608
  350.5 12.3 %copy-start.4 = (bf16[1280,256]{1,0:T(8,128)(2,1)S(1)}, bf16[1280,256]{1,0:T(8,128)(2,1)}, u32[]{:S(2)}) copy-start(bf16[1280,256]{1,0:T(8,128)(2,1)} %fusion.21.refs_0_.refs_1_) | copy-start | bytes 1966084
  350.5 12.3 %copy-start.7 = (bf16[704,2048]{1,0:T(8,128)(2,1)S(1)}, bf16[704,2048]{1,0:T(8,128)(2,1)}, u32[]{:S(2)}) copy-start(bf16[704,2048]{1,0:T(8,128)(2,1)} %convolution_convert_fusion.6.refs_6_) | copy-start | bytes 8650756
  350.5 12.3 %copy-start.8 = (bf16[1280,256]{1,0:T(8,128)(2,1)S(1)}, bf16[1280,256]{1,0:T(8,128)(2,1)}, u32[]{:S(2)}) copy-start(bf16[1280,256]{1,0:T(8,128)(2,1)} %refs_3_.1) | copy-start | bytes 1966084
  585.7 16.1 %slice-start.3 = ((s8[4718592]{0:T(1024)(128)(4,1)}), s8[4194304]{0:T(1024)(128)(4,1)S(1)}, s32[]{:S(2)}) async-start(s8[4718592]{0:T(1024)(128)(4,1)} %bitcast.61), calls=%async_computation.10 | async-start | bytes 8388608
  590.9 10.9 %slice-start.4 = ((s8[4718592]{0:T(1024)(128)(4,1)}), s8[524288]{0:T(1024)(128)(4,1)S(1)}, s32[]{:S(2)}) async-start(s8[4718592]{0:T(1024)(128)(4,1)} %bitcast.61), calls=%async_computation.11 | async-start | bytes 1048576
  684.3 19.5 %copy-start.29 = (s32[1280]{0:T(1024)S(1)}, s32[1280]{0:T(1024)}, u32[]{:S(2)}) copy-start(s32[1280]{0:T(1024)} %copy-done.28) | copy-start | bytes 15364
  703.8 7.8 %slice-start = ((f32[512,1152]{1,0:T(8,128)}), f32[512,2]{1,0:T(8,128)S(1)}, s32[]{:S(2)}) async-start(f32[512,1152]{1,0:T(8,128)} %copy-done.19), calls=%async_computation.7 | async-start | bytes 524288 | tf_op jit(solution)/shard_map/slice | solution.py:1006
  708.1 13.5 %all-to-all-start.1 = ((bf16[4,324,256]{2,1,0:T(8,128)(2,1)}), bf16[4,324,256]{2,1,0:T(8,128)(2,1)S(1)}, u32[]{:S(2)}, u32[]{:S(2)}) async-start(bf16[4,324,256]{2,1,0:T(8,128)(2,1)} %reshape.311), calls=%async_computation.2 | async-start | bytes 1343488 | tf_op jit(solution)/shard_map/all_to_all | solution.py:991
  711.6 10.1 %copy-start.31 = (s32[1152]{0:T(1024)S(1)}, s32[1152]{0:T(1024)}, u32[]{:S(2)}) copy-start(s32[1152]{0:T(1024)} %copy-done.30) | copy-start | bytes 13828
  721.6 8.0 %copy-start.1 = (bf16[1152,1,256]{2,0,1:T(8,128)(2,1)S(1)}, bf16[1152,1,256]{2,0,1:T(8,128)(2,1)}, u32[]{:S(2)}) copy-start(bf16[1152,1,256]{2,0,1:T(8,128)(2,1)} %param.17) | copy-start | bytes 1769476
  (18 other events, 47.1 us)
Sparse Core Ops, SparseCore 0:
  87.9 26.6 all-gather.3
  116.2 56.4 all-gather.5
  174.6 81.3 all-gather.7
  495.6 59.0 reduce-scatter.1

commit v2 on v1

v2 whole, which is shorter than its diff:
```python
import functools
import jax
import jax.numpy as jnp
from jax import lax
from jax.experimental import pallas as pl
from jax.experimental.pallas import tpu as pltpu

from jax.sharding import PartitionSpec as P

D = 2048
HD = 128
CONV = 4
BLOCK = 64
SEQ_DEV = 4
REAL_DEV = 1152
CAP = 1280
NB = CAP // BLOCK
EPSILON = 1e-06
HEAD_FLOOR = 0.01
F32 = jnp.float32
BF = jnp.bfloat16

def split(x):
    hi = x.astype(BF)
    return hi, (x - hi.astype(F32)).astype(BF)

NN=(((1,),(0,)),((),())); NT=(((1,),(1,)),((),())); TN=(((0,),(0,)),((),()))

def dg(a, b, dims):
    return lax.dot_general(a, b, dims, preferred_element_type=F32)

def d3(a, b, dims=NN):
    ah, al = split(a); bh, bl = split(b)
    return dg(ah, bh, dims) + (dg(ah, bl, dims) + dg(al, bh, dims))

def twice(step):
    return lambda i, c: step(2 * i + 1, step(2 * i, c))

def masks():
    ri = lax.broadcasted_iota(jnp.int32, (BLOCK, BLOCK), 0)
    ci = lax.broadcasted_iota(jnp.int32, (BLOCK, BLOCK), 1)
    return ri, ci

def sigmoid(x):
    return 1.0 / (1.0 + jnp.exp(-x))

def conv_rows(cur, tail, wt, pos):
    ext = jnp.concatenate([tail, cur], axis=0)
    out = wt[0] * cur
    for j in range(1, CONV):
        sh = pltpu.roll(ext, j, axis=0)[8:]
        out = out + wt[j] * jnp.where(pos >= j, sh, 0.0)
    return out

def inverses(lmats, ri, ci):
    apart = ri ^ ci
    xs = [jnp.where(apart == 0, 1.0, 0.0) - jnp.where(apart == 1, m, 0.0) for m in lmats]
    s = 2
    while s < BLOCK:
        at = (apart >= s) & (apart < 2 * s)
        ys = [d3(x, jnp.where(at, m, 0.0)) for x, m in zip(xs, lmats)]
        xs = [x - d3(y, x) for x, y in zip(xs, ys)]
        s *= 2
    return xs

def fwd_kernel(persist, pre, pos_ref, fill_ref, cw, gain, mixed, c_out, qk, w_out, u_out, u2_out, o_out, p_out, t_out, m_out, s_out, b_s):
    ri, ci = masks()
    heads = 2
    def phase_a(n, tails):
        r = pl.ds(pl.multiple_of(n * BLOCK, BLOCK), BLOCK)
        pos = pos_ref[r, :]; fil = fill_ref[r, :]
        new_tails = []
        acts = []
        for i in range(3):
            cur = pre[r, i*256:(i+1)*256]
            wt = [cw[j*3+i:j*3+i+1, :] for j in range(CONV)]
            cc = conv_rows(cur, tails[i], wt, pos)
            c_out[r, i*256:(i+1)*256] = cc
            acts.append(cc * sigmoid(cc) * fil)
            new_tails.append(cur[BLOCK-8:])
        beta = sigmoid(pre[r, 1024:1152])
        for h in range(heads):
            hs = slice(h*HD, (h+1)*HD)
            yq = acts[0][:, hs]; yk = acts[1][:, hs]; v = acts[2][:, hs]
            q = yq * lax.rsqrt(jnp.sum(yq*yq, axis=1, keepdims=True) + EPSILON)
            k = yk * lax.rsqrt(jnp.sum(yk*yk, axis=1, keepdims=True) + EPSILON)
            b = beta[:, h:h+1]
            qk[r, h*HD:(h+1)*HD] = q
            qk[r, 256+h*HD:256+(h+1)*HD] = k
            lmat = jnp.where(ri > ci, b * d3(k, k, NT), 0.0)
            p_out[n*2+h] = jnp.where(ri >= ci, d3(q, k, NT), 0.0)
            t_out[n*2+h] = lmat
            u_out[r, hs] = b*v
            w_out[r, hs] = b*k
        return tuple(new_tails)
    z8 = jnp.zeros((8, 256), F32)
    lax.fori_loop(0, NB // 2, twice(phase_a), (z8, z8, z8))
    GRP = 8
    def phase_t(i, _):
        ts = inverses([t_out[i*GRP+j] for j in range(GRP)], ri, ci)
        for j in range(GRP):
            t_out[i*GRP+j] = ts[j]
        return 0
    lax.fori_loop(0, 2*NB//GRP, phase_t, 0)
    def phase_w(i, _):
        todo = [(n, pl.ds(pl.multiple_of(n * BLOCK, BLOCK), BLOCK), h, slice(h*HD, (h+1)*HD)) for n in (2*i, 2*i+1) for h in range(heads)]
        wu = [d3(t_out[n*2+h], jnp.concatenate([w_out[r, c], u_out[r, c]], axis=1)) for n, r, h, c in todo]
        mb = [d3(qk[r, 256+h*HD:256+(h+1)*HD], x, TN) for x, (n, r, h, c) in zip(wu, todo)]
        for x, y, (n, r, h, c) in zip(wu, mb, todo):
            w_out[r, c] = x[:, :HD]; u_out[r, c] = x[:, HD:]
            m_out[n*2+h] = y[:, :HD]; b_s[n*2+h] = y[:, HD:]
        return 0
    lax.fori_loop(0, NB//2, phase_w, 0)
    def phase_b(n, ss):
        out = []
        for h in range(heads):
            e = n*2+h
            s = ss[h] * persist[n]
            s_out[e] = s
            out.append(s - d3(m_out[e], s) + b_s[e])
        return tuple(out)
    zs = jnp.zeros((HD, HD), F32)
    lax.fori_loop(0, NB, phase_b, (zs, zs))
    def phase_c(i, _):
        todo = [(n, pl.ds(pl.multiple_of(n * BLOCK, BLOCK), BLOCK), h, slice(h*HD, (h+1)*HD)) for n in (2*i, 2*i+1) for h in range(heads)]
        rr = [d3(jnp.concatenate([w_out[r, c], qk[r, c]], axis=0), s_out[n*2+h]) for n, r, h, c in todo]
        u2 = [u_out[r, c] - v[:BLOCK] for v, (n, r, h, c) in zip(rr, todo)]
        os_ = [v[BLOCK:] + d3(p_out[n*2+h], u) for v, u, (n, r, h, c) in zip(rr, u2, todo)]
        for o, u, (n, r, h, c) in zip(os_, u2, todo):
            u2_out[r, c] = u
            o_out[r, c] = o
            ms = jnp.mean(o*o, axis=1, keepdims=True)
            sc = lax.rsqrt(jnp.maximum(ms, HEAD_FLOOR))
            gg = pre[r, 768+h*HD:768+(h+1)*HD]
            mixed[r, c] = (o * sc * gain[...] * (gg * sigmoid(gg))).astype(BF)
        return 0
    lax.fori_loop(0, NB // 2, phase_c, 0)

def sds(*s, dt=F32): return jax.ShapeDtypeStruct(s, dt)
VM = pl.BlockSpec(memory_space=pltpu.VMEM)
SM = pl.BlockSpec(memory_space=pltpu.SMEM)

def mixer_fwd(persist, pre, pos, fil, cw, gain):
    outs = (sds(CAP,256,dt=BF), sds(CAP,768), sds(CAP,512), sds(CAP,256), sds(CAP,256), sds(CAP,256), sds(CAP,256),
            sds(2*NB,BLOCK,BLOCK), sds(2*NB,BLOCK,BLOCK), sds(2*NB,HD,HD), sds(2*NB,HD,HD))
    return pl.pallas_call(fwd_kernel, out_shape=outs, in_specs=[SM]+[VM]*5, out_specs=[VM]*len(outs),
        scratch_shapes=[pltpu.VMEM((2*NB,HD,HD),F32)],
        compiler_params=pltpu.CompilerParams(vmem_limit_bytes=56*2**20), cost_estimate=pl.CostEstimate(flops=0, bytes_accessed=140 * 2**20, transcendentals=0),
        name="mixer_forward")(persist, pre, pos, fil, cw, gain)

def bwd_kernel(persist, dmix, pre, pos_ref, fill_ref, cw, gain, c_in, qk, w_in, u_in, u2_in, o_in, p_in, t_in, m_in, s_in,
               dpre, dcw, dgain, e_s, do_s):
    ri, ci = masks()
    heads = 2
    lane = lax.broadcasted_iota(jnp.int32, (BLOCK, HD), 1)
    dgain[...] = jnp.zeros_like(dgain)
    dcw[...] = jnp.zeros_like(dcw)
    def phase_a(n, _):
        r = pl.ds(pl.multiple_of(n * BLOCK, BLOCK), BLOCK)
        for h in range(heads):
            hs = slice(h*HD, (h+1)*HD)
            e = n*2+h
            o = o_in[r, hs]; dm = dmix[r, hs]
            gg = pre[r, 768+h*HD:768+(h+1)*HD]
            sg = sigmoid(gg); si = gg*sg
            ms = jnp.mean(o*o, axis=1, keepdims=True)
            sc = lax.rsqrt(jnp.maximum(ms, HEAD_FLOOR))
            on = o*sc
            gn = gain[...]
            dpre[r, 768+h*HD:768+(h+1)*HD] = (dm * on * gn * (sg * (1.0 + gg*(1.0-sg)))).astype(BF)
            dgs = dm * on * si
            dgain[...] += jnp.sum(dgs.reshape(8, 8, HD), axis=0)
            dn = dm * gn * si
            corr = jnp.where(ms > HEAD_FLOOR, jnp.mean(dn*on, axis=1, keepdims=True), 0.0)
            do = sc * (dn - on*corr)
            do_s[r, hs] = do
            pdo = d3(p_in[e], do, TN)
            qw = jnp.concatenate([qk[r, hs], w_in[r, hs]], axis=0)
            dd = jnp.concatenate([do, -pdo], axis=0)
            e_s[e] = d3(qw, dd, TN)
        return 0
    lax.fori_loop(0, NB // 2, twice(phase_a), 0)
    def phase_b(i, ds):
        n = NB-1-i
        out = []
        for h in range(heads):
            e = n*2+h
            d = ds[h]
            ee = e_s[e]
            e_s[e] = d
            out.append((d - d3(m_in[e], d, TN) + ee) * persist[n])
        return tuple(out)
    zs = jnp.zeros((HD, HD), F32)
    lax.fori_loop(0, NB, phase_b, (zs, zs))
    def phase_c(i, heads_dc):
        blocks = (NB - 1 - 2 * i, NB - 2 - 2 * i)
        todo = [(n, pl.ds(pl.multiple_of(n * BLOCK, BLOCK), BLOCK), h, slice(h*HD, (h+1)*HD)) for n in blocks for h in range(heads)]
        def every(f, *lists):
            return [f(*v) for v in zip(*lists)]
        ns, rs, hh, hs = zip(*todo)
        es = [n*2+h for n, h in zip(ns, hh)]
        fil = [fill_ref[r, :] for r in rs]
        beta_t = [sigmoid(pre[r, 1024:1152]) for r in rs]
        q = [qk[r, c] for r, c in zip(rs, hs)]
        k = [qk[r, 256+h*HD:256+(h+1)*HD] for r, h in zip(rs, hh)]
        w = [w_in[r, c] for r, c in zip(rs, hs)]
        u = [u_in[r, c] for r, c in zip(rs, hs)]
        u2 = [u2_in[r, c] for r, c in zip(rs, hs)]
        do = [do_s[r, c] for r, c in zip(rs, hs)]
        p = [p_in[e] for e in es]
        t = [t_in[e] for e in es]
        s = [s_in[e] for e in es]
        ds = [e_s[e] for e in es]
        b = [x[:, h:h+1] for x, h in zip(beta_t, hh)]
        du2 = every(lambda p, do, k, ds: d3(p, do, TN) + d3(k, ds), p, do, k, ds)
        dp = every(lambda do, u2: jnp.where(ri >= ci, d3(do, u2, NT), 0.0), do, u2)
        g = every(lambda k: d3(k, k, NT), k)
        xs = every(lambda do, du2, s: d3(jnp.concatenate([do, -du2], axis=0), s, NT), do, du2, s)
        dq = every(lambda xs, dp, k: xs[:BLOCK] + d3(dp, k), xs, dp, k)
        xx = every(lambda t, xs, du2: d3(t, jnp.concatenate([xs[BLOCK:], du2], axis=1), TN), t, xs, du2)
        dk = every(lambda dp, q, u2, ds: d3(dp, q, TN) + d3(u2, ds, NT), dp, q, u2, ds)
        mm = every(lambda xx, w, u: jnp.where(ri > ci, -d3(xx, jnp.concatenate([w, u], axis=1), NT), 0.0), xx, w, u)
        cv = [c_in[r, 512+h*HD:512+(h+1)*HD] for r, h in zip(rs, hh)]
        sv = every(sigmoid, cv)
        bm = every(lambda b, mm: b*mm, b, mm)
        dk = every(lambda dk, bm, k, b, xx: dk + d3(bm + bm.T, k) + b*xx[:, :HD], dk, bm, k, b, xx)
        db = every(lambda mm, g, xx, k, cv, sv, fil: jnp.sum(mm*g, axis=1, keepdims=True)
                   + jnp.sum(xx[:, :HD]*k + xx[:, HD:]*(cv*sv*fil), axis=1, keepdims=True), mm, g, xx, k, cv, sv, fil)
        cq = [c_in[r, c] for r, c in zip(rs, hs)]
        ck = [c_in[r, 256+h*HD:256+(h+1)*HD] for r, h in zip(rs, hh)]
        def unit_back(c, fil, n, d):
            sg = sigmoid(c)
            y = c*sg*fil
            r = lax.rsqrt(jnp.sum(y*y, axis=1, keepdims=True) + EPSILON)
            return r*(d - n*jnp.sum(d*n, axis=1, keepdims=True))*fil*(sg*(1.0+c*(1.0-sg)))
        aq = every(unit_back, cq, fil, q, dq)
        ak = every(unit_back, ck, fil, k, dk)
        av = every(lambda b, xx, fil, sv, cv: b*xx[:, HD:]*fil*(sv*(1.0+cv*(1.0-sv))), b, xx, fil, sv, cv)
        for j, n in enumerate(blocks):
            r = rs[2*j]
            dbt = jnp.where(lane == 0, db[2*j], jnp.where(lane == 1, db[2*j+1], 0.0))
            dpre[r, 1024:1152] = (dbt*beta_t[2*j]*(1.0-beta_t[2*j])).astype(BF)
            pos = pos_ref[r, :]
            nxt = jnp.minimum(n+1, NB-1)
            posx = jnp.concatenate([pos, pos_ref[pl.ds(pl.multiple_of(nxt*BLOCK, BLOCK), 8), :]], axis=0)
            prv = jnp.maximum(n*BLOCK-8, 0)
            new = []
            for i, acts in enumerate((aq, ak, av)):
                dc = jnp.concatenate(acts[2*j:2*j+2], axis=1)
                ext = jnp.concatenate([dc, heads_dc[i]], axis=0)
                cur = pre[r, i*256:(i+1)*256]
                tail = pre[pl.ds(pl.multiple_of(prv, 8), 8), i*256:(i+1)*256]
                xext = jnp.concatenate([tail, cur], axis=0)
                dx = cw[i:i+1, :]*dc
                dcw[i] += jnp.sum((dc*cur).reshape(8, 8, 256), axis=0)
                for o in range(1, CONV):
                    z = jnp.where(posx >= o, ext, 0.0)
                    dx = dx + cw[o*3+i:o*3+i+1, :]*pltpu.roll(z, BLOCK+8-o, axis=0)[:BLOCK]
                    sh = pltpu.roll(xext, o, axis=0)[8:]
                    dcw[o*3+i] += jnp.sum(jnp.where(pos >= o, dc*sh, 0.0).reshape(8, 8, 256), axis=0)
                dpre[r, i*256:(i+1)*256] = dx.astype(BF)
                new.append(dc[:8])
            heads_dc = tuple(new)
        return heads_dc
    z8 = jnp.zeros((8, 256), F32)
    lax.fori_loop(0, NB // 2, phase_c, (z8, z8, z8))

def mixer_bwd(persist, dmix, pre, pos, fil, cw, gain, saved):
    outs = (sds(CAP,1152,dt=BF), sds(12,8,256), sds(8,HD))
    return pl.pallas_call(bwd_kernel, out_shape=outs, in_specs=[SM]+[VM]*(6+len(saved)), out_specs=[VM]*3,
        scratch_shapes=[pltpu.VMEM((2*NB,HD,HD),F32), pltpu.VMEM((CAP,256),F32)],
        compiler_params=pltpu.CompilerParams(vmem_limit_bytes=58*2**20), cost_estimate=pl.CostEstimate(flops=0, bytes_accessed=200 * 2**20, transcendentals=0),
        name="mixer_backward")(persist, dmix, pre, pos, fil, cw, gain, *saved)


MESH = pl.DeviceIdType.MESH
LINK_COST = 150 * 2**20
HBM = pl.BlockSpec(memory_space=pltpu.HBM)


def places():
    s, h, t = lax.axis_index("shard"), lax.axis_index("head"), lax.axis_index("tensor")
    return h, t, (s, h + 1, t), (s, h - 1, t), (s, h, 1 - t)


def shard_peers(m):
    s, h, t = lax.axis_index("shard"), lax.axis_index("head"), lax.axis_index("tensor")
    return [((lax.rem(s + i, m), h, t), lax.rem(s + i, m)) for i in range(1, m)]


class Carry:
    def __init__(self, hops, kinds, m, ins, outs, send, recv, here):
        self.hops, self.kinds, self.m, self.ins, self.outs = hops, kinds, m, ins, outs
        self.send, self.recv, self.here = send, recv, here
        s, self.h, self.t = lax.axis_index("shard"), lax.axis_index("head"), lax.axis_index("tensor")
        self.me = s
        self.side = s + 1 - 2 * lax.rem(s, 2)
        self.over = lax.rem(s + 2, 4)
        self.corner = lax.rem(self.side + 2, 4)

    def relayed(self, e):
        return self.hops and self.m == 4 and self.kinds[e] in ("gather", "abreast")

    def part(self, e, src, half=None):
        rows = self.ins[e].shape[0]
        span = pl.ds(0, rows) if half is None else pl.ds(half * (rows // 2), rows // 2)
        if self.kinds[e] == "gather":
            first = src * rows + (0 if half is None else half * (rows // 2))
            return self.outs[e].at[pl.ds(pl.multiple_of(first, rows // 2), span.size)]
        if self.kinds[e] == "abreast":
            w = self.ins[e].shape[1]
            return self.outs[e].at[span, pl.ds(pl.multiple_of(src * w, w), w)]
        return self.outs[e].at[src]

    def given(self, e, dst):
        if self.kinds[e] == "columns":
            w = self.ins[e].shape[1] // self.m
            return self.ins[e].at[:, pl.ds(pl.multiple_of(dst * w, w), w)]
        return self.ins[e].at[dst] if self.kinds[e] == "swap" else self.ins[e]

    def move(self, e, src, dst, i, j, to):
        return pltpu.make_async_remote_copy(src_ref=src, dst_ref=dst, send_sem=self.send.at[e, i], recv_sem=self.recv.at[e, j],
                                            device_id=(to, self.h, self.t), device_id_type=MESH)

    def copy(self, e, i, to):
        return self.move(e, self.given(e, to), self.part(e, self.me), i, self.me, to)

    def came(self, e, src):
        return self.move(e, self.given(e, src), self.part(e, src), 0, src, src)

    def hand(self, e, half):
        src, to = (self.side, self.over) if half == 0 else (self.over, self.side)
        piece = self.part(e, src, half)
        return self.move(e, piece, piece, 2 + half, src if half == 0 else self.m, to)

    def handed(self, e, half):
        piece = self.part(e, self.corner, half)
        return self.move(e, piece, piece, 2 + half, self.corner if half == 0 else self.m, self.over if half == 0 else self.side)

    def local(self, e):
        return pltpu.make_async_copy(self.given(e, self.me), self.part(e, self.me), self.here.at[e])

    def targets(self, e):
        return [self.side, self.over] if self.relayed(e) else [p[1] for p in shard_peers(self.m)]

    def greet(self):
        barrier = pltpu.get_barrier_semaphore()
        if self.kinds:
            for p, _ in shard_peers(self.m):
                pl.semaphore_signal(barrier, inc=1, device_id=p, device_id_type=MESH)
        return self.m - 1 if self.kinds else 0

    def start(self):
        for e in range(len(self.kinds)):
            for i, to in enumerate(self.targets(e)):
                self.copy(e, i, to).start()
            self.local(e).start()

    def relay(self, e):
        if e < len(self.kinds) and self.relayed(e):
            self.came(e, self.side).wait_recv()
            self.hand(e, 0).start()
            self.came(e, self.over).wait_recv()
            self.hand(e, 1).start()

    def wait(self):
        for e in range(len(self.kinds)):
            self.local(e).wait()
            for i, to in enumerate(self.targets(e)):
                self.copy(e, i, to).wait_send()
                if not self.relayed(e):
                    self.came(e, to).wait_recv()
            if self.relayed(e):
                for half in range(2):
                    self.handed(e, half).wait_recv()
                    self.hand(e, half).wait_send()


def carried(kinds, m, arrays):
    dma = pltpu.SemaphoreType.DMA
    give = {"gather": lambda a: (m * a.shape[0], a.shape[1]), "swap": lambda a: a.shape,
            "abreast": lambda a: (a.shape[0], m * a.shape[1]), "pile": lambda a: (m,) + a.shape,
            "columns": lambda a: (m, a.shape[0], a.shape[1] // m)}
    shapes = [jax.ShapeDtypeStruct(give[k](a), a.dtype) for k, a in zip(kinds, arrays)]
    e = len(kinds)
    return shapes, ([dma((e, m + 1)), dma((e, m + 1)), dma((e,))] if e else [])


def carry_of(kinds, m, refs, n_in, n_out, hops=False):
    e = len(kinds)
    ins, refs = refs[:n_in], refs[n_in:]
    c_in, refs = refs[:e], refs[e:]
    outs, refs = refs[:n_out], refs[n_out:]
    c_out, refs = refs[:e], refs[e:]
    sems = (refs[-3:] if e else (None,) * 3)
    scratch = refs[:-3] if e else refs
    return ins, outs, scratch, Carry(hops, kinds, m, c_in, c_out, *sems)


def greet(n, h, up, down, across, more=0):
    barrier = pltpu.get_barrier_semaphore()
    pl.semaphore_signal(barrier, inc=1, device_id=across, device_id_type=MESH)

    @pl.when(h < n - 1)
    def _():
        pl.semaphore_signal(barrier, inc=1, device_id=up, device_id_type=MESH)

    @pl.when(h > 0)
    def _():
        pl.semaphore_signal(barrier, inc=1, device_id=down, device_id_type=MESH)

    pl.semaphore_wait(barrier, 1 + more + (h < n - 1).astype(jnp.int32) + (h > 0).astype(jnp.int32))


def gather_kernel(n, width, m, kinds, *refs):
    (tokens, sent, place), (x, out), scratch, carry = carry_of(kinds, m, refs, 3, 2)
    outbox, inbox, deal_s, deal_r, here, up_s, up_r, down_s, down_r, core_s, core_r = scratch
    h, t, up, down, across = places()
    per_peer = outbox.shape[1]

    def cols(j):
        return out.at[:, pl.ds(pl.multiple_of((j * 2 + t) * width, width), width)]

    def other(j):
        return out.at[:, pl.ds(pl.multiple_of((j * 2 + 1 - t) * width, width), width)]

    def send(j, src, ss, rs, to):
        return pltpu.make_async_remote_copy(src_ref=src, dst_ref=cols(j), send_sem=ss.at[j], recv_sem=rs.at[j],
                                            device_id=to, device_id_type=MESH)

    greet(n, h, up, down, across, carry.greet())
    peers = shard_peers(m)
    mine = lax.axis_index("shard")
    ids = lax.broadcasted_iota(jnp.int32, (per_peer, sent.shape[1]), 0)

    def deal(i, p, src):
        return pltpu.make_async_remote_copy(src_ref=outbox.at[p[1]], dst_ref=inbox.at[src], send_sem=deal_s.at[i],
                                            recv_sem=deal_r.at[src], device_id=p[0], device_id_type=MESH)

    def pick(q):
        return dg(jnp.where(sent[...] - q * per_peer == ids, 1.0, 0.0).astype(BF), tokens[...], NN).astype(BF)

    for i, p in enumerate(peers):
        outbox[p[1]] = pick(p[1])
        deal(i, p, mine).start()
    carry.start()
    inbox[mine] = pick(mine)
    for i, p in enumerate(peers):
        deal(i, p, p[1]).wait_recv()
    lanes = lax.broadcasted_iota(jnp.int32, (STEP, m * per_peer), 1)

    def settle(i, c):
        r = pl.ds(pl.multiple_of(i * STEP, STEP), STEP)
        chosen = jnp.where(place[r, :] == lanes, 1.0, 0.0).astype(BF)
        x[r, :] = dg(chosen, inbox[...].reshape(m * per_peer, width), NN).astype(BF)
        return c

    lax.fori_loop(0, CAP // STEP, settle, 0)
    local = pltpu.make_async_copy(x, cols(h), here)
    local.start()

    @pl.when(h < n - 1)
    def _():
        send(h, x, up_s, up_r, up).start()

    @pl.when(h > 0)
    def _():
        send(h, x, down_s, down_r, down).start()

    send(h, x, core_s, core_r, across).start()
    for k in range(1, n):
        below, above = h - k, h + k

        @pl.when(below >= 0)
        def _():
            send(below, cols(below), up_s, up_r, up).wait_recv()

            @pl.when(h < n - 1)
            def _():
                send(below, cols(below), up_s, up_r, up).start()

            send(below, cols(below), core_s, core_r, across).start()

        @pl.when(above < n)
        def _():
            send(above, cols(above), down_s, down_r, down).wait_recv()

            @pl.when(h > 0)
            def _():
                send(above, cols(above), down_s, down_r, down).start()

            send(above, cols(above), core_s, core_r, across).start()

    for j in range(n):
        back = pltpu.make_async_remote_copy(src_ref=cols(j), dst_ref=other(j), send_sem=core_s.at[j], recv_sem=core_r.at[j],
                                            device_id=across, device_id_type=MESH)
        back.wait_recv()
        back.wait_send()

        @pl.when((j <= h) & (h < n - 1))
        def _():
            send(j, cols(j), up_s, up_r, up).wait_send()

        @pl.when((j >= h) & (h > 0))
        def _():
            send(j, cols(j), down_s, down_r, down).wait_send()

    local.wait()
    for i, p in enumerate(peers):
        deal(i, p, mine).wait_send()
    carry.wait()


def z_gather(n, tokens, sent, place, per_peer, collective_id, name, m, kinds, arrays):
    width = tokens.shape[1]
    dma = pltpu.SemaphoreType.DMA
    shapes, sems = carried(kinds, m, arrays)
    return pl.pallas_call(
        functools.partial(gather_kernel, n, width, m, kinds),
        out_shape=[jax.ShapeDtypeStruct((CAP, width), BF), jax.ShapeDtypeStruct((CAP, 2 * n * width), BF)] + shapes,
        in_specs=[VM] * 3 + [HBM] * len(shapes), out_specs=[VM, HBM] + [HBM] * len(shapes),
        scratch_shapes=[pltpu.VMEM((m, per_peer, width), BF)] * 2 + [dma((m,)), dma((m,)), dma] + [dma((n,))] * 6 + sems,
        compiler_params=pltpu.CompilerParams(collective_id=collective_id, has_side_effects=True, vmem_limit_bytes=32 * 2**20),
        cost_estimate=pl.CostEstimate(flops=0, bytes_accessed=LINK_COST, transcendentals=0),
        name=name,
    )(tokens, sent, place, *arrays)


STEP = 128


def group_peers(n):
    s, h, t = lax.axis_index("shard"), lax.axis_index("head"), lax.axis_index("tensor")
    peers = []
    for i in range(1, 2 * n):
        hh, tt = lax.rem(h + i // 2, n), lax.rem(t + i % 2, 2)
        peers.append(((s, hh, tt), hh * 2 + tt))
    return peers


def greet_group(n, more=0):
    barrier = pltpu.get_barrier_semaphore()
    for p, _ in group_peers(n):
        pl.semaphore_signal(barrier, inc=1, device_id=p, device_id_type=MESH)
    pl.semaphore_wait(barrier, 2 * n - 1 + more)


def finish_kernel(n, width, m, kinds, *refs):
    (part, kept, scale, base, gain, share, small, sent, place), (tokens, every), scratch, carry = carry_of(kinds, m, refs, 9, 2)
    (low, dgain, outbox, inbox, deal_s, deal_r, held, ours, shard_s, shard_r, group_s, group_r,
     acc, tots, tot_s, tot_r, mine, theirs, from_below, from_above,
     here, core_s, core_r, up_s, up_r, down_s, down_r) = scratch
    h, t, up, down, across = places()

    def cols(j, c):
        return part.at[:, pl.ds(pl.multiple_of((j * 2 + c) * width, width), width)]

    def swap(j):
        return pltpu.make_async_remote_copy(src_ref=cols(j, 1 - t), dst_ref=theirs.at[j], send_sem=core_s.at[j],
                                            recv_sem=core_r.at[j], device_id=across, device_id_type=MESH)

    def own(j):
        return pltpu.make_async_copy(cols(j, t), mine.at[j], here.at[j])

    def rise(k):
        return pltpu.make_async_remote_copy(src_ref=mine.at[n - 1 - k], dst_ref=from_below.at[k], send_sem=up_s.at[k],
                                            recv_sem=up_r.at[k], device_id=up, device_id_type=MESH)

    def fall(k):
        return pltpu.make_async_remote_copy(src_ref=mine.at[k], dst_ref=from_above.at[k], send_sem=down_s.at[k],
                                            recv_sem=down_r.at[k], device_id=down, device_id_type=MESH)

    def total(j, extra):
        def step(i, c):
            r = pl.ds(pl.multiple_of(i * STEP, STEP), STEP)
            v = mine[j, r, :].astype(F32) + theirs[j, r, :].astype(F32)
            if extra is not None:
                v = v + extra(r).astype(F32)
            mine[j, r, :] = v.astype(BF)
            return c
        lax.fori_loop(0, CAP // STEP, step, 0)

    order = [j for i in range(n // 2) for j in (n - 1 - i, i)]
    for j in order:
        own(j).start()
    greet_group(n, carry.greet())
    me = h * 2 + t
    peers = group_peers(n)

    def tot_copy(i, p, dst):
        return pltpu.make_async_remote_copy(src_ref=share, dst_ref=tots.at[dst], send_sem=tot_s.at[i], recv_sem=tot_r.at[dst],
                                            device_id=p, device_id_type=MESH)

    for i, p in enumerate(peers):
        tot_copy(i, p[0], me).start()
    for j in order:
        swap(j).start()
    carry.start()

    def arrive(j):
        own(j).wait()
        swap(j).wait_recv()

    for tick in range(2 * n - 2):
        ku = tick - h
        tu = n - 1 - ku

        @pl.when((ku >= 0) & (tu > h))
        def _():
            arrive(tu)

            @pl.when(h == 0)
            def _():
                total(tu, None)

            @pl.when(h > 0)
            def _():
                rise(ku).wait_recv()
                total(tu, lambda r: from_below[ku, r, :])

            rise(ku).start()

        kd = tick - (n - 1 - h)

        @pl.when((kd >= 0) & (kd < h))
        def _():
            arrive(kd)

            @pl.when(h == n - 1)
            def _():
                total(kd, None)

            @pl.when(h < n - 1)
            def _():
                fall(kd).wait_recv()
                total(kd, lambda r: from_above[kd, r, :])

            fall(kd).start()

    arrive(h)
    for i, p in enumerate(peers):
        tot_copy(i, p[0], p[1]).wait_recv()
    tots[me] = share[...]
    for i, p in enumerate(peers):
        tots[me] = tots[me] + tots[p[1]]
    dgain[...] = jnp.zeros_like(dgain)
    gains = gain[...]
    eighth = jnp.full((8, 128), 0.125, BF)

    def final(get):
        def step(i, c):
            r = pl.ds(pl.multiple_of(i * STEP, STEP), STEP)
            acc[r, :] = get(r)
            return c
        lax.fori_loop(0, CAP // STEP, step, 0)

    final(lambda r: mine[h, r, :].astype(F32) + theirs[h, r, :].astype(F32))

    def first(get):
        final(lambda r: acc[r, :] + get(r).astype(F32))

    @pl.when((h > 0) & (h < n - 1))
    def _():
        @pl.when(2 * h < n)
        def _():
            fall(h).wait_recv()
            first(lambda r: from_above[h, r, :])

        @pl.when(2 * h >= n)
        def _():
            rise(n - 1 - h).wait_recv()
            first(lambda r: from_below[n - 1 - h, r, :])

    by_below = (h > 0) & ((2 * h < n) | (h == n - 1))

    @pl.when(by_below)
    def _():
        rise(n - 1 - h).wait_recv()

    @pl.when(jnp.logical_not(by_below))
    def _():
        fall(h).wait_recv()

    def close(get):
        def step(i, c):
            r = pl.ds(pl.multiple_of(i * STEP, STEP), STEP)
            hi, lo = split(tots[me, i])
            total_r = dg(hi, eighth, TN) + dg(lo, eighth, TN)
            sc = scale[r, :]
            kp = kept[r, :].astype(F32)
            dn = acc[r, :] + get(r).astype(F32)
            back = base[r, :].astype(F32) + sc * (gains * dn) - kp * jnp.tile((sc * sc * sc) * (total_r * (1.0 / D)), (1, width // 128))
            low[r, :] = back.astype(BF)
            dgain[...] += jnp.sum((dn * kp * sc).reshape(STEP // 8, 8, width), axis=0)
            return c
        lax.fori_loop(0, CAP // STEP, step, 0)

    @pl.when(by_below)
    def _():
        close(lambda r: from_below[n - 1 - h, r, :])

    @pl.when(jnp.logical_not(by_below))
    def _():
        close(lambda r: from_above[h, r, :])

    for i, p in enumerate(peers):
        tot_copy(i, p[0], me).wait_send()

    others = shard_peers(m)
    shard = lax.axis_index("shard")
    per_peer = outbox.shape[1]
    ids = lax.broadcasted_iota(jnp.int32, (per_peer, place.shape[1]), 0)

    def back(i, p, src):
        return pltpu.make_async_remote_copy(src_ref=outbox.at[p[1]], dst_ref=inbox.at[src], send_sem=deal_s.at[i],
                                            recv_sem=deal_r.at[src], device_id=p[0], device_id_type=MESH)

    def pick(q):
        return dg(jnp.where(place[...] - q * per_peer == ids, 1.0, 0.0).astype(BF), low[...], NN).astype(BF)

    def over(i, p, src):
        return pltpu.make_async_remote_copy(src_ref=ours, dst_ref=held.at[src], send_sem=shard_s.at[i],
                                            recv_sem=shard_r.at[src], device_id=p[0], device_id_type=MESH)

    def along(i, p, src):
        return pltpu.make_async_remote_copy(src_ref=held.at[shard], dst_ref=every.at[src], send_sem=group_s.at[i],
                                            recv_sem=group_r.at[src], device_id=p[0], device_id_type=MESH)

    for i, p in enumerate(others):
        outbox[p[1]] = pick(p[1])
        back(i, p, shard).start()
    at = lax.broadcasted_iota(jnp.int32, small.shape, 0)
    ours[...] = small[...] + jnp.where(at == 12, jnp.sum(dgain[...], axis=0, keepdims=True), 0.0)
    for i, p in enumerate(others):
        over(i, p, shard).start()
    inbox[shard] = pick(shard)
    v = ours[...]
    for i, p in enumerate(others):
        over(i, p, p[1]).wait_recv()
        v = v + held[p[1]]
    held[shard] = v
    every[me] = v
    for i, p in enumerate(peers):
        along(i, p, me).start()
    for i, p in enumerate(others):
        back(i, p, p[1]).wait_recv()
    lanes = lax.broadcasted_iota(jnp.int32, (STEP, m * per_peer), 1)

    def settle(i, c):
        r = pl.ds(pl.multiple_of(i * STEP, STEP), STEP)
        chosen = jnp.where(sent[r, :] == lanes, 1.0, 0.0).astype(BF)
        tokens[r, :] = dg(chosen, inbox[...].reshape(m * per_peer, width), NN)
        return c

    lax.fori_loop(0, REAL_DEV // STEP, settle, 0)
    for i, p in enumerate(peers):
        along(i, p, p[1]).wait_recv()
        along(i, p, me).wait_send()
    for i, p in enumerate(others):
        over(i, p, shard).wait_send()
        back(i, p, shard).wait_send()
    for j in range(n):
        swap(j).wait_send()
    for k in range(n - 1):
        @pl.when(n - 1 - k > h)
        def _():
            rise(k).wait_send()

        @pl.when(k < h)
        def _():
            fall(k).wait_send()
    carry.wait()


def z_finish(n, part, kept, scale, base, gain, share, small, sent, place, per_peer, collective_id, name, m, kinds, arrays):
    rows, width = part.shape[0], part.shape[1] // (2 * n)
    dma = pltpu.SemaphoreType.DMA
    shapes, sems = carried(kinds, m, arrays)
    return pl.pallas_call(
        functools.partial(finish_kernel, n, width, m, kinds),
        out_shape=[jax.ShapeDtypeStruct((REAL_DEV, width), F32), jax.ShapeDtypeStruct((2 * n,) + small.shape, F32)] + shapes,
        in_specs=[HBM] + [VM] * 8 + [HBM] * len(shapes), out_specs=[VM] * 2 + [HBM] * len(shapes),
        scratch_shapes=[pltpu.VMEM((rows, width), BF), pltpu.VMEM((8, width), F32)]
        + [pltpu.VMEM((m, per_peer, width), BF)] * 2 + [dma((m,))] * 2
        + [pltpu.VMEM((m,) + small.shape, F32), pltpu.VMEM(small.shape, F32), dma((m,)), dma((m,)), dma((2 * n,)), dma((2 * n,))]
        + [pltpu.VMEM((rows, width), F32), pltpu.VMEM((2 * n, rows // STEP, 8, STEP), F32), dma((2 * n,)), dma((2 * n,))]
        + [pltpu.VMEM((n, rows, width), BF)] * 2 + [pltpu.VMEM((n - 1, rows, width), BF)] * 2
        + [dma((n,))] * 3 + [dma((n - 1,))] * 4 + sems,
        compiler_params=pltpu.CompilerParams(collective_id=collective_id, has_side_effects=True, vmem_limit_bytes=48 * 2**20),
        cost_estimate=pl.CostEstimate(flops=0, bytes_accessed=LINK_COST, transcendentals=0),
        name=name,
    )(part, kept, scale, base, gain, share, small, sent, place, *arrays)


CHUNKS = 4
SUBS = 4
UNITS = CHUNKS * SUBS
UNIT = CAP // UNITS


def turn_kernel(n, width, m, kinds, norm, *refs):
    if norm:
        (part, kept, scale, base, gain, share), (out, full, low, dgain), scratch, carry = carry_of(kinds, m, refs, 6, 4)
        tots, tot_s, tot_r = scratch[-3:]
        scratch = scratch[:-3]
    else:
        (part, base), (out, full, low), scratch, carry = carry_of(kinds, m, refs, 2, 3, True)
    (mine, theirs, from_below, from_above, here, core_s, core_r, up_s, up_r, down_s, down_r,
     gu_s, gu_r, gd_s, gd_r, gc_s, gc_r, flat) = scratch
    h, t, up, down, across = places()
    me = h * 2 + t
    chunks = CHUNKS

    def rows(u):
        return pl.ds(pl.multiple_of(u * UNIT, UNIT), UNIT)

    def wide(r):
        return pl.ds(pl.multiple_of(r * SUBS * UNIT, SUBS * UNIT), SUBS * UNIT)

    def lanes(j, c):
        return pl.ds(pl.multiple_of((j * 2 + c) * width, width), width)

    def remote(src, dst, ss, rs, to):
        return pltpu.make_async_remote_copy(src_ref=src, dst_ref=dst, send_sem=ss, recv_sem=rs, device_id=to, device_id_type=MESH)

    def swap(j, r):
        return remote(part.at[wide(r), lanes(j, 1 - t)], theirs.at[j, wide(r)], core_s.at[j, r], core_r.at[j, r], across)

    def own(j, r):
        return pltpu.make_async_copy(part.at[wide(r), lanes(j, t)], mine.at[j, wide(r)], here.at[j, r])

    def rise(k, u):
        return remote(mine.at[n - 1 - k, rows(u)], from_below.at[k, rows(u)], up_s.at[k, u], up_r.at[k, u], up)

    def fall(k, u):
        return remote(mine.at[k, rows(u)], from_above.at[k, rows(u)], down_s.at[k, u], down_r.at[k, u], down)

    def spread(j, u, src, ss, rs, to):
        return remote(src, full.at[rows(u), lanes(j, t)], ss.at[j, u], rs.at[j, u], to)

    def piece(j, u):
        return full.at[rows(u), lanes(j, t)]

    def tot_copy(i, p, dst):
        return remote(share, tots.at[dst], tot_s.at[i], tot_r.at[dst], p)

    order = [j for i in range(n // 2) for j in (n - 1 - i, i)]
    for r in range(chunks):
        for j in order:
            own(j, r).start()
    if norm:
        greet_group(n, carry.greet())
        for i, p in enumerate(group_peers(n)):
            tot_copy(i, p[0], me).start()
        dgain[...] = jnp.zeros_like(dgain)
    else:
        greet(n, h, up, down, across, carry.greet())
    for r in range(chunks):
        for j in order:
            swap(j, r).start()
    carry.start()

    def arrive(j, r):
        own(j, r).wait()
        swap(j, r).wait_recv()

    def both(j, u):
        return mine[j, rows(u), :].astype(F32) + theirs[j, rows(u), :].astype(F32)

    def climb(o, r, s):
        u = SUBS * r + s

        @pl.when(h <= o)
        def _():
            ku = o - h
            tu = n - 1 - ku
            if s == 0:
                arrive(tu, r)

            @pl.when(h == 0)
            def _():
                mine[tu, rows(u), :] = both(tu, u).astype(BF)

            @pl.when(h > 0)
            def _():
                rise(ku, u).wait_recv()
                mine[tu, rows(u), :] = (both(tu, u) + from_below[ku, rows(u), :].astype(F32)).astype(BF)

            rise(ku, u).start()

        @pl.when(h >= n - 1 - o)
        def _():
            kd = o - (n - 1 - h)
            if s == 0:
                arrive(kd, r)

            @pl.when(h == n - 1)
            def _():
                mine[kd, rows(u), :] = both(kd, u).astype(BF)

            @pl.when(h < n - 1)
            def _():
                fall(kd, u).wait_recv()
                mine[kd, rows(u), :] = (both(kd, u) + from_above[kd, rows(u), :].astype(F32)).astype(BF)

            fall(kd, u).start()

    def gather_totals():
        for i, p in enumerate(group_peers(n)):
            tot_copy(i, p[0], p[1]).wait_recv()
        tots[me] = share[...]
        for i, p in enumerate(group_peers(n)):
            tots[me] = tots[me] + tots[p[1]]

    def last(r, s):
        u = SUBS * r + s
        if s == 0:
            arrive(h, r)
        flat[rows(u), :] = both(h, u)

        @pl.when(h > 0)
        def _():
            k = n - 1 - h
            rise(k, u).wait_recv()
            flat[rows(u), :] = flat[rows(u), :] + from_below[k, rows(u), :].astype(F32)

        @pl.when(h < n - 1)
        def _():
            fall(h, u).wait_recv()
            flat[rows(u), :] = flat[rows(u), :] + from_above[h, rows(u), :].astype(F32)

        if norm:
            close(u)
        else:
            v = base[rows(u), :].astype(F32) + flat[rows(u), :]
            out[rows(u), :] = v
            low[rows(u), :] = v.astype(BF)
            set_out(u)

    def close(u):
        hi, lo = split(tots[me, u])
        eighth = jnp.full((8, 128), 0.125, BF)
        total_r = (dg(hi, eighth, TN) + dg(lo, eighth, TN))[:UNIT]
        sc = scale[rows(u), :]
        kp = kept[rows(u), :].astype(F32)
        dn = flat[rows(u), :]
        v = (base[rows(u), :].astype(F32) + sc * (gain[...] * dn)
             - kp * jnp.tile((sc * sc * sc) * (total_r * (1.0 / D)), (1, width // 128)))
        out[rows(u), :] = v
        low[rows(u), :] = v.astype(BF)
        dgain[...] += jnp.sum((dn * kp * sc).reshape(UNIT // 8, 8, width), axis=0)
        set_out(u)

    def set_out(u):
        src = low.at[rows(u)]

        @pl.when(h < n - 1)
        def _():
            spread(h, u, src, gu_s, gu_r, up).start()

        @pl.when(h > 0)
        def _():
            spread(h, u, src, gd_s, gd_r, down).start()

        spread(h, u, src, gc_s, gc_r, across).start()

    def pass_on(k, r, s):
        u = SUBS * r + s
        below, above = h - k, h + k

        @pl.when(below >= 0)
        def _():
            spread(below, u, piece(below, u), gu_s, gu_r, up).wait_recv()

            @pl.when(h < n - 1)
            def _():
                spread(below, u, piece(below, u), gu_s, gu_r, up).start()

            spread(below, u, piece(below, u), gc_s, gc_r, across).start()

        @pl.when(above < n)
        def _():
            spread(above, u, piece(above, u), gd_s, gd_r, down).wait_recv()

            @pl.when(h > 0)
            def _():
                spread(above, u, piece(above, u), gd_s, gd_r, down).start()

            spread(above, u, piece(above, u), gc_s, gc_r, across).start()

    def at(o, r, s):
        if o < n - 1:
            climb(o, r, s)
        elif o == n - 1:
            if norm and s == 0:
                @pl.when(r == 0)
                def _():
                    gather_totals()
            last(r, s)
        elif o < 2 * n - 1:
            pass_on(o - n + 1, r, s)

    def period(r, c):
        for e in range(len(kinds)):
            @pl.when(r == e + 1)
            def _():
                carry.relay(e)

        for o in range(n):
            for s in range(SUBS):
                @pl.when(r > 0)
                def _():
                    at(o + n, r - 1, s)

                @pl.when(r < chunks)
                def _():
                    at(o, r, s)
        return c

    lax.fori_loop(0, chunks + 1, period, 0)
    mine_out = pltpu.make_async_copy(low, full.at[:, lanes(h, t)], here.at[0, 0])
    mine_out.start()

    def drain(u, c):
        for j in range(n):
            back = remote(piece(j, u), full.at[rows(u), lanes(j, 1 - t)], gc_s.at[j, u], gc_r.at[j, u], across)
            back.wait_recv()
            back.wait_send()

            @pl.when((j <= h) & (h < n - 1))
            def _():
                spread(j, u, piece(j, u), gu_s, gu_r, up).wait_send()

            @pl.when((j >= h) & (h > 0))
            def _():
                spread(j, u, piece(j, u), gd_s, gd_r, down).wait_send()

        for k in range(n - 1):
            @pl.when(n - 1 - k > h)
            def _():
                rise(k, u).wait_send()

            @pl.when(k < h)
            def _():
                fall(k, u).wait_send()

        return c

    if norm:
        for i, p in enumerate(group_peers(n)):
            tot_copy(i, p[0], me).wait_send()
    lax.fori_loop(0, UNITS, drain, 0)
    for r in range(chunks):
        for j in range(n):
            swap(j, r).wait_send()
    mine_out.wait()
    carry.wait()


def z_turn(n, part, base, collective_id, name, m=1, kinds=(), arrays=(), norm=None):
    rows, width = part.shape[0], part.shape[1] // (2 * n)
    dma = pltpu.SemaphoreType.DMA
    shapes, sems = carried(kinds, m, arrays)
    shape = jax.ShapeDtypeStruct
    ins = [part, base] if norm is None else [part, norm[0], norm[1], base, norm[2], norm[3]]
    outs = [shape((rows, width), F32), shape((rows, 2 * n * width), BF), shape((rows, width), BF)]
    out_specs = [VM, HBM, VM]
    more = []
    if norm is not None:
        outs, out_specs = outs + [shape((8, width), F32)], out_specs + [VM]
        more = [pltpu.VMEM((2 * n, UNITS, 8, 128), F32), dma((2 * n,)), dma((2 * n,))]
    return pl.pallas_call(
        functools.partial(turn_kernel, n, width, m, kinds, norm is not None),
        out_shape=outs + shapes,
        in_specs=[HBM] + [VM] * (len(ins) - 1) + [HBM] * len(shapes), out_specs=out_specs + [HBM] * len(shapes),
        scratch_shapes=[pltpu.VMEM((n, rows, width), BF)] * 2 + [pltpu.VMEM((n - 1, rows, width), BF)] * 2
        + [dma((n, CHUNKS))] * 3 + [dma((n - 1, UNITS))] * 4 + [dma((n, UNITS))] * 6 + [pltpu.VMEM((rows, width), F32)]
        + more + sems,
        compiler_params=pltpu.CompilerParams(collective_id=collective_id, has_side_effects=True, vmem_limit_bytes=40 * 2**20),
        cost_estimate=pl.CostEstimate(flops=0, bytes_accessed=LINK_COST, transcendentals=0),
        name=name,
    )(*ins, *arrays)


PRE = 1152
GROUP = ("head", "tensor")


def int_sum(values, along_axis):
    return jnp.sum(values, axis=along_axis)


def before(values):
    at = jnp.arange(values.shape[0], dtype=jnp.int32)
    return int_sum(jnp.where(at[None, :] < at[:, None], values[None, :], 0), 1)


def layout(seq_lengths, starts, dealing, group_idx):
    total_seqs = seq_lengths.shape[0]
    chosen = lax.dynamic_slice_in_dim(dealing, group_idx * SEQ_DEV, SEQ_DEV)
    picked = (chosen[:, None] == jnp.arange(total_seqs, dtype=jnp.int32)[None, :]).astype(jnp.int32)
    own_length = int_sum(picked * seq_lengths[None, :], 1)
    own_start = int_sum(picked * starts[None, :], 1)
    padded = (own_length + BLOCK - 1) // BLOCK * BLOCK
    buffer_start = before(padded)
    row_ids = jnp.arange(CAP, dtype=jnp.int32)
    member = int_sum((row_ids[:, None] >= buffer_start[None, :]).astype(jnp.int32), 1) - 1
    owned_by = (member[:, None] == jnp.arange(SEQ_DEV, dtype=jnp.int32)[None, :]).astype(jnp.int32)
    position = row_ids - int_sum(owned_by * buffer_start[None, :], 1)
    row_length = int_sum(owned_by * own_length[None, :], 1)
    seq_first = int_sum(owned_by * own_start[None, :], 1)
    filled = position < row_length
    return (seq_first + position, position, filled, seq_first, own_start, own_length)


def congruent(lower_end, upper_end, residue, modulus):
    return (upper_end - 1 - residue) // modulus - (lower_end - 1 - residue) // modulus


def mm(left, right, dims=NN):
    return lax.dot_general(left, right, dims, preferred_element_type=F32)


def full_rows(piece_in):
    return lax.all_gather(piece_in, GROUP, axis=1, tiled=True)


def shares(partial_sum):
    return lax.psum_scatter(partial_sum.astype(BF), GROUP, scatter_dimension=1, tiled=True).astype(F32)


def column_blocks(grad, m):
    rows, wide = grad.shape[0], grad.shape[1] // m
    if wide % 128 == 0:
        return "columns", grad
    return "swap", grad.reshape(rows, m, wide).transpose(1, 0, 2)


def side_by_side(wide):
    return "abreast" if wide % 128 == 0 else "pile"


def level(weights):
    if weights.ndim == 2:
        return weights
    return weights.transpose(1, 0, 2).reshape(weights.shape[1], -1)


def swap_ring(*grads):
    shards, device = lax.axis_size("shard"), lax.axis_index("shard")
    wide = grads[0].shape[1] // shards

    def block(i):
        at = lax.rem(device + i, shards) * wide
        return jnp.concatenate([lax.dynamic_slice_in_dim(g, at, wide, 1) for g in grads], axis=0)

    total = block(0).astype(F32)
    for i in range(1, shards):
        total = total + lax.ppermute(block(i), "shard", [(a, (a + i) % shards) for a in range(shards)]).astype(F32)
    ends = [0]
    for g in grads:
        ends.append(ends[-1] + g.shape[0])
    return [total[i:j] for i, j in zip(ends, ends[1:])]


def along_lanes(values, units):
    rows = values.reshape(units, 1, -1)
    return jnp.broadcast_to(jnp.pad(rows, ((0, 0), (0, 0), (0, 128 - rows.shape[2]))), (units, 8, 128))


def sum_blocks(blocks):
    return jnp.sum(blocks.astype(F32), axis=0)


def body(tokens, seq_lengths, dealing, gain_mixer, w_query, w_key, w_value, w_gate, w_beta, conv_weight,
         gain_heads, w_out, gain_ffn, w_up_gate, w_up, w_down, cotangent):
    shards = lax.axis_size("shard")
    device = lax.axis_index("shard")
    width = tokens.shape[2]
    col_start = lax.axis_index(GROUP) * width
    per_peer = (CAP // shards + SEQ_DEV + 15) // 16 * 16
    total_seqs = seq_lengths.shape[0]

    w_piece = jnp.concatenate(
        [w_query, w_key, w_value, w_gate, w_beta, jnp.zeros((w_beta.shape[0], PRE - 4 * width - w_beta.shape[1]), BF)], axis=1)

    starts = before(seq_lengths)
    finish = starts + seq_lengths
    own_rows = tokens.reshape(REAL_DEV, width)
    own_ids = jnp.arange(REAL_DEV, dtype=jnp.int32)
    packed_ids = own_ids * shards + device
    inside = ((packed_ids[:, None] >= starts[None, :]) & (packed_ids[:, None] < finish[None, :])).astype(jnp.int32)
    seq_ids = jnp.arange(total_seqs, dtype=jnp.int32)
    matches = (dealing[:, None] == seq_ids[None, :]).astype(jnp.int32)
    seq_home = int_sum(matches * (seq_ids // SEQ_DEV)[:, None], 0)
    held = congruent(starts, finish, device, shards)
    ahead = (seq_home[:, None] == seq_home[None, :]) & (seq_ids[None, :] < seq_ids[:, None])
    seq_slot = (seq_home * per_peer + int_sum(jnp.where(ahead, held[None, :], 0), 1)
                - 1 - (starts - 1 - device) // shards)
    sent_slot = int_sum(inside * seq_slot[None, :], 1) + own_ids
    natural, position, filled, seq_first, own_start, own_length = layout(seq_lengths, starts, dealing, device)
    source = natural % shards
    earlier = own_start[None, :] < seq_first[:, None]
    span_counts = congruent(own_start[None, :], (own_start + own_length)[None, :], source[:, None], shards)
    arrival = int_sum(jnp.where(earlier, span_counts, 0), 1) + congruent(seq_first, natural, source, shards)
    recv_slot = jnp.where(filled, source * per_peer + arrival, -1)
    filled_f = filled.astype(F32)[:, None]
    persist = (position.reshape(-1, BLOCK)[:, 0] != 0).astype(F32)
    pos = position[:, None]
    taps = conv_weight.reshape(3 * CONV, width)
    head_gain = gain_heads[None, :]

    n = lax.axis_size("head")
    side = side_by_side(w_up.shape[0])
    x_rows, rows_full, w_in, w_o = z_gather(
        n, own_rows, sent_slot[None, :], recv_slot[:, None], per_peer, 1, "gather_rows", shards, ("gather", side), (w_piece, w_out))
    w_o = level(w_o)
    rows_full, cot_piece = lax.optimization_barrier((rows_full, cotangent))
    cot_full = full_rows(cot_piece)
    rows_full = rows_full.astype(F32)
    scale_one = lax.rsqrt(jnp.mean(rows_full * rows_full, axis=1) + EPSILON)
    normed = lax.optimization_barrier((rows_full * scale_one[:, None] * gain_mixer[None, :]).astype(BF))
    pre = mm(normed, w_in)
    mixed, *saved = mixer_fwd(persist, pre, pos, filled_f, taps, head_gain)
    branch_part, cot_full = lax.optimization_barrier((mm(mixed, w_o).astype(BF), cot_full))
    hidden, held_full, held_low, w_ug, w_u, w_d = z_turn(
        n, branch_part, x_rows, 2, "turn_branch", shards, (side,) * 3, (w_up_gate.T, w_up.T, w_down))
    w_ug, w_u, w_d = level(w_ug), level(w_u), level(w_d)
    held_full = held_full.astype(F32)
    scale_two = lax.rsqrt(jnp.mean(held_full * held_full, axis=1) + EPSILON)
    normed_two = lax.optimization_barrier((held_full * scale_two[:, None] * gain_ffn[None, :]).astype(BF))
    gate_act = mm(normed_two, w_ug, NT)
    up_act = mm(normed_two, w_u, NT)
    sig = jax.nn.sigmoid(gate_act)
    product = (gate_act * sig * up_act).astype(BF)
    d_product = mm(cot_full, w_d, NT)
    d_gate = (d_product * up_act * sig * (1.0 + gate_act * (1.0 - sig))).astype(BF)
    d_up = (d_product * gate_act * sig).astype(BF)
    share_two = jnp.sum(d_gate.astype(F32) * gate_act + d_up.astype(F32) * up_act, axis=1) / scale_two
    d_normed_two = (mm(d_gate, w_ug) + mm(d_up, w_u)).astype(BF)
    down_kind, d_w_down = column_blocks(mm(product, cot_full, TN).astype(BF), shards)
    gate_kind, d_w_ug = column_blocks(mm(d_gate, normed_two, TN).astype(BF), shards)
    d_w_u = mm(d_up, normed_two, TN).astype(BF)
    ffn_gain_part = lax.dynamic_slice_in_dim(gain_ffn, col_start, width)[None, :]
    d_hidden, d_branch_full, _, ffn_gain_grad, d_w_ug, d_w_down = z_turn(
        n, d_normed_two, cotangent, 4, "turn_normed_two", shards, (gate_kind, down_kind), (d_w_ug, d_w_down),
        norm=(held_low, scale_two[:, None], ffn_gain_part, along_lanes(share_two, UNITS)))
    out_part = mm(product, w_d).astype(BF)
    out_part, d_branch_full = lax.optimization_barrier((out_part, d_branch_full))
    d_w_u, d_w_out = swap_ring(d_w_u, mm(mixed, d_branch_full, TN).astype(BF))
    out_sum = shares(out_part)
    d_mixed = mm(d_branch_full, w_o, NT)
    d_pre, d_taps, d_head_gain = mixer_bwd(persist, d_mixed, pre, pos, filled_f, taps, head_gain, saved)
    d_normed = mm(d_pre, w_in, NT).astype(BF)
    share_one = jnp.sum(d_pre.astype(F32) * pre, axis=1) / scale_one
    d_w_in = mm(normed, d_pre, TN).astype(BF).reshape(shards, w_piece.shape[0], PRE)
    d_normed, out_sum = lax.optimization_barrier((d_normed, out_sum))
    block_out = (hidden + out_sum).astype(BF)
    mixer_gain_part = lax.dynamic_slice_in_dim(gain_mixer, col_start, width)[None, :]
    small = jnp.concatenate([
        jnp.sum(d_taps, axis=1), jnp.zeros((1, width), F32), jnp.sum(ffn_gain_grad, axis=0)[None, :],
        jnp.pad(jnp.sum(d_head_gain, axis=0), (0, width - HD))[None, :],
        jnp.zeros((1, width), F32)], axis=0)
    d_tokens, summed, d_w_in = z_finish(
        n, d_normed, x_rows, scale_one[:, None], d_hidden, mixer_gain_part, along_lanes(share_one, CAP // STEP), small,
        sent_slot[:, None], recv_slot[None, :], per_peer, 6, "finish_rows", shards, ("swap",), (d_w_in,))
    d_tokens = d_tokens.reshape(REAL_DEV, 1, width)
    d_w_in = sum_blocks(d_w_in)
    by_row = summed.transpose(1, 0, 2).reshape(16, D)
    d_conv = by_row[:12].reshape(CONV, 3, D)
    d_gain_heads = jnp.sum(summed[:, 14, :HD], axis=0)
    cut = [0, width, 2 * width, 3 * width, 4 * width]
    return (
        block_out, d_tokens, by_row[12],
        d_w_in[:, cut[0]:cut[1]], d_w_in[:, cut[1]:cut[2]], d_w_in[:, cut[2]:cut[3]], d_w_in[:, cut[3]:cut[4]],
        d_w_in[:, 4 * width:4 * width + w_beta.shape[1]],
        d_conv, d_gain_heads, d_w_out, by_row[13],
        sum_blocks(d_w_ug).T, d_w_u.T, sum_blocks(d_w_down),
    )


def solution(mesh):
    feat = ("head", "tensor")
    placed = (
        P(None, "shard", feat), P(), P(), P(),
        P("shard", feat), P("shard", feat), P("shard", feat), P("shard", feat), P("shard", feat),
        P(None, None, feat), P(), P(feat, "shard"), P(),
        P("shard", feat), P("shard", feat), P(feat, "shard"), P("shard", feat),
    )
    given = (
        P("shard", feat), P(None, "shard", feat), P(),
        P("shard", feat), P("shard", feat), P("shard", feat), P("shard", feat), P("shard", feat),
        P(), P(), P(feat, "shard"), P(),
        P("shard", feat), P("shard", feat), P(feat, "shard"),
    )
    return jax.shard_map(body, mesh=mesh, in_specs=placed, out_specs=given, check_vma=False)
```

time: 743 us -> 609 us (0.82)
  Pallas kernels: 472 us -> 398 us
  matrix products: 134 us -> 108 us
  waiting for transfers between devices: 22.1 us -> 0.04 us
  local copies, waits for them, and re-layouts: 50.2 us -> 34.7 us
  other arithmetic: 34.9 us -> 44.9 us
    pallas_call x3 -> x1, Pallas kernels: 159 us -> 75.8 us  [z_gather(): pl.pallas_call(functools.partial(gather_kernel, n, width, m, kinds), out_...]
    pallas_call x4 -> x3, Pallas kernels: 201 us -> 237 us  [the longest x2 168 us: z_turn(): pl.pallas_call(functools.partial(turn_kernel, n, width, m, kinds, norm is...]
    dot_general x19 -> x15, matrix products: 134 us -> 108 us  [mm(): return lax.dot_general(left, right, dims, preferred_element_type=F32)]
    pallas_call x1, Pallas kernels: 65.9 us -> 45.5 us  [mixer_bwd(): pl.pallas_call(bwd_kernel, out_shape=outs, in_specs=[SM] + [VM] * (6 + le...]
    all_to_all x2 -> x0, waiting for transfers between devices: 11.1 us -> none  [the longest x1 6.39 us: body(): lax.all_to_all(outbox.reshape(shards, per_peer, width), 'shard', split_ax...]
    all_gather x1, waiting for transfers between devices: 10.3 us -> 0.01 us  [full_rows(): return lax.all_gather(piece_in, GROUP, axis=1, tiled=True)]
    convert_element_type x2 -> x0, local copies, waits for them, and re-layouts: 9.35 us -> none  [the longest x1 4.74 us: body(): d_w_ug = mm(normed_two, d_gate, TN).astype(BF).reshape(blocks)]
    all_to_all x2 -> x0, starting transfers between devices: 8.64 us -> none  [the longest x1 5.16 us: body(): lax.all_to_all(outbox.reshape(shards, per_peer, width), 'shard', split_ax...]
  transfers between devices with their start and end apart: 6 -> 5, of which waited for: 3 -> 0; matrix products, arithmetic and copies ran while one was open for 14% -> 13% of each run, Pallas kernels for 29% -> 14%
where the time goes in v2:
time: 609 us; the launch traced here: 605 us
  Pallas kernels  398 us (65%)
  matrix products  108 us (18%)
  other arithmetic  44.9 us (7%)
  local copies, waits for them, and re-layouts  34.7 us (6%)
  between operations  15.1 us (2%)
    pallas_call x2, Pallas kernels, z_turn(): pl.pallas_call(functools.partial(turn_kernel, n, width, m, kinds, norm is...  168 us
    dot_general x15, matrix products, mm(): return lax.dot_general(left, right, dims, preferred_element_type=F32)  108 us
    pallas_call x1, Pallas kernels, z_gather(): pl.pallas_call(functools.partial(gather_kernel, n, width, m, kinds), out_...  75.8 us
    pallas_call x1, Pallas kernels, z_finish(): pl.pallas_call(functools.partial(finish_kernel, n, width, m, kinds), out_...  69.5 us
    pallas_call x1, Pallas kernels, mixer_bwd(): pl.pallas_call(bwd_kernel, out_shape=outs, in_specs=[SM] + [VM] * (6 + le...  45.5 us
    pallas_call x1, Pallas kernels, mixer_fwd(): pl.pallas_call(fwd_kernel, out_shape=outs, in_specs=[SM] + [VM] * 5, out_...  39.1 us
    unnamed x115, local copies, waits for them, and re-layouts  23.4 us
  transfers between devices with their start and end apart: 5, of which 0 were waited for; matrix products, arithmetic and copies ran while one was open for 13% of the time, Pallas kernels for 14%

profile of v2, /device:TPU:0, one launch (start us, length us, event | category | flops | bytes accessed | tf_op | source)
XLA Modules:
  0.0 605.1 jit_solution(3114744494649064626)
XLA Ops:
  14.0 2.7 reshape_subtract_fusion
  16.7 2.5 concatenate.18.refs_3_
  21.2 75.8 %gather_rows.1 = (bf16[1280,256]{1,0:T(8,128)(2,1)S(1)}, bf16[1280,2048]{1,0:T(8,128)(2,1)S(1)}, bf16[2048,1152]{1,0:T(8,128)(2,1)S(1)}, bf16[256,2048]{1,0:T(8,128)(2,1)S(1)}) custom-call(bf16[1152,256]{1,0:T(8,128)(2,1)S(1)} %bitcast.54, s32[1,1152]{1,0:T(1,128)S(1)} %iota_add_fusion.refs_1_, s32[1280,1]{1,0:T(8,128)S(1)} %get-tuple-element.197.refs_2_, ...), custom_call_target="tpu_custom_call" | custom-call | bytes 157286400 | tf_op jit(solution)/shard_map/gather_rows/pallas_call | solution.py:518
  97.0 2.3 copy-done
  102.5 3.7 fusion
  106.9 3.5 fusion.2
  113.3 11.8 %fusion.37.pre = f32[1280,1152]{1,0:T(8,128)} fusion(bf16[1280,2048]{1,0:T(8,128)(2,1)} %fusion.2, bf16[2048,1152]{1,0:T(8,128)(2,1)} %copy-done.23), kind=kOutput, calls=%fused_computation.170 | convolution fusion | flops 6039797760 | bytes 15859712 | tf_op jit(solution)/shard_map/dot_general | solution.py:1121
  125.1 39.1 %mixer_forward.1 = (bf16[1280,256]{1,0:T(8,128)(2,1)}, f32[1280,768]{1,0:T(8,128)}, f32[1280,512]{1,0:T(8,128)}, f32[1280,256]{1,0:T(8,128)}, f32[1280,256]{1,0:...) custom-call(f32[20]{0:T(128)} %convert_reduce_fusion.4.persist, ...), custom_call_target="tpu_custom_call" | custom-call | bytes 146800640 | tf_op jit(solution)/shard_map/mixer_forward/pallas_call | solution.py:146
  164.2 5.0 convolution_convert_fusion.3.refs_0_
  171.5 82.3 %turn_branch.1 = (f32[1280,256]{1,0:T(8,128)S(1)}, bf16[1280,2048]{1,0:T(8,128)(2,1)}, bf16[1280,256]{1,0:T(8,128)(2,1)S(1)}, bf16[704,2048]{1,0:T(8,128)(2,1)S(...) custom-call(bf16[1280,2048]{1,0:T(8,128)(2,1)} %convolution_convert_fusion.3.refs_0_, ...), custom_call_target="tpu_custom_call" | custom-call | bytes 157286400 | tf_op jit(solution)/shard_map/turn_branch/pallas_call | solution.py:1072
  253.8 5.4 fusion.3
  260.9 8.3 %fusion.39 = f32[1280,704]{0,1:T(8,128)S(1)} fusion(bf16[1280,2048]{1,0:T(8,128)(2,1)} %all-gather.2.cloned.1.call-done, bf16[704,2048]{1,0:T(8,128)(2,1)S(1)} %get-tuple-element.67), kind=kOutput, calls=%fused_computation.172 | convolution fusion | flops 3690987520 | bytes 11730944 | tf_op jit(solution)/shard_map/dot_general | solution.py:1121
  269.2 3.9 fusion.38
  273.2 8.4 %add_reduce_fusion = (f32[1280]{0:T(1024)}, bf16[1280,704]{0,1:T(8,128)(2,1)}, bf16[1280,704]{0,1:T(8,128)(2,1)S(1)}, bf16[1280,704]{0,1:T(8,128)(2,1)}) fusion(f32[1280,704]{0,1:T(8,128)S(1)} %fusion.38, f32[1280,704]{0,1:T(8,128)S(1)} %fusion.39, bf16[1280,2048]{1,0:T(8,128)(2,1)S(1)} %fusion.5, bf16[704,2048]{1,0:T(8,128)(2,1)S(1)} %get-tuple-element.66), kind=kOutput, calls=%fused_computation.19 | convolution fusion | flops 3710810880 | bytes 20747264 | tf_op jit(solution)/shard_map/dot_general | solution.py:1121
  281.5 4.1 convolution_convert_fusion.6.refs_6_
  285.7 6.8 %fusion.40 = f32[1280,2048]{1,0:T(8,128)} fusion(bf16[1280,704]{0,1:T(8,128)(2,1)S(1)} %get-tuple-element.177, bf16[704,2048]{1,0:T(8,128)(2,1)S(1)} %get-tuple-element.65), kind=kOutput, calls=%fused_computation.173 | convolution fusion | flops 3690987520 | bytes 15171584 | tf_op jit(solution)/shard_map/dot_general | solution.py:1121
  292.7 5.2 convolution_convert_fusion.5.refs_7_
  297.9 6.2 %convolution_convert_fusion.2 = bf16[1280,2048]{1,0:T(8,128)(2,1)} fusion(bf16[1280,704]{0,1:T(8,128)(2,1)S(1)} %copy-done.50, bf16[704,2048]{1,0:T(8,128)(2,1)S(1)} %get-tuple-element.67), kind=kOutput, calls=%fused_computation.14 | convolution fusion | flops 3693608960 | bytes 9928704 | tf_op jit(solution)/shard_map/dot_general | solution.py:1121
  306.3 12.2 %add_convert_fusion.refs_0_ = bf16[1280,2048]{1,0:T(8,128)(2,1)} fusion(f32[1280,2048]{1,0:T(8,128)} %fusion.40, bf16[1280,704]{0,1:T(8,128)(2,1)} %get-tuple-element.176, bf16[704,2048]{1,0:T(8,128)(2,1)} %copy-done.24), kind=kOutput, calls=%fused_computation.10 | convolution fusion | flops 3696230400 | bytes 20414464 | tf_op jit(solution)/shard_map/dot_general | solution.py:1121
  318.5 85.5 %turn_normed_two.1 = (f32[1280,256]{1,0:T(8,128)S(1)}, bf16[1280,2048]{1,0:T(8,128)(2,1)}, bf16[1280,256]{1,0:T(8,128)(2,1)}, f32[8,256]{1,0:T(8,128)S(1)}, bf16...) custom-call(bf16[1280,2048]{1,0:T(8,128)(2,1)} %add_convert_fusion.refs_0_, ...), custom_call_target="tpu_custom_call" | custom-call | bytes 157286400 | tf_op jit(solution)/shard_map/turn_normed_two/pallas_call | solution.py:1072
  410.2 4.2 convolution_convert_fusion.7
  414.5 6.7 %convolution_convert_fusion.4 = bf16[704,2048]{1,0:T(8,128)(2,1)S(1)} fusion(bf16[1280,704]{0,1:T(8,128)(2,1)S(1)} %copy-done.49, bf16[1280,2048]{1,0:T(8,128)(2,1)} %copy-done.26), kind=kOutput, calls=%fused_computation.24 | convolution fusion | flops 3692429312 | bytes 9928704 | tf_op jit(solution)/shard_map/dot_general | solution.py:1121
  426.9 2.2 collective-permute-start.2
  429.2 2.7 fusion.41.dmix
  431.9 45.5 %mixer_backward.1 = (bf16[1280,1152]{1,0:T(8,128)(2,1)}, f32[12,8,256]{2,1,0:T(8,128)}, f32[8,128]{1,0:T(8,128)}) custom-call(f32[20]{0:T(128)} %convert_reduce_fusion.4.persist, f32[1280,256]{1,0:T(8,128)} %fusion.41.dmix, f32[1280,1152]{1,0:T(8,128)} %fusion.37.pre, s32[1280,1]{1,0:T(8,128)} %get-tuple-element.196.pos_ref, f32[1280,1]{1,0:T(8,128)} %fusion.17.fill_ref, ...), custom_call_target="tpu_custom_call" | custom-call | bytes 209715200 | tf_op jit(solution)/shard_map/mixer_backward/pallas_call | solution.py:270
  479.0 11.5 %convolution_convert_fusion = bf16[2048,1152]{1,0:T(8,128)(2,1)} fusion(bf16[1280,2048]{1,0:T(8,128)(2,1)} %fusion.2, bf16[1280,1152]{1,0:T(8,128)(2,1)} %get-tuple-element.82), kind=kOutput, calls=%fused_computation.12 | convolution fusion | flops 6042157056 | bytes 12910592 | tf_op jit(solution)/shard_map/dot_general | solution.py:1121
  490.5 11.1 %convolution_convert_fusion.1.refs_0_ = bf16[1280,2048]{1,0:T(8,128)(2,1)} fusion(bf16[1280,1152]{1,0:T(8,128)(2,1)S(1)} %copy-done.28, bf16[2048,1152]{1,0:T(8,128)(2,1)} %copy-done.23), kind=kOutput, calls=%fused_computation.13 | convolution fusion | flops 6042419200 | bytes 12910592 | tf_op jit(solution)/shard_map/dot_general | solution.py:1121
  501.6 3.6 multiply_reduce_fusion
  513.1 2.3 convert_element_type.129
  515.4 69.5 %finish_rows.1 = (f32[1152,256]{1,0:T(8,128)S(1)}, f32[8,16,256]{2,1,0:T(8,128)S(1)}, bf16[4,512,1152]{2,1,0:T(8,128)(2,1)}) custom-call(bf16[1280,2048]{1,0:T(8,128)(2,1)} %convolution_convert_fusion.1.refs_0_, bf16[1280,256]{1,0:T(8,128)(2,1)S(1)} %copy-done.8, f32[1280,1]{1,0:T(8,128)S(1)} %rsqrt.41.refs_2_, f32[1280,256]{1,0:T(8,128)S(1)} %copy-done.12, ...), custom_call_target="tpu_custom_call" | custom-call | bytes 157286400 | tf_op jit(solution)/shard_map/finish_rows/pallas_call | solution.py:779
  584.9 3.5 convert_reduce_fusion
  590.5 4.6 copy.113
  (186 shorter events, 48.1 us)
Async XLA Ops:
  7.2 162.1 %all-gather.2.cloned.1.call-start = ((), (), s32[]{:S(2)}) async-start(), calls=%async_computation.1 | async-start | bytes 5898240 | tf_op jit(solution)/shard_map/all_gather | solution.py:1125
  101.4 62.8 %copy-start.14 = (bf16[256,2048]{1,0:T(8,128)(2,1)}, bf16[256,2048]{1,0:T(8,128)(2,1)S(1)}, u32[]{:S(2)}) copy-start(bf16[256,2048]{1,0:T(8,128)(2,1)S(1)} %get-tuple-element.59) | copy-start | bytes 3145732
  101.4 67.8 %copy-start.7 = (bf16[1280,256]{1,0:T(8,128)(2,1)}, bf16[1280,256]{1,0:T(8,128)(2,1)S(1)}, u32[]{:S(2)}) copy-start(bf16[1280,256]{1,0:T(8,128)(2,1)S(1)} %get-tuple-element.62.refs_1_) | copy-start | bytes 1966084
  101.4 5.4 copy-start.48
  101.4 411.7 %reduce-scatter.2.cloned.1.call-start = ((), (), s32[]{:S(2)}) async-start(), calls=%async_computation.2 | async-start | bytes 5898240 | tf_op jit(solution)/shard_map/reduce_scatter | solution.py:1129
  102.5 4.3 copy-start.1
  106.8 4.9 copy-start.31
  106.8 4.9 copy-start.36
  164.2 5.0 copy-start.16
  253.8 7.1 %copy-start.9 = (f32[1280,256]{1,0:T(8,128)}, f32[1280,256]{1,0:T(8,128)S(1)}, u32[]{:S(2)}) copy-start(f32[1280,256]{1,0:T(8,128)S(1)} %get-tuple-element.63) | copy-start | bytes 3932164
  253.8 7.1 %copy-start.19 = (bf16[1280,256]{1,0:T(8,128)(2,1)}, bf16[1280,256]{1,0:T(8,128)(2,1)S(1)}, u32[]{:S(2)}) copy-start(bf16[1280,256]{1,0:T(8,128)(2,1)S(1)} %get-tuple-element.69.refs_1_) | copy-start | bytes 1966084
  253.8 19.3 %copy-start.24 = (bf16[704,2048]{1,0:T(8,128)(2,1)}, bf16[704,2048]{1,0:T(8,128)(2,1)S(1)}, u32[]{:S(2)}) copy-start(bf16[704,2048]{1,0:T(8,128)(2,1)S(1)} %get-tuple-element.66) | copy-start | bytes 8650756
  253.8 5.8 copy-start.25
  260.9 20.7 %copy-start.26 = (bf16[1280,2048]{1,0:T(8,128)(2,1)}, bf16[1280,2048]{1,0:T(8,128)(2,1)S(1)}, u32[]{:S(2)}) copy-start(bf16[1280,2048]{1,0:T(8,128)(2,1)S(1)} %fusion.5) | copy-start | bytes 15728644
  281.5 11.1 %slice-start.2 = ((s8[5242880]{0:T(1024)(128)(4,1)}), s8[4194304]{0:T(1024)(128)(4,1)S(1)}, s32[]{:S(2)}) async-start(s8[5242880]{0:T(1024)(128)(4,1)} %bitcast.69), calls=%async_computation.5 | async-start | bytes 8388608
  285.6 7.1 %slice-start.3 = ((s8[5242880]{0:T(1024)(128)(4,1)}), s8[1048576]{0:T(1024)(128)(4,1)S(1)}, s32[]{:S(2)}) async-start(s8[5242880]{0:T(1024)(128)(4,1)} %bitcast.69), calls=%async_computation.6 | async-start | bytes 2097152
  285.6 7.1 %copy-start.50 = (bf16[1280,704]{0,1:T(8,128)(2,1)S(1)}, bf16[1280,704]{0,1:T(8,128)(2,1)}, u32[]{:S(2)}) copy-start(bf16[1280,704]{0,1:T(8,128)(2,1)} %get-tuple-element.181) | copy-start | bytes 5406724
  306.3 12.2 %copy-start.6 = (bf16[1280,256]{1,0:T(8,128)(2,1)S(1)}, bf16[1280,256]{1,0:T(8,128)(2,1)}, u32[]{:S(2)}) copy-start(bf16[1280,256]{1,0:T(8,128)(2,1)} %refs_3_.1) | copy-start | bytes 1966084
  306.3 12.2 %copy-start.20 = (bf16[1280,256]{1,0:T(8,128)(2,1)S(1)}, bf16[1280,256]{1,0:T(8,128)(2,1)}, u32[]{:S(2)}) copy-start(bf16[1280,256]{1,0:T(8,128)(2,1)} %copy-done.19) | copy-start | bytes 1966084
  410.2 4.3 copy-start.49
  414.4 14.8 %slice-start = ((s8[5242880]{0:T(1024)(128)(4,1)}), s8[4194304]{0:T(1024)(128)(4,1)S(1)}, s32[]{:S(2)}) async-start(s8[5242880]{0:T(1024)(128)(4,1)} %bitcast.67), calls=%async_computation.3 | async-start | bytes 8388608
  414.5 14.6 %slice-start.1 = ((s8[5242880]{0:T(1024)(128)(4,1)}), s8[1048576]{0:T(1024)(128)(4,1)S(1)}, s32[]{:S(2)}) async-start(s8[5242880]{0:T(1024)(128)(4,1)} %bitcast.67), calls=%async_computation.4 | async-start | bytes 2097152
  421.6 7.5 %copy-start.15 = (bf16[256,2048]{1,0:T(8,128)(2,1)S(1)}, bf16[256,2048]{1,0:T(8,128)(2,1)}, u32[]{:S(2)}) copy-start(bf16[256,2048]{1,0:T(8,128)(2,1)} %copy-done.14) | copy-start | bytes 3145732
  422.7 86.4 %collective-permute-start = (bf16[960,512]{1,0:T(8,128)(2,1)}, bf16[960,512]{1,0:T(8,128)(2,1)S(1)}, u32[]{:S(2)}, u32[]{:S(2)}) collective-permute-start(bf16[960,512]{1,0:T(8,128)(2,1)} %pad_maximum_fusion), channel_id=1, source_target_pairs={{0,8},{8,16},{16,24},{24,0},{1,9},{9,17},{17,25},{25,1},{2,10},{10... | collective-permute-start | bytes 2949128 | tf_op jit(solution)/shard_map/ppermute | solution.py:1159
  425.2 83.9 %collective-permute-start.1 = (bf16[960,512]{1,0:T(8,128)(2,1)}, bf16[960,512]{1,0:T(8,128)(2,1)}, u32[]{:S(2)}, u32[]{:S(2)}) collective-permute-start(bf16[960,512]{1,0:T(8,128)(2,1)} %pad_maximum_fusion.1), channel_id=1, source_target_pairs={{0,16},{8,24},{16,0},{24,8},{1,17},{9,25},{17,1},{25,9},{2,18},{10... | collective-permute-start | bytes 2949128 | tf_op jit(solution)/shard_map/ppermute | solution.py:1159
  426.9 82.2 %collective-permute-start.2 = (bf16[960,512]{1,0:T(8,128)(2,1)}, bf16[960,512]{1,0:T(8,128)(2,1)}, u32[]{:S(2)}, u32[]{:S(2)}) collective-permute-start(bf16[960,512]{1,0:T(8,128)(2,1)} %pad_maximum_fusion.2), channel_id=1, source_target_pairs={{0,24},{8,0},{16,8},{24,16},{1,25},{9,1},{17,9},{25,17},{2,26},{10... | collective-permute-start | bytes 2949128 | tf_op jit(solution)/shard_map/ppermute | solution.py:1159
  479.0 11.5 %copy-start.28 = (bf16[1280,1152]{1,0:T(8,128)(2,1)S(1)}, bf16[1280,1152]{1,0:T(8,128)(2,1)}, u32[]{:S(2)}) copy-start(bf16[1280,1152]{1,0:T(8,128)(2,1)} %get-tuple-element.82) | copy-start | bytes 8847364
  511.1 4.3 copy-start.8
  511.1 4.3 copy-start.12
  584.9 4.9 copy-start.13
  588.4 8.7 %copy-start.10 = (f32[1280,256]{1,0:T(8,128)S(1)}, f32[1280,256]{1,0:T(8,128)}, u32[]{:S(2)}) copy-start(f32[1280,256]{1,0:T(8,128)} %copy-done.9) | copy-start | bytes 3932164
  588.4 8.6 %copy-start.27 = (f32[1280,256]{1,0:T(8,128)S(1)}, f32[1280,256]{1,0:T(8,128)}, u32[]{:S(2)}) copy-start(f32[1280,256]{1,0:T(8,128)} %convert_element_type.129) | copy-start | bytes 3932164
  (28 other events, 55.0 us)
Sparse Core Ops, SparseCore 0:
  101.6 57.0 all-gather.1
  408.3 58.6 reduce-scatter.1

commit v3 on v2

--- a/solution.py
+++ b/solution.py
@@ -36,6 +36,10 @@
 def twice(step):
     return lambda i, c: step(2 * i + 1, step(2 * i, c))
 
+def goes_on(pos_ref, n):
+    first = pos_ref[pl.ds(pl.multiple_of(n * BLOCK, BLOCK), 8), :][:1]
+    return jnp.where(first != 0, 1.0, 0.0)
+
 def masks():
     ri = lax.broadcasted_iota(jnp.int32, (BLOCK, BLOCK), 0)
     ci = lax.broadcasted_iota(jnp.int32, (BLOCK, BLOCK), 1)
@@ -63,7 +67,14 @@
         s *= 2
     return xs
 
-def fwd_kernel(persist, pre, pos_ref, fill_ref, cw, gain, mixed, c_out, qk, w_out, u_out, u2_out, o_out, p_out, t_out, m_out, s_out, b_s):
+def fwd_kernel(pre, pos_ref, fill_ref, cw, gain, mixed, *refs):
+    given, (c_out, qk, w_out, u_out, u2_out, o_out, p_out, t_out, m_out, s_out, b_s), sem = refs[:10], refs[10:21], refs[21]
+    held = (c_out, qk, w_out, u_out, u2_out, o_out, p_out, t_out, m_out, s_out)
+
+    def keep(*which):
+        for i in which:
+            pltpu.make_async_copy(held[i], given[i], sem.at[i]).start()
+
     ri, ci = masks()
     heads = 2
     def phase_a(n, tails):
@@ -95,6 +106,7 @@
         return tuple(new_tails)
     z8 = jnp.zeros((8, 256), F32)
     lax.fori_loop(0, NB // 2, twice(phase_a), (z8, z8, z8))
+    keep(0, 1, 6)
     GRP = 8
     def phase_t(i, _):
         ts = inverses([t_out[i*GRP+j] for j in range(GRP)], ri, ci)
@@ -102,6 +114,7 @@
             t_out[i*GRP+j] = ts[j]
         return 0
     lax.fori_loop(0, 2*NB//GRP, phase_t, 0)
+    keep(7)
     def phase_w(i, _):
         todo = [(n, pl.ds(pl.multiple_of(n * BLOCK, BLOCK), BLOCK), h, slice(h*HD, (h+1)*HD)) for n in (2*i, 2*i+1) for h in range(heads)]
         wu = [d3(t_out[n*2+h], jnp.concatenate([w_out[r, c], u_out[r, c]], axis=1)) for n, r, h, c in todo]
@@ -111,16 +124,18 @@
             m_out[n*2+h] = y[:, :HD]; b_s[n*2+h] = y[:, HD:]
         return 0
     lax.fori_loop(0, NB//2, phase_w, 0)
+    keep(2, 3, 8)
     def phase_b(n, ss):
         out = []
         for h in range(heads):
             e = n*2+h
-            s = ss[h] * persist[n]
+            s = ss[h] * goes_on(pos_ref, n)
             s_out[e] = s
             out.append(s - d3(m_out[e], s) + b_s[e])
         return tuple(out)
     zs = jnp.zeros((HD, HD), F32)
     lax.fori_loop(0, NB, phase_b, (zs, zs))
+    keep(9)
     def phase_c(i, _):
         todo = [(n, pl.ds(pl.multiple_of(n * BLOCK, BLOCK), BLOCK), h, slice(h*HD, (h+1)*HD)) for n in (2*i, 2*i+1) for h in range(heads)]
         rr = [d3(jnp.concatenate([w_out[r, c], qk[r, c]], axis=0), s_out[n*2+h]) for n, r, h, c in todo]
@@ -135,21 +150,33 @@
             mixed[r, c] = (o * sc * gain[...] * (gg * sigmoid(gg))).astype(BF)
         return 0
     lax.fori_loop(0, NB // 2, phase_c, 0)
+    keep(4, 5)
+    for i in range(10):
+        pltpu.make_async_copy(held[i], given[i], sem.at[i]).wait()
 
 def sds(*s, dt=F32): return jax.ShapeDtypeStruct(s, dt)
 VM = pl.BlockSpec(memory_space=pltpu.VMEM)
 SM = pl.BlockSpec(memory_space=pltpu.SMEM)
 
-def mixer_fwd(persist, pre, pos, fil, cw, gain):
+def mixer_fwd(pre, pos, fil, cw, gain):
     outs = (sds(CAP,256,dt=BF), sds(CAP,768), sds(CAP,512), sds(CAP,256), sds(CAP,256), sds(CAP,256), sds(CAP,256),
             sds(2*NB,BLOCK,BLOCK), sds(2*NB,BLOCK,BLOCK), sds(2*NB,HD,HD), sds(2*NB,HD,HD))
-    return pl.pallas_call(fwd_kernel, out_shape=outs, in_specs=[SM]+[VM]*5, out_specs=[VM]*len(outs),
-        scratch_shapes=[pltpu.VMEM((2*NB,HD,HD),F32)],
-        compiler_params=pltpu.CompilerParams(vmem_limit_bytes=56*2**20), cost_estimate=pl.CostEstimate(flops=0, bytes_accessed=140 * 2**20, transcendentals=0),
-        name="mixer_forward")(persist, pre, pos, fil, cw, gain)
-
-def bwd_kernel(persist, dmix, pre, pos_ref, fill_ref, cw, gain, c_in, qk, w_in, u_in, u2_in, o_in, p_in, t_in, m_in, s_in,
-               dpre, dcw, dgain, e_s, do_s):
+    return pl.pallas_call(fwd_kernel, out_shape=outs, in_specs=[VM]*5, out_specs=[VM]+[pl.BlockSpec(memory_space=pltpu.HBM)]*(len(outs)-1),
+        scratch_shapes=[pltpu.VMEM(o.shape,F32) for o in outs[1:]]+[pltpu.VMEM((2*NB,HD,HD),F32), pltpu.SemaphoreType.DMA((10,))],
+        compiler_params=pltpu.CompilerParams(vmem_limit_bytes=60*2**20), cost_estimate=pl.CostEstimate(flops=0, bytes_accessed=140 * 2**20, transcendentals=0),
+        name="mixer_forward")(pre, pos, fil, cw, gain)
+
+def bwd_kernel(dmix, pre, pos_ref, fill_ref, cw, gain, *refs):
+    kept, (dpre, dcw, dgain), held, (e_s, do_s, sem) = refs[:10], refs[10:13], refs[13:23], refs[23:]
+    c_in, qk, w_in, u_in, u2_in, o_in, p_in, t_in, m_in, s_in = held
+
+    def fetch(i):
+        return pltpu.make_async_copy(kept[i], held[i], sem.at[i])
+
+    for i in (5, 6, 1, 2, 8, 7, 9, 0, 3, 4):
+        fetch(i).start()
+    for i in (5, 6, 1, 2):
+        fetch(i).wait()
     ri, ci = masks()
     heads = 2
     lane = lax.broadcasted_iota(jnp.int32, (BLOCK, HD), 1)
@@ -180,6 +207,8 @@
             e_s[e] = d3(qw, dd, TN)
         return 0
     lax.fori_loop(0, NB // 2, twice(phase_a), 0)
+    fetch(8).wait()
+
     def phase_b(i, ds):
         n = NB-1-i
         out = []
@@ -188,10 +217,13 @@
             d = ds[h]
             ee = e_s[e]
             e_s[e] = d
-            out.append((d - d3(m_in[e], d, TN) + ee) * persist[n])
+            out.append((d - d3(m_in[e], d, TN) + ee) * goes_on(pos_ref, n))
         return tuple(out)
     zs = jnp.zeros((HD, HD), F32)
     lax.fori_loop(0, NB, phase_b, (zs, zs))
+    for i in (7, 9, 0, 3, 4):
+        fetch(i).wait()
+
     def phase_c(i, heads_dc):
         blocks = (NB - 1 - 2 * i, NB - 2 - 2 * i)
         todo = [(n, pl.ds(pl.multiple_of(n * BLOCK, BLOCK), BLOCK), h, slice(h*HD, (h+1)*HD)) for n in blocks for h in range(heads)]
@@ -265,15 +297,16 @@
     z8 = jnp.zeros((8, 256), F32)
     lax.fori_loop(0, NB // 2, phase_c, (z8, z8, z8))
 
-def mixer_bwd(persist, dmix, pre, pos, fil, cw, gain, saved):
+def mixer_bwd(dmix, pre, pos, fil, cw, gain, saved):
     outs = (sds(CAP,1152,dt=BF), sds(12,8,256), sds(8,HD))
-    return pl.pallas_call(bwd_kernel, out_shape=outs, in_specs=[SM]+[VM]*(6+len(saved)), out_specs=[VM]*3,
-        scratch_shapes=[pltpu.VMEM((2*NB,HD,HD),F32), pltpu.VMEM((CAP,256),F32)],
-        compiler_params=pltpu.CompilerParams(vmem_limit_bytes=58*2**20), cost_estimate=pl.CostEstimate(flops=0, bytes_accessed=200 * 2**20, transcendentals=0),
-        name="mixer_backward")(persist, dmix, pre, pos, fil, cw, gain, *saved)
+    return pl.pallas_call(bwd_kernel, out_shape=outs, in_specs=[VM]*6+[pl.BlockSpec(memory_space=pltpu.HBM)]*len(saved), out_specs=[VM]*3,
+        scratch_shapes=[pltpu.VMEM(a.shape, F32) for a in saved]+[pltpu.VMEM((2*NB,HD,HD),F32), pltpu.VMEM((CAP,256),F32), pltpu.SemaphoreType.DMA((10,))],
+        compiler_params=pltpu.CompilerParams(vmem_limit_bytes=60*2**20), cost_estimate=pl.CostEstimate(flops=0, bytes_accessed=200 * 2**20, transcendentals=0),
+        name="mixer_backward")(dmix, pre, pos, fil, cw, gain, *saved)
 
 
 MESH = pl.DeviceIdType.MESH
+ROOM = 60 * 2**20
 LINK_COST = 150 * 2**20
 HBM = pl.BlockSpec(memory_space=pltpu.HBM)
 
@@ -412,9 +445,62 @@
     pl.semaphore_wait(barrier, 1 + more + (h < n - 1).astype(jnp.int32) + (h > 0).astype(jnp.int32))
 
 
+class Plan:
+    def __init__(self, m, per_peer, lengths, dealing, starts):
+        self.m, self.per_peer, self.lengths, self.dealing, self.starts = m, per_peer, lengths, dealing, starts
+        self.shift = m.bit_length() - 1
+        self.device = lax.axis_index("shard")
+
+        def begin(q, total):
+            starts[q] = total
+            return total + lengths[q]
+
+        lax.fori_loop(0, lengths.shape[0], begin, jnp.int32(0))
+
+    def under(self, row, residue):
+        return lax.shift_right_arithmetic(row - 1 - residue + self.m, self.shift + jnp.zeros_like(row))
+
+    def members(self, g):
+        at = [self.dealing[g * SEQ_DEV + i] for i in range(SEQ_DEV)]
+        return [(self.starts[q], self.lengths[q]) for q in at]
+
+    def sent(self, ids):
+        packed = ids * self.m + self.device
+
+        def group(g, slot):
+            seqs = self.members(g)
+            counts = [self.under(s + n, self.device) - self.under(s, self.device) for s, n in seqs]
+            for s, n in seqs:
+                first = g * self.per_peer - self.under(s, self.device)
+                for (other, _), count in zip(seqs, counts):
+                    first = first + jnp.where(other < s, count, 0)
+                slot = slot + jnp.where((packed >= s) & (packed < s + n), first, 0)
+            return slot
+
+        return lax.fori_loop(0, self.lengths.shape[0] // SEQ_DEV, group, ids)
+
+    def rows(self, ids):
+        seqs = self.members(self.device)
+        place, start, length, below = ids, jnp.zeros_like(ids), jnp.zeros_like(ids), jnp.int32(0)
+        for s, n in seqs:
+            here = ids >= below
+            place = jnp.where(here, ids - below, place)
+            start = jnp.where(here, s, start)
+            length = jnp.where(here, n, length)
+            below = below + lax.shift_right_arithmetic(n + BLOCK - 1, jnp.int32(6)) * BLOCK
+        filled = place < length
+        natural = start + place
+        source = natural & (self.m - 1)
+        slot = source * self.per_peer + self.under(natural, source) - self.under(start, source)
+        for s, n in seqs:
+            span = self.under(jnp.zeros_like(ids) + (s + n), source) - self.under(jnp.zeros_like(ids) + s, source)
+            slot = slot + jnp.where(s < start, span, 0)
+        return place, filled, jnp.where(filled, slot, -1)
+
+
 def gather_kernel(n, width, m, kinds, *refs):
-    (tokens, sent, place), (x, out), scratch, carry = carry_of(kinds, m, refs, 3, 2)
-    outbox, inbox, deal_s, deal_r, here, up_s, up_r, down_s, down_r, core_s, core_r = scratch
+    (lengths, dealing, tokens), (x, out, sent_at, slot_at, pos_at, fill_at), scratch, carry = carry_of(kinds, m, refs, 3, 6)
+    place_at, starts, outbox, inbox, deal_s, deal_r, here, up_s, up_r, down_s, down_r, core_s, core_r = scratch
     h, t, up, down, across = places()
     per_peer = outbox.shape[1]
 
@@ -429,29 +515,32 @@
                                             device_id=to, device_id_type=MESH)
 
     greet(n, h, up, down, across, carry.greet())
+    plan = Plan(m, per_peer, lengths, dealing, starts)
     peers = shard_peers(m)
     mine = lax.axis_index("shard")
-    ids = lax.broadcasted_iota(jnp.int32, (per_peer, sent.shape[1]), 0)
+    sent = plan.sent(lax.broadcasted_iota(jnp.int32, (1, REAL_DEV), 1))
+    ids = lax.broadcasted_iota(jnp.int32, (per_peer, REAL_DEV), 0)
 
     def deal(i, p, src):
         return pltpu.make_async_remote_copy(src_ref=outbox.at[p[1]], dst_ref=inbox.at[src], send_sem=deal_s.at[i],
                                             recv_sem=deal_r.at[src], device_id=p[0], device_id_type=MESH)
 
     def pick(q):
-        return dg(jnp.where(sent[...] - q * per_peer == ids, 1.0, 0.0).astype(BF), tokens[...], NN).astype(BF)
+        return dg(jnp.where(sent - q * per_peer == ids, 1.0, 0.0).astype(BF), tokens[...], NN).astype(BF)
 
     for i, p in enumerate(peers):
         outbox[p[1]] = pick(p[1])
         deal(i, p, mine).start()
     carry.start()
     inbox[mine] = pick(mine)
+    place_at[...] = plan.rows(lax.broadcasted_iota(jnp.int32, (CAP, 1), 0))[2]
     for i, p in enumerate(peers):
         deal(i, p, p[1]).wait_recv()
     lanes = lax.broadcasted_iota(jnp.int32, (STEP, m * per_peer), 1)
 
     def settle(i, c):
         r = pl.ds(pl.multiple_of(i * STEP, STEP), STEP)
-        chosen = jnp.where(place[r, :] == lanes, 1.0, 0.0).astype(BF)
+        chosen = jnp.where(place_at[r, :] == lanes, 1.0, 0.0).astype(BF)
         x[r, :] = dg(chosen, inbox[...].reshape(m * per_peer, width), NN).astype(BF)
         return c
 
@@ -468,6 +557,11 @@
         send(h, x, down_s, down_r, down).start()
 
     send(h, x, core_s, core_r, across).start()
+    sent_at[...] = plan.sent(lax.broadcasted_iota(jnp.int32, (REAL_DEV, 1), 0))
+    slot_at[...] = plan.rows(lax.broadcasted_iota(jnp.int32, (1, CAP), 1))[2]
+    position, filled, _ = plan.rows(lax.broadcasted_iota(jnp.int32, (CAP, 1), 0))
+    pos_at[...] = position
+    fill_at[...] = jnp.where(filled, 1.0, 0.0)
     for k in range(1, n):
         below, above = h - k, h + k
 
@@ -511,19 +605,22 @@
     carry.wait()
 
 
-def z_gather(n, tokens, sent, place, per_peer, collective_id, name, m, kinds, arrays):
+def z_gather(n, lengths, dealing, tokens, per_peer, collective_id, name, m, kinds, arrays):
     width = tokens.shape[1]
     dma = pltpu.SemaphoreType.DMA
+    sd = jax.ShapeDtypeStruct
     shapes, sems = carried(kinds, m, arrays)
     return pl.pallas_call(
         functools.partial(gather_kernel, n, width, m, kinds),
-        out_shape=[jax.ShapeDtypeStruct((CAP, width), BF), jax.ShapeDtypeStruct((CAP, 2 * n * width), BF)] + shapes,
-        in_specs=[VM] * 3 + [HBM] * len(shapes), out_specs=[VM, HBM] + [HBM] * len(shapes),
-        scratch_shapes=[pltpu.VMEM((m, per_peer, width), BF)] * 2 + [dma((m,)), dma((m,)), dma] + [dma((n,))] * 6 + sems,
-        compiler_params=pltpu.CompilerParams(collective_id=collective_id, has_side_effects=True, vmem_limit_bytes=32 * 2**20),
+        out_shape=[sd((CAP, width), BF), sd((CAP, 2 * n * width), BF), sd((REAL_DEV, 1), jnp.int32), sd((1, CAP), jnp.int32),
+                   sd((CAP, 1), jnp.int32), sd((CAP, 1), F32)] + shapes,
+        in_specs=[SM, SM, VM] + [HBM] * len(shapes), out_specs=[VM, HBM] + [VM] * 4 + [HBM] * len(shapes),
+        scratch_shapes=[pltpu.VMEM((CAP, 1), jnp.int32), pltpu.SMEM(lengths.shape, jnp.int32)]
+        + [pltpu.VMEM((m, per_peer, width), BF)] * 2 + [dma((m,)), dma((m,)), dma] + [dma((n,))] * 6 + sems,
+        compiler_params=pltpu.CompilerParams(collective_id=collective_id, has_side_effects=True, vmem_limit_bytes=ROOM),
         cost_estimate=pl.CostEstimate(flops=0, bytes_accessed=LINK_COST, transcendentals=0),
         name=name,
-    )(tokens, sent, place, *arrays)
+    )(lengths, dealing, tokens, *arrays)
 
 
 STEP = 128
@@ -786,7 +883,7 @@
         + [pltpu.VMEM((rows, width), F32), pltpu.VMEM((2 * n, rows // STEP, 8, STEP), F32), dma((2 * n,)), dma((2 * n,))]
         + [pltpu.VMEM((n, rows, width), BF)] * 2 + [pltpu.VMEM((n - 1, rows, width), BF)] * 2
         + [dma((n,))] * 3 + [dma((n - 1,))] * 4 + sems,
-        compiler_params=pltpu.CompilerParams(collective_id=collective_id, has_side_effects=True, vmem_limit_bytes=48 * 2**20),
+        compiler_params=pltpu.CompilerParams(collective_id=collective_id, has_side_effects=True, vmem_limit_bytes=ROOM),
         cost_estimate=pl.CostEstimate(flops=0, bytes_accessed=LINK_COST, transcendentals=0),
         name=name,
     )(part, kept, scale, base, gain, share, small, sent, place, *arrays)
@@ -1076,45 +1173,104 @@
         scratch_shapes=[pltpu.VMEM((n, rows, width), BF)] * 2 + [pltpu.VMEM((n - 1, rows, width), BF)] * 2
         + [dma((n, CHUNKS))] * 3 + [dma((n - 1, UNITS))] * 4 + [dma((n, UNITS))] * 6 + [pltpu.VMEM((rows, width), F32)]
         + more + sems,
-        compiler_params=pltpu.CompilerParams(collective_id=collective_id, has_side_effects=True, vmem_limit_bytes=40 * 2**20),
+        compiler_params=pltpu.CompilerParams(collective_id=collective_id, has_side_effects=True, vmem_limit_bytes=ROOM),
         cost_estimate=pl.CostEstimate(flops=0, bytes_accessed=LINK_COST, transcendentals=0),
         name=name,
     )(*ins, *arrays)
 
 
+def rows_spec(rows, cols):
+    return pl.BlockSpec((rows, cols), lambda i: (i, 0))
+
+
+def fixed_spec(*shape):
+    return pl.BlockSpec(shape, lambda i: (0,) * len(shape), pipeline_mode=pl.Buffered(1))
+
+
+def by_rows(kernel, rows, ins, fixed, outs, lanes, flops, name):
+    specs = [rows_spec(rows, a.shape[1]) for a in ins] + [fixed_spec(*a.shape) for a in fixed]
+    out_specs = [rows_spec(rows, o.shape[1]) for o in outs]
+    shapes = list(outs)
+    if lanes:
+        out_specs.append(pl.BlockSpec((lanes * rows // CAP, 8, 128), lambda i: (i, 0, 0)))
+        shapes.append(jax.ShapeDtypeStruct((lanes, 8, 128), F32))
+    return pl.pallas_call(
+        kernel, grid=(CAP // rows,), out_shape=shapes, in_specs=specs, out_specs=out_specs,
+        compiler_params=pltpu.CompilerParams(dimension_semantics=("arbitrary",), vmem_limit_bytes=ROOM),
+        cost_estimate=pl.CostEstimate(flops=flops, bytes_accessed=20 * 2**20, transcendentals=0),
+        name=name,
+    )(*ins, *fixed)
+
+
+def lane_sums(values, share):
+    units, rows = share.shape[0], values.shape[0] // share.shape[0]
+    hi, lo = split(values)
+    ones = jnp.ones((8, values.shape[1]), BF)
+    for i in range(units):
+        r = slice(i * rows, (i + 1) * rows)
+        share[i, :, :rows] = dg(ones, hi[r], NT) + dg(ones, lo[r], NT)
+        if rows < 128:
+            share[i, :, rows:] = jnp.zeros((8, 128 - rows), F32)
+
+
+def normal(x, gain):
+    x = x.astype(F32)
+    scale = lax.rsqrt(jnp.mean(x * x, axis=1, keepdims=True) + EPSILON)
+    return scale, (x * scale * gain).astype(BF)
+
+
+def project_kernel(x, gain, w, pre, normed, scale):
+    sc, nb = normal(x[...], gain[...])
+    scale[...] = sc
+    normed[...] = nb
+    pre[...] = dg(nb, w[...], NN)
+
+
+def project(rows_full, gain, w_in):
+    sd = jax.ShapeDtypeStruct
+    outs = [sd((CAP, w_in.shape[1]), F32), sd((CAP, D), BF), sd((CAP, 1), F32)]
+    return by_rows(project_kernel, 256, [rows_full], [gain, w_in], outs, 0, 2 * CAP * D * w_in.shape[1], "project")
+
+
+def ffn_kernel(x, cot, gain, w_ug, w_u, w_d, normed, product, d_gate, d_up, d_normed, scale, share):
+    sc, nb = normal(x[...], gain[...])
+    scale[...] = sc
+    normed[...] = nb
+    gate = dg(nb, w_ug[...], NT)
+    up = dg(nb, w_u[...], NT)
+    sig = sigmoid(gate)
+    act = gate * sig
+    product[...] = (act * up).astype(BF)
+    d_product = dg(cot[...], w_d[...], NT)
+    dgt = (d_product * up * sig * (1.0 + gate * (1.0 - sig))).astype(BF)
+    dup = (d_product * act).astype(BF)
+    d_gate[...] = dgt
+    d_up[...] = dup
+    d_normed[...] = (dg(dgt, w_ug[...], NN) + dg(dup, w_u[...], NN)).astype(BF)
+    lane_sums((dgt.astype(F32) * gate + dup.astype(F32) * up) / sc, share)
+
+
+def ffn(held_full, cot_full, gain, w_ug, w_u, w_d):
+    sd = jax.ShapeDtypeStruct
+    ff = w_u.shape[0]
+    outs = [sd((CAP, D), BF)] + [sd((CAP, ff), BF)] * 3 + [sd((CAP, D), BF), sd((CAP, 1), F32)]
+    return by_rows(ffn_kernel, CAP // CHUNKS, [held_full, cot_full], [gain, w_ug, w_u, w_d], outs, UNITS,
+                   10 * CAP * D * ff, "feed_forward")
+
+
+def unproject_kernel(d_pre, pre, scale, w, d_normed, share):
+    d = d_pre[...]
+    d_normed[...] = dg(d, w[...], NT).astype(BF)
+    lane_sums(d.astype(F32) * pre[...] / scale[...], share)
+
+
+def unproject(d_pre, pre, scale, w_in):
+    outs = [jax.ShapeDtypeStruct((CAP, D), BF)]
+    return by_rows(unproject_kernel, 256, [d_pre, pre, scale], [w_in], outs, CAP // STEP, 2 * CAP * D * w_in.shape[1], "unproject")
+
+
 PRE = 1152
 GROUP = ("head", "tensor")
-
-
-def int_sum(values, along_axis):
-    return jnp.sum(values, axis=along_axis)
-
-
-def before(values):
-    at = jnp.arange(values.shape[0], dtype=jnp.int32)
-    return int_sum(jnp.where(at[None, :] < at[:, None], values[None, :], 0), 1)
-
-
-def layout(seq_lengths, starts, dealing, group_idx):
-    total_seqs = seq_lengths.shape[0]
-    chosen = lax.dynamic_slice_in_dim(dealing, group_idx * SEQ_DEV, SEQ_DEV)
-    picked = (chosen[:, None] == jnp.arange(total_seqs, dtype=jnp.int32)[None, :]).astype(jnp.int32)
-    own_length = int_sum(picked * seq_lengths[None, :], 1)
-    own_start = int_sum(picked * starts[None, :], 1)
-    padded = (own_length + BLOCK - 1) // BLOCK * BLOCK
-    buffer_start = before(padded)
-    row_ids = jnp.arange(CAP, dtype=jnp.int32)
-    member = int_sum((row_ids[:, None] >= buffer_start[None, :]).astype(jnp.int32), 1) - 1
-    owned_by = (member[:, None] == jnp.arange(SEQ_DEV, dtype=jnp.int32)[None, :]).astype(jnp.int32)
-    position = row_ids - int_sum(owned_by * buffer_start[None, :], 1)
-    row_length = int_sum(owned_by * own_length[None, :], 1)
-    seq_first = int_sum(owned_by * own_start[None, :], 1)
-    filled = position < row_length
-    return (seq_first + position, position, filled, seq_first, own_start, own_length)
-
-
-def congruent(lower_end, upper_end, residue, modulus):
-    return (upper_end - 1 - residue) // modulus - (lower_end - 1 - residue) // modulus
 
 
 def mm(left, right, dims=NN):
@@ -1163,11 +1319,6 @@
     return [total[i:j] for i, j in zip(ends, ends[1:])]
 
 
-def along_lanes(values, units):
-    rows = values.reshape(units, 1, -1)
-    return jnp.broadcast_to(jnp.pad(rows, ((0, 0), (0, 0), (0, 128 - rows.shape[2]))), (units, 8, 128))
-
-
 def sum_blocks(blocks):
     return jnp.sum(blocks.astype(F32), axis=0)
 
@@ -1175,84 +1326,46 @@
 def body(tokens, seq_lengths, dealing, gain_mixer, w_query, w_key, w_value, w_gate, w_beta, conv_weight,
          gain_heads, w_out, gain_ffn, w_up_gate, w_up, w_down, cotangent):
     shards = lax.axis_size("shard")
-    device = lax.axis_index("shard")
     width = tokens.shape[2]
     col_start = lax.axis_index(GROUP) * width
     per_peer = (CAP // shards + SEQ_DEV + 15) // 16 * 16
-    total_seqs = seq_lengths.shape[0]
 
     w_piece = jnp.concatenate(
         [w_query, w_key, w_value, w_gate, w_beta, jnp.zeros((w_beta.shape[0], PRE - 4 * width - w_beta.shape[1]), BF)], axis=1)
 
-    starts = before(seq_lengths)
-    finish = starts + seq_lengths
     own_rows = tokens.reshape(REAL_DEV, width)
-    own_ids = jnp.arange(REAL_DEV, dtype=jnp.int32)
-    packed_ids = own_ids * shards + device
-    inside = ((packed_ids[:, None] >= starts[None, :]) & (packed_ids[:, None] < finish[None, :])).astype(jnp.int32)
-    seq_ids = jnp.arange(total_seqs, dtype=jnp.int32)
-    matches = (dealing[:, None] == seq_ids[None, :]).astype(jnp.int32)
-    seq_home = int_sum(matches * (seq_ids // SEQ_DEV)[:, None], 0)
-    held = congruent(starts, finish, device, shards)
-    ahead = (seq_home[:, None] == seq_home[None, :]) & (seq_ids[None, :] < seq_ids[:, None])
-    seq_slot = (seq_home * per_peer + int_sum(jnp.where(ahead, held[None, :], 0), 1)
-                - 1 - (starts - 1 - device) // shards)
-    sent_slot = int_sum(inside * seq_slot[None, :], 1) + own_ids
-    natural, position, filled, seq_first, own_start, own_length = layout(seq_lengths, starts, dealing, device)
-    source = natural % shards
-    earlier = own_start[None, :] < seq_first[:, None]
-    span_counts = congruent(own_start[None, :], (own_start + own_length)[None, :], source[:, None], shards)
-    arrival = int_sum(jnp.where(earlier, span_counts, 0), 1) + congruent(seq_first, natural, source, shards)
-    recv_slot = jnp.where(filled, source * per_peer + arrival, -1)
-    filled_f = filled.astype(F32)[:, None]
-    persist = (position.reshape(-1, BLOCK)[:, 0] != 0).astype(F32)
-    pos = position[:, None]
     taps = conv_weight.reshape(3 * CONV, width)
     head_gain = gain_heads[None, :]
 
     n = lax.axis_size("head")
     side = side_by_side(w_up.shape[0])
-    x_rows, rows_full, w_in, w_o = z_gather(
-        n, own_rows, sent_slot[None, :], recv_slot[:, None], per_peer, 1, "gather_rows", shards, ("gather", side), (w_piece, w_out))
+    x_rows, rows_full, sent_slot, recv_slot, pos, filled_f, w_in, w_o = z_gather(
+        n, seq_lengths, dealing, own_rows, per_peer, 1, "gather_rows", shards, ("gather", side), (w_piece, w_out))
     w_o = level(w_o)
     rows_full, cot_piece = lax.optimization_barrier((rows_full, cotangent))
     cot_full = full_rows(cot_piece)
-    rows_full = rows_full.astype(F32)
-    scale_one = lax.rsqrt(jnp.mean(rows_full * rows_full, axis=1) + EPSILON)
-    normed = lax.optimization_barrier((rows_full * scale_one[:, None] * gain_mixer[None, :]).astype(BF))
-    pre = mm(normed, w_in)
-    mixed, *saved = mixer_fwd(persist, pre, pos, filled_f, taps, head_gain)
+    pre, normed, scale_one = project(rows_full, gain_mixer[None, :], w_in)
+    mixed, *saved = mixer_fwd(pre, pos, filled_f, taps, head_gain)
     branch_part, cot_full = lax.optimization_barrier((mm(mixed, w_o).astype(BF), cot_full))
     hidden, held_full, held_low, w_ug, w_u, w_d = z_turn(
         n, branch_part, x_rows, 2, "turn_branch", shards, (side,) * 3, (w_up_gate.T, w_up.T, w_down))
     w_ug, w_u, w_d = level(w_ug), level(w_u), level(w_d)
-    held_full = held_full.astype(F32)
-    scale_two = lax.rsqrt(jnp.mean(held_full * held_full, axis=1) + EPSILON)
-    normed_two = lax.optimization_barrier((held_full * scale_two[:, None] * gain_ffn[None, :]).astype(BF))
-    gate_act = mm(normed_two, w_ug, NT)
-    up_act = mm(normed_two, w_u, NT)
-    sig = jax.nn.sigmoid(gate_act)
-    product = (gate_act * sig * up_act).astype(BF)
-    d_product = mm(cot_full, w_d, NT)
-    d_gate = (d_product * up_act * sig * (1.0 + gate_act * (1.0 - sig))).astype(BF)
-    d_up = (d_product * gate_act * sig).astype(BF)
-    share_two = jnp.sum(d_gate.astype(F32) * gate_act + d_up.astype(F32) * up_act, axis=1) / scale_two
-    d_normed_two = (mm(d_gate, w_ug) + mm(d_up, w_u)).astype(BF)
+    normed_two, product, d_gate, d_up, d_normed_two, scale_two, share_two = ffn(
+        held_full, cot_full, gain_ffn[None, :], w_ug, w_u, w_d)
     down_kind, d_w_down = column_blocks(mm(product, cot_full, TN).astype(BF), shards)
     gate_kind, d_w_ug = column_blocks(mm(d_gate, normed_two, TN).astype(BF), shards)
     d_w_u = mm(d_up, normed_two, TN).astype(BF)
     ffn_gain_part = lax.dynamic_slice_in_dim(gain_ffn, col_start, width)[None, :]
     d_hidden, d_branch_full, _, ffn_gain_grad, d_w_ug, d_w_down = z_turn(
         n, d_normed_two, cotangent, 4, "turn_normed_two", shards, (gate_kind, down_kind), (d_w_ug, d_w_down),
-        norm=(held_low, scale_two[:, None], ffn_gain_part, along_lanes(share_two, UNITS)))
+        norm=(held_low, scale_two, ffn_gain_part, share_two))
     out_part = mm(product, w_d).astype(BF)
     out_part, d_branch_full = lax.optimization_barrier((out_part, d_branch_full))
     d_w_u, d_w_out = swap_ring(d_w_u, mm(mixed, d_branch_full, TN).astype(BF))
     out_sum = shares(out_part)
     d_mixed = mm(d_branch_full, w_o, NT)
-    d_pre, d_taps, d_head_gain = mixer_bwd(persist, d_mixed, pre, pos, filled_f, taps, head_gain, saved)
-    d_normed = mm(d_pre, w_in, NT).astype(BF)
-    share_one = jnp.sum(d_pre.astype(F32) * pre, axis=1) / scale_one
+    d_pre, d_taps, d_head_gain = mixer_bwd(d_mixed, pre, pos, filled_f, taps, head_gain, saved)
+    d_normed, share_one = unproject(d_pre, pre, scale_one, w_in)
     d_w_in = mm(normed, d_pre, TN).astype(BF).reshape(shards, w_piece.shape[0], PRE)
     d_normed, out_sum = lax.optimization_barrier((d_normed, out_sum))
     block_out = (hidden + out_sum).astype(BF)
@@ -1262,8 +1375,8 @@
         jnp.pad(jnp.sum(d_head_gain, axis=0), (0, width - HD))[None, :],
         jnp.zeros((1, width), F32)], axis=0)
     d_tokens, summed, d_w_in = z_finish(
-        n, d_normed, x_rows, scale_one[:, None], d_hidden, mixer_gain_part, along_lanes(share_one, CAP // STEP), small,
-        sent_slot[:, None], recv_slot[None, :], per_peer, 6, "finish_rows", shards, ("swap",), (d_w_in,))
+        n, d_normed, x_rows, scale_one, d_hidden, mixer_gain_part, share_one, small,
+        sent_slot, recv_slot, per_peer, 6, "finish_rows", shards, ("swap",), (d_w_in,))
     d_tokens = d_tokens.reshape(REAL_DEV, 1, width)
     d_w_in = sum_blocks(d_w_in)
     by_row = summed.transpose(1, 0, 2).reshape(16, D)

time: 609 us -> 577 us (0.947)
  Pallas kernels: 398 us -> 459 us
  matrix products: 108 us -> 53 us
  other arithmetic: 44.9 us -> 16 us
  local copies, waits for them, and re-layouts: 34.7 us -> 22.6 us
    dot_general x15 -> x8, matrix products: 108 us -> 53 us  [mm(): return lax.dot_general(left, right, dims, preferred_element_type=F32)]
    pallas_call x2 -> x5, Pallas kernels: 84.5 us -> 137 us  [the longest x3 58.5 us: by_rows(): pl.pallas_call(kernel, grid=(CAP // rows,), out_shape=shapes, in_specs=sp...]
    reduce_sum x12 -> x0, other arithmetic: 15.8 us -> none  [the longest x1 5.35 us: body(): scale_two = lax.rsqrt(jnp.mean(held_full * held_full, axis=1) + EPSILON)]
    unnamed x115 -> x37, local copies, waits for them, and re-layouts: 23.4 us -> 8.74 us
    convert_element_type x4 -> x0, other arithmetic: 6.97 us -> none  [the longest x1 3.54 us: body(): (rows_full * scale_one[:, None] * gain_mixer[None, :]).astype(BF)]
  transfers between devices with their start and end apart: 5 -> 5, of which waited for: 0 -> 1; matrix products, arithmetic and copies ran while one was open for 13% -> 8% of each run, Pallas kernels for 14% -> 18%
where the time goes in v3:
time: 577 us; the launch traced here: 571 us
  Pallas kernels  459 us (80%)
  matrix products  53 us (9%)
  local copies, waits for them, and re-layouts  22.6 us (4%)
  other arithmetic  16 us (3%)
  between operations  14.9 us (3%)
    pallas_call x2, Pallas kernels, z_turn(): pl.pallas_call(functools.partial(turn_kernel, n, width, m, kinds, norm is...  171 us
    pallas_call x1, Pallas kernels, z_gather(): pl.pallas_call(functools.partial(gather_kernel, n, width, m, kinds), out_...  78.7 us
    pallas_call x1, Pallas kernels, z_finish(): pl.pallas_call(functools.partial(finish_kernel, n, width, m, kinds), out_...  72.4 us
    pallas_call x3, Pallas kernels, by_rows(): pl.pallas_call(kernel, grid=(CAP // rows,), out_shape=shapes, in_specs=sp...  58.5 us
    dot_general x8, matrix products, mm(): return lax.dot_general(left, right, dims, preferred_element_type=F32)  53 us
    pallas_call x1, Pallas kernels, mixer_bwd(): pl.pallas_call(bwd_kernel, out_shape=outs, in_specs=[VM] * 6 + [pl.BlockS...  42.6 us
    pallas_call x1, Pallas kernels, mixer_fwd(): pl.pallas_call(fwd_kernel, out_shape=outs, in_specs=[VM] * 5, out_specs=[...  35.5 us
  transfers between devices with their start and end apart: 5, of which 1 were waited for; matrix products, arithmetic and copies ran while one was open for 8% of the time, Pallas kernels for 18%

profile of v3, /device:TPU:0, one launch (start us, length us, event | category | flops | bytes accessed | tf_op | source)
XLA Modules:
  0.0 571.1 jit_solution(1988324963059876710)
XLA Ops:
  8.1 3.1 concatenate.18.refs_3_
  11.3 78.7 %gather_rows.1 = (bf16[1280,256]{1,0:T(8,128)(2,1)}, bf16[1280,2048]{1,0:T(8,128)(2,1)}, s32[1152,1]{1,0:T(8,128)}, s32[1,1280]{1,0:T(1,128)}, s32[1280,1]{1,0:T...) custom-call(s32[16]{0:T(128)} %refs_0_.1, s32[16]{0:T(128)} %refs_1_.1, ...), custom_call_target="tpu_custom_call" | custom-call | bytes 157286400 | tf_op jit(solution)/shard_map/gather_rows/pallas_call | solution.py:613
  90.9 1.3 dynamic_slice.30
  92.2 13.2 %project.1 = (f32[1280,1152]{1,0:T(8,128)}, bf16[1280,2048]{1,0:T(8,128)(2,1)}, f32[1280,1]{1,0:T(8,128)}) custom-call(bf16[1280,2048]{1,0:T(8,128)(2,1)} %get-tuple-element.72.x, f32[1,2048]{1,0:T(1,128)} %bitcast.52, bf16[2048,1152]{1,0:T(8,128)(2,1)} %get-tuple-element.73.w), custom_call_target="tpu_custom_call" | custom-call | flops 6039797760 | bytes 20971520 | tf_op jit(solution)/shard_map/project/pallas_call | solution.py:1197
  105.5 35.5 %mixer_forward.1 = (bf16[1280,256]{1,0:T(8,128)(2,1)}, f32[1280,768]{1,0:T(8,128)}, f32[1280,512]{1,0:T(8,128)}, f32[1280,256]{1,0:T(8,128)}, f32[1280,256]{1,0:...) custom-call(f32[1280,1152]{1,0:T(8,128)} %get-tuple-element.74.pre, ...), custom_call_target="tpu_custom_call" | custom-call | bytes 146800640 | tf_op jit(solution)/shard_map/mixer_forward/pallas_call | solution.py:164
  141.0 4.9 convolution_convert_fusion.2.refs_0_
  146.0 1.3 all-gather.2.cloned.1.call-done.cot
  147.2 83.9 %turn_branch.1 = (f32[1280,256]{1,0:T(8,128)}, bf16[1280,2048]{1,0:T(8,128)(2,1)}, bf16[1280,256]{1,0:T(8,128)(2,1)}, bf16[704,2048]{1,0:T(8,128)(2,1)}, bf16[70...) custom-call(bf16[1280,2048]{1,0:T(8,128)(2,1)} %convolution_convert_fusion.2.refs_0_, ...), custom_call_target="tpu_custom_call" | custom-call | bytes 157286400 | tf_op jit(solution)/shard_map/turn_branch/pallas_call | solution.py:1169
  231.1 31.9 %feed_forward.1 = (bf16[1280,2048]{1,0:T(8,128)(2,1)}, bf16[1280,704]{1,0:T(8,128)(2,1)}, bf16[1280,704]{1,0:T(8,128)(2,1)}, bf16[1280,704]{1,0:T(8,128)(2,1)}, ...) custom-call(bf16[1280,2048]{1,0:T(8,128)(2,1)} %get-tuple-element.83.x, ...), custom_call_target="tpu_custom_call" | custom-call | flops 18454937600 | bytes 20971520 | tf_op jit(solution)/shard_map/feed_forward/pallas_call | solution.py:1197
  263.1 8.7 %convolution_convert_fusion.4.refs_7_ = bf16[704,2048]{1,0:T(8,128)(2,1)} fusion(bf16[1280,704]{1,0:T(8,128)(2,1)} %get-tuple-element.88, bf16[1280,2048]{1,0:T(8,128)(2,1)} %all-gather.2.cloned.1.call-done.cot), kind=kOutput, calls=%fused_computation.7 | convolution fusion | flops 3692429312 | bytes 9928704 | tf_op jit(solution)/shard_map/dot_general | solution.py:1277
  271.8 6.0 %convolution_convert_fusion.1 = bf16[1280,2048]{1,0:T(8,128)(2,1)} fusion(bf16[1280,704]{1,0:T(8,128)(2,1)S(1)} %copy-done.13, bf16[704,2048]{1,0:T(8,128)(2,1)S(1)} %copy-done.11), kind=kOutput, calls=%fused_computation.2 | convolution fusion | flops 3693608960 | bytes 9928704 | tf_op jit(solution)/shard_map/dot_general | solution.py:1277
  277.8 8.6 %convolution_convert_fusion.5.refs_6_ = bf16[704,2048]{1,0:T(8,128)(2,1)} fusion(bf16[1280,704]{1,0:T(8,128)(2,1)} %get-tuple-element.93, bf16[1280,2048]{1,0:T(8,128)(2,1)} %get-tuple-element.94), kind=kOutput, calls=%fused_computation.8 | convolution fusion | flops 3692429312 | bytes 9928704 | tf_op jit(solution)/shard_map/dot_general | solution.py:1277
  286.4 87.3 %turn_normed_two.1 = (f32[1280,256]{1,0:T(8,128)}, bf16[1280,2048]{1,0:T(8,128)(2,1)}, bf16[1280,256]{1,0:T(8,128)(2,1)}, f32[8,256]{1,0:T(8,128)}, bf16[4,704,5...) custom-call(bf16[1280,2048]{1,0:T(8,128)(2,1)} %get-tuple-element.89.refs_0_, ...), custom_call_target="tpu_custom_call" | custom-call | bytes 157286400 | tf_op jit(solution)/shard_map/turn_normed_two/pallas_call | solution.py:1169
  373.7 1.4 dynamic_slice.31
  375.1 4.2 convolution_convert_fusion.6
  379.5 6.6 %convolution_convert_fusion.3 = bf16[704,2048]{1,0:T(8,128)(2,1)S(1)} fusion(bf16[1280,704]{1,0:T(8,128)(2,1)S(1)} %copy-done.12, bf16[1280,2048]{1,0:T(8,128)(2,1)} %get-tuple-element.94), kind=kOutput, calls=%fused_computation.6 | convolution fusion | flops 3692429312 | bytes 9928704 | tf_op jit(solution)/shard_map/dot_general | solution.py:1277
  386.0 1.2 constant_dynamic-slice_fusion.7
  388.3 1.1 collective-permute-start
  392.3 2.1 collective-permute-start.2
  394.4 2.6 fusion.2.dmix
  397.0 42.6 %mixer_backward.1 = (bf16[1280,1152]{1,0:T(8,128)(2,1)}, f32[12,8,256]{2,1,0:T(8,128)}, f32[8,128]{1,0:T(8,128)}) custom-call(f32[1280,256]{1,0:T(8,128)} %fusion.2.dmix, f32[1280,1152]{1,0:T(8,128)} %get-tuple-element.74.pre, s32[1280,1]{1,0:T(8,128)} %get-tuple-element.75.pos_ref, f32[1280,1]{1,0:T(8,128)} %get-tuple-element.76.fill_ref, ...), custom_call_target="tpu_custom_call" | custom-call | bytes 209715200 | tf_op jit(solution)/shard_map/mixer_backward/pallas_call | solution.py:302
  439.7 11.5 %convolution_convert_fusion = bf16[2048,1152]{1,0:T(8,128)(2,1)} fusion(bf16[1280,2048]{1,0:T(8,128)(2,1)} %get-tuple-element.120, bf16[1280,1152]{1,0:T(8,128)(2,1)} %get-tuple-element.107.d_pre), kind=kOutput, calls=%fused_computation.1 | convolution fusion | flops 6042157056 | bytes 12910592 | tf_op jit(solution)/shard_map/dot_general | solution.py:1277
  451.3 1.9 concatenate.19.refs_6_
  453.2 4.6 convert_reduce_fusion.1
  457.8 13.3 %unproject.1 = (bf16[1280,2048]{1,0:T(8,128)(2,1)}, f32[10,8,128]{2,1,0:T(8,128)}) custom-call(bf16[1280,1152]{1,0:T(8,128)(2,1)} %get-tuple-element.107.d_pre, f32[1280,1152]{1,0:T(8,128)} %get-tuple-element.74.pre, f32[1280,1]{1,0:T(8,128)} %get-tuple-element.108.scale.refs_2_, bf16[2048,1152]{1,0:T(8,128)(2,1)} %get-tuple-element.73.w), custom_call_target="tpu_custom_call" | custom-call | flops 6039797760 | bytes 20971520 | tf_op jit(solution)/shard_map/unproject/pallas_call | solution.py:1197
  471.2 2.3 convert_add_fusion
  474.3 1.2 slice_bitcast_fusion
  475.5 1.2 convert_element_type.54
  476.7 72.4 %finish_rows.1 = (f32[1152,256]{1,0:T(8,128)}, f32[8,16,256]{2,1,0:T(8,128)}, bf16[4,512,1152]{2,1,0:T(8,128)(2,1)}) custom-call(bf16[1280,2048]{1,0:T(8,128)(2,1)} %get-tuple-element.112.refs_0_, bf16[1280,256]{1,0:T(8,128)(2,1)} %get-tuple-element.81.refs_1_, f32[1280,1]{1,0:T(8,128)} %get-tuple-element.108.scale.refs_2_, ...), custom_call_target="tpu_custom_call" | custom-call | bytes 157286400 | tf_op jit(solution)/shard_map/finish_rows/pallas_call | solution.py:876
  549.1 3.3 convert_reduce_fusion
  552.5 1.4 fusion
  554.3 5.9 %copy.51 = f32[1152,1,256]{2,1,0:T(1,128)} copy(f32[1152,1,256]{2,0,1:T(8,128)S(1)} %bitcast.37) | data formatting | bytes 2359296
  (64 shorter events, 11.0 us)
Async XLA Ops:
  7.2 83.1 %copy-start.8 = (f32[4,3,256]{2,0,1:T(4,128)S(1)}, f32[4,3,256]{2,0,1:T(4,128)}, u32[]{:S(2)}) copy-start(f32[4,3,256]{2,0,1:T(4,128)} %param.26) | copy-start | bytes 36868
  7.2 140.0 %all-gather.2.cloned.1.call-start = ((), (), s32[]{:S(2)}) async-start(), calls=%async_computation.1 | async-start | bytes 5898240 | tf_op jit(solution)/shard_map/all_gather | solution.py:1281
  90.0 385.5 %reduce-scatter.2.cloned.1.call-start = ((), (), s32[]{:S(2)}) async-start(), calls=%async_computation.2 | async-start | bytes 5898240 | tf_op jit(solution)/shard_map/reduce_scatter | solution.py:1285
  105.5 35.6 %copy-start.5 = (bf16[256,2048]{1,0:T(8,128)(2,1)S(1)}, bf16[256,2048]{1,0:T(8,128)(2,1)}, u32[]{:S(2)}) copy-start(bf16[256,2048]{1,0:T(8,128)(2,1)} %get-tuple-element.78) | copy-start | bytes 3145732
  263.1 8.7 %copy-start.11 = (bf16[704,2048]{1,0:T(8,128)(2,1)S(1)}, bf16[704,2048]{1,0:T(8,128)(2,1)}, u32[]{:S(2)}) copy-start(bf16[704,2048]{1,0:T(8,128)(2,1)} %get-tuple-element.87.w_d) | copy-start | bytes 8650756
  263.1 8.7 %copy-start.13 = (bf16[1280,704]{1,0:T(8,128)(2,1)S(1)}, bf16[1280,704]{1,0:T(8,128)(2,1)}, u32[]{:S(2)}) copy-start(bf16[1280,704]{1,0:T(8,128)(2,1)} %get-tuple-element.88) | copy-start | bytes 5406724
  373.7 1.4 copy-start.3
  375.1 4.3 copy-start.12
  379.3 15.1 %slice-start = ((s8[5242880]{0:T(1024)(128)(4,1)}), s8[4194304]{0:T(1024)(128)(4,1)S(1)}, s32[]{:S(2)}) async-start(s8[5242880]{0:T(1024)(128)(4,1)} %bitcast.53), calls=%async_computation.3 | async-start | bytes 8388608
  379.4 15.0 %slice-start.1 = ((s8[5242880]{0:T(1024)(128)(4,1)}), s8[1048576]{0:T(1024)(128)(4,1)S(1)}, s32[]{:S(2)}) async-start(s8[5242880]{0:T(1024)(128)(4,1)} %bitcast.53), calls=%async_computation.4 | async-start | bytes 2097152
  388.3 82.8 %collective-permute-start = (bf16[960,512]{1,0:T(8,128)(2,1)}, bf16[960,512]{1,0:T(8,128)(2,1)}, u32[]{:S(2)}, u32[]{:S(2)}) collective-permute-start(bf16[960,512]{1,0:T(8,128)(2,1)} %pad_maximum_fusion), channel_id=1, source_target_pairs={{0,8},{8,16},{16,24},{24,0},{1,9},{9,17},{17,25},{25,1},{2,10},{10... | collective-permute-start | bytes 2949128 | tf_op jit(solution)/shard_map/ppermute | solution.py:1315
  390.4 80.8 %collective-permute-start.1 = (bf16[960,512]{1,0:T(8,128)(2,1)}, bf16[960,512]{1,0:T(8,128)(2,1)}, u32[]{:S(2)}, u32[]{:S(2)}) collective-permute-start(bf16[960,512]{1,0:T(8,128)(2,1)} %pad_maximum_fusion.1), channel_id=1, source_target_pairs={{0,16},{8,24},{16,0},{24,8},{1,17},{9,25},{17,1},{25,9},{2,18},{10... | collective-permute-start | bytes 2949128 | tf_op jit(solution)/shard_map/ppermute | solution.py:1315
  392.3 78.8 %collective-permute-start.2 = (bf16[960,512]{1,0:T(8,128)(2,1)}, bf16[960,512]{1,0:T(8,128)(2,1)}, u32[]{:S(2)}, u32[]{:S(2)}) collective-permute-start(bf16[960,512]{1,0:T(8,128)(2,1)} %pad_maximum_fusion.2), channel_id=1, source_target_pairs={{0,24},{8,0},{16,8},{24,16},{1,25},{9,1},{17,9},{25,17},{2,26},{10... | collective-permute-start | bytes 2949128 | tf_op jit(solution)/shard_map/ppermute | solution.py:1315
  439.7 11.5 %copy-start.9 = (f32[8,256]{1,0:T(8,128)S(1)}, f32[8,256]{1,0:T(8,128)}, u32[]{:S(2)}) copy-start(f32[8,256]{1,0:T(8,128)} %get-tuple-element.116) | copy-start | bytes 24580
  439.7 11.5 %copy-start.7 = (f32[12,8,256]{2,1,0:T(8,128)S(1)}, f32[12,8,256]{2,1,0:T(8,128)}, u32[]{:S(2)}) copy-start(f32[12,8,256]{2,1,0:T(8,128)} %get-tuple-element.115) | copy-start | bytes 294916
  439.7 11.5 %copy-start.10 = (f32[8,128]{1,0:T(8,128)S(1)}, f32[8,128]{1,0:T(8,128)}, u32[]{:S(2)}) copy-start(f32[8,128]{1,0:T(8,128)} %get-tuple-element.117) | copy-start | bytes 12292
  439.7 13.5 %copy-start = (bf16[4,704,512]{2,1,0:T(8,128)(2,1)S(1)}, bf16[4,704,512]{2,1,0:T(8,128)(2,1)}, u32[]{:S(2)}) copy-start(bf16[4,704,512]{2,1,0:T(8,128)(2,1)} %get-tuple-element.125) | copy-start | bytes 8650756
  457.8 13.4 %copy-start.1 = (bf16[704,512]{1,0:T(8,128)(2,1)S(1)}, bf16[704,512]{1,0:T(8,128)(2,1)}, u32[]{:S(2)}) copy-start(bf16[704,512]{1,0:T(8,128)(2,1)} %get-tuple-element.172) | copy-start | bytes 2162692
  552.4 1.9 copy-start.4
  552.4 7.8 %copy-start.6 = (f32[8,16,256]{2,1,0:T(8,128)S(1)}, f32[8,16,256]{2,1,0:T(8,128)}, u32[]{:S(2)}) copy-start(f32[8,16,256]{2,1,0:T(8,128)} %get-tuple-element.122) | copy-start | bytes 393220
  552.5 10.4 %copy-start.2 = (f32[1280,256]{1,0:T(8,128)S(1)}, f32[1280,256]{1,0:T(8,128)}, u32[]{:S(2)}) copy-start(f32[1280,256]{1,0:T(8,128)} %get-tuple-element.82) | copy-start | bytes 3932164
Sparse Core Ops, SparseCore 0:
  90.1 57.0 all-gather.1
  373.8 58.4 reduce-scatter.1

commit v4 on v3

--- a/solution.py
+++ b/solution.py
@@ -33,8 +33,8 @@
     ah, al = split(a); bh, bl = split(b)
     return dg(ah, bh, dims) + (dg(ah, bl, dims) + dg(al, bh, dims))
 
-def twice(step):
-    return lambda i, c: step(2 * i + 1, step(2 * i, c))
+def four_times(step):
+    return lambda i, c: step(4 * i + 3, step(4 * i + 2, step(4 * i + 1, step(4 * i, c))))
 
 def goes_on(pos_ref, n):
     first = pos_ref[pl.ds(pl.multiple_of(n * BLOCK, BLOCK), 8), :][:1]
@@ -105,9 +105,9 @@
             w_out[r, hs] = b*k
         return tuple(new_tails)
     z8 = jnp.zeros((8, 256), F32)
-    lax.fori_loop(0, NB // 2, twice(phase_a), (z8, z8, z8))
+    lax.fori_loop(0, NB // 4, four_times(phase_a), (z8, z8, z8))
     keep(0, 1, 6)
-    GRP = 8
+    GRP = 20
     def phase_t(i, _):
         ts = inverses([t_out[i*GRP+j] for j in range(GRP)], ri, ci)
         for j in range(GRP):
@@ -116,14 +116,14 @@
     lax.fori_loop(0, 2*NB//GRP, phase_t, 0)
     keep(7)
     def phase_w(i, _):
-        todo = [(n, pl.ds(pl.multiple_of(n * BLOCK, BLOCK), BLOCK), h, slice(h*HD, (h+1)*HD)) for n in (2*i, 2*i+1) for h in range(heads)]
+        todo = [(n, pl.ds(pl.multiple_of(n * BLOCK, BLOCK), BLOCK), h, slice(h*HD, (h+1)*HD)) for n in (4*i, 4*i+1, 4*i+2, 4*i+3) for h in range(heads)]
         wu = [d3(t_out[n*2+h], jnp.concatenate([w_out[r, c], u_out[r, c]], axis=1)) for n, r, h, c in todo]
         mb = [d3(qk[r, 256+h*HD:256+(h+1)*HD], x, TN) for x, (n, r, h, c) in zip(wu, todo)]
         for x, y, (n, r, h, c) in zip(wu, mb, todo):
             w_out[r, c] = x[:, :HD]; u_out[r, c] = x[:, HD:]
             m_out[n*2+h] = y[:, :HD]; b_s[n*2+h] = y[:, HD:]
         return 0
-    lax.fori_loop(0, NB//2, phase_w, 0)
+    lax.fori_loop(0, NB//4, phase_w, 0)
     keep(2, 3, 8)
     def phase_b(n, ss):
         out = []
@@ -137,7 +137,7 @@
     lax.fori_loop(0, NB, phase_b, (zs, zs))
     keep(9)
     def phase_c(i, _):
-        todo = [(n, pl.ds(pl.multiple_of(n * BLOCK, BLOCK), BLOCK), h, slice(h*HD, (h+1)*HD)) for n in (2*i, 2*i+1) for h in range(heads)]
+        todo = [(n, pl.ds(pl.multiple_of(n * BLOCK, BLOCK), BLOCK), h, slice(h*HD, (h+1)*HD)) for n in (4*i, 4*i+1, 4*i+2, 4*i+3) for h in range(heads)]
         rr = [d3(jnp.concatenate([w_out[r, c], qk[r, c]], axis=0), s_out[n*2+h]) for n, r, h, c in todo]
         u2 = [u_out[r, c] - v[:BLOCK] for v, (n, r, h, c) in zip(rr, todo)]
         os_ = [v[BLOCK:] + d3(p_out[n*2+h], u) for v, u, (n, r, h, c) in zip(rr, u2, todo)]
@@ -149,7 +149,7 @@
             gg = pre[r, 768+h*HD:768+(h+1)*HD]
             mixed[r, c] = (o * sc * gain[...] * (gg * sigmoid(gg))).astype(BF)
         return 0
-    lax.fori_loop(0, NB // 2, phase_c, 0)
+    lax.fori_loop(0, NB // 4, phase_c, 0)
     keep(4, 5)
     for i in range(10):
         pltpu.make_async_copy(held[i], given[i], sem.at[i]).wait()
@@ -206,7 +206,7 @@
             dd = jnp.concatenate([do, -pdo], axis=0)
             e_s[e] = d3(qw, dd, TN)
         return 0
-    lax.fori_loop(0, NB // 2, twice(phase_a), 0)
+    lax.fori_loop(0, NB // 4, four_times(phase_a), 0)
     fetch(8).wait()
 
     def phase_b(i, ds):
@@ -225,7 +225,7 @@
         fetch(i).wait()
 
     def phase_c(i, heads_dc):
-        blocks = (NB - 1 - 2 * i, NB - 2 - 2 * i)
+        blocks = tuple(NB - 1 - j - 4 * i for j in range(4))
         todo = [(n, pl.ds(pl.multiple_of(n * BLOCK, BLOCK), BLOCK), h, slice(h*HD, (h+1)*HD)) for n in blocks for h in range(heads)]
         def every(f, *lists):
             return [f(*v) for v in zip(*lists)]
@@ -295,7 +295,7 @@
             heads_dc = tuple(new)
         return heads_dc
     z8 = jnp.zeros((8, 256), F32)
-    lax.fori_loop(0, NB // 2, phase_c, (z8, z8, z8))
+    lax.fori_loop(0, NB // 4, phase_c, (z8, z8, z8))
 
 def mixer_bwd(dmix, pre, pos, fil, cw, gain, saved):
     outs = (sds(CAP,1152,dt=BF), sds(12,8,256), sds(8,HD))
@@ -319,6 +319,13 @@
 def shard_peers(m):
     s, h, t = lax.axis_index("shard"), lax.axis_index("head"), lax.axis_index("tensor")
     return [((lax.rem(s + i, m), h, t), lax.rem(s + i, m)) for i in range(1, m)]
+
+
+def greet_shard(m):
+    barrier = pltpu.get_barrier_semaphore()
+    for p, _ in shard_peers(m):
+        pl.semaphore_signal(barrier, inc=1, device_id=p, device_id_type=MESH)
+    return m - 1
 
 
 class Carry:
@@ -377,11 +384,7 @@
         return [self.side, self.over] if self.relayed(e) else [p[1] for p in shard_peers(self.m)]
 
     def greet(self):
-        barrier = pltpu.get_barrier_semaphore()
-        if self.kinds:
-            for p, _ in shard_peers(self.m):
-                pl.semaphore_signal(barrier, inc=1, device_id=p, device_id_type=MESH)
-        return self.m - 1 if self.kinds else 0
+        return greet_shard(self.m) if self.kinds else 0
 
     def start(self):
         for e in range(len(self.kinds)):
@@ -642,8 +645,15 @@
     pl.semaphore_wait(barrier, 2 * n - 1 + more)
 
 
-def finish_kernel(n, width, m, kinds, *refs):
-    (part, kept, scale, base, gain, share, small, sent, place), (tokens, every), scratch, carry = carry_of(kinds, m, refs, 9, 2)
+def finish_kernel(n, width, m, kinds, fill, piles, *refs):
+    (part, kept, scale, base, gain, share, small, sent, place, *left), (tokens, every, *grads), scratch, carry = carry_of(
+        kinds, m, refs, 9 + piles + 2 * fill, 2 + piles + fill)
+    stacks, left = left[:piles], left[piles:]
+    added, grads = grads[:piles], grads[piles:]
+    *scratch, pile_sem = scratch
+    heaps, scratch = scratch[:piles], scratch[piles:]
+    if fill:
+        *scratch, l_buf, r_buf, blocks, l_sem, r_sem, w_s, w_r, w_own = scratch
     (low, dgain, outbox, inbox, deal_s, deal_r, held, ours, shard_s, shard_r, group_s, group_r,
      acc, tots, tot_s, tot_r, mine, theirs, from_below, from_above,
      here, core_s, core_r, up_s, up_r, down_s, down_r) = scratch
@@ -680,7 +690,27 @@
     order = [j for i in range(n // 2) for j in (n - 1 - i, i)]
     for j in order:
         own(j).start()
-    greet_group(n, carry.greet())
+
+    def load(i):
+        return pltpu.make_async_copy(stacks[i], heaps[i], pile_sem.at[i])
+
+    def add_up(i):
+        load(i).wait()
+        tall = heaps[i].shape[1] // 4
+
+        def step(q, c):
+            r = pl.ds(pl.multiple_of(q * tall, tall), tall)
+            v = heaps[i][0, r, :].astype(F32)
+            for b in range(1, m):
+                v = v + heaps[i][b, r, :].astype(F32)
+            added[i][r, :] = v
+            return c
+
+        lax.fori_loop(0, 4, step, 0)
+
+    for i in range(piles):
+        load(i).start()
+    greet_group(n, greet_shard(m))
     me = h * 2 + t
     peers = group_peers(n)
 
@@ -693,6 +723,40 @@
     for j in order:
         swap(j).start()
     carry.start()
+    shard = lax.axis_index("shard")
+    others = shard_peers(m)
+    if fill:
+        lhs, rhs = left
+        wide = lhs.shape[1] // m
+
+        def columns(q):
+            return lhs.at[:, pl.ds(pl.multiple_of(q * wide, wide), wide)]
+
+        def fetch(i, q):
+            return pltpu.make_async_copy(columns(q), l_buf.at[i], l_sem.at[i])
+
+        def grad(i, p, src):
+            return pltpu.make_async_remote_copy(src_ref=blocks.at[i], dst_ref=grads[0].at[src], send_sem=w_s.at[i],
+                                                recv_sem=w_r.at[src], device_id=p[0], device_id_type=MESH)
+
+        own_grad = pltpu.make_async_copy(blocks.at[m - 1], grads[0].at[shard], w_own)
+        whole = pltpu.make_async_copy(rhs, r_buf, r_sem)
+        whole.start()
+        for i, p in enumerate(others):
+            fetch(i, p[1]).start()
+        fetch(m - 1, shard).start()
+
+        def multiply(i):
+            if i == 0:
+                whole.wait()
+            fetch(i, shard).wait()
+            blocks[i] = dg(l_buf[i], r_buf[...], TN).astype(BF)
+            if i < m - 1:
+                grad(i, others[i], shard).start()
+            else:
+                own_grad.start()
+
+        multiply(0)
 
     def arrive(j):
         own(j).wait()
@@ -734,6 +798,15 @@
 
             fall(kd).start()
 
+        if fill and tick + 1 < m:
+            multiply(tick + 1)
+
+        if tick >= 2 * n - 2 - piles:
+            add_up(tick - (2 * n - 2 - piles))
+
+    if fill:
+        for i in range(2 * n - 1, m):
+            multiply(i)
     arrive(h)
     for i, p in enumerate(peers):
         tot_copy(i, p[0], p[1]).wait_recv()
@@ -803,8 +876,6 @@
     for i, p in enumerate(peers):
         tot_copy(i, p[0], me).wait_send()
 
-    others = shard_peers(m)
-    shard = lax.axis_index("shard")
     per_peer = outbox.shape[1]
     ids = lax.broadcasted_iota(jnp.int32, (per_peer, place.shape[1]), 0)
 
@@ -846,7 +917,7 @@
     def settle(i, c):
         r = pl.ds(pl.multiple_of(i * STEP, STEP), STEP)
         chosen = jnp.where(sent[r, :] == lanes, 1.0, 0.0).astype(BF)
-        tokens[r, :] = dg(chosen, inbox[...].reshape(m * per_peer, width), NN)
+        tokens[r, :, :] = dg(chosen, inbox[...].reshape(m * per_peer, width), NN).reshape(STEP, 1, width)
         return c
 
     lax.fori_loop(0, REAL_DEV // STEP, settle, 0)
@@ -867,26 +938,43 @@
         def _():
             fall(k).wait_send()
     carry.wait()
-
-
-def z_finish(n, part, kept, scale, base, gain, share, small, sent, place, per_peer, collective_id, name, m, kinds, arrays):
+    if fill:
+        own_grad.wait()
+        for i, p in enumerate(others):
+            grad(i, p, p[1]).wait_recv()
+            grad(i, p, shard).wait_send()
+
+
+def z_finish(n, part, kept, scale, base, gain, share, small, sent, place, per_peer, collective_id, name, m, lhs, rhs, stacks):
     rows, width = part.shape[0], part.shape[1] // (2 * n)
     dma = pltpu.SemaphoreType.DMA
+    wide = lhs.shape[1] // m
+    fill = wide % 128 == 0
+    if fill:
+        kinds, arrays, extra = (), (), [lhs, rhs]
+        made = [jax.ShapeDtypeStruct((m, wide, rhs.shape[1]), BF)]
+        room = [pltpu.VMEM((m, rows, wide), BF), pltpu.VMEM(rhs.shape, BF), pltpu.VMEM(made[0].shape, BF),
+                dma((m,)), dma, dma((m,)), dma((m,)), dma]
+    else:
+        kinds, arrays = ("swap",), (dg(lhs, rhs, TN).astype(BF).reshape(m, wide, rhs.shape[1]),)
+        extra, made, room = [], [], []
     shapes, sems = carried(kinds, m, arrays)
     return pl.pallas_call(
-        functools.partial(finish_kernel, n, width, m, kinds),
-        out_shape=[jax.ShapeDtypeStruct((REAL_DEV, width), F32), jax.ShapeDtypeStruct((2 * n,) + small.shape, F32)] + shapes,
-        in_specs=[HBM] + [VM] * 8 + [HBM] * len(shapes), out_specs=[VM] * 2 + [HBM] * len(shapes),
-        scratch_shapes=[pltpu.VMEM((rows, width), BF), pltpu.VMEM((8, width), F32)]
+        functools.partial(finish_kernel, n, width, m, kinds, int(fill), len(stacks)),
+        out_shape=[jax.ShapeDtypeStruct((REAL_DEV, 1, width), F32), jax.ShapeDtypeStruct((2 * n,) + small.shape, F32)]
+        + [jax.ShapeDtypeStruct(a.shape[1:], F32) for a in stacks] + made + shapes,
+        in_specs=[HBM] + [VM] * 8 + [HBM] * (len(stacks) + len(extra) + len(shapes)),
+        out_specs=[VM] * (2 + len(stacks)) + [HBM] * (len(made) + len(shapes)),
+        scratch_shapes=[pltpu.VMEM(a.shape, BF) for a in stacks] + [pltpu.VMEM((rows, width), BF), pltpu.VMEM((8, width), F32)]
         + [pltpu.VMEM((m, per_peer, width), BF)] * 2 + [dma((m,))] * 2
         + [pltpu.VMEM((m,) + small.shape, F32), pltpu.VMEM(small.shape, F32), dma((m,)), dma((m,)), dma((2 * n,)), dma((2 * n,))]
         + [pltpu.VMEM((rows, width), F32), pltpu.VMEM((2 * n, rows // STEP, 8, STEP), F32), dma((2 * n,)), dma((2 * n,))]
         + [pltpu.VMEM((n, rows, width), BF)] * 2 + [pltpu.VMEM((n - 1, rows, width), BF)] * 2
-        + [dma((n,))] * 3 + [dma((n - 1,))] * 4 + sems,
+        + [dma((n,))] * 3 + [dma((n - 1,))] * 4 + room + [dma((len(stacks),))] + sems,
         compiler_params=pltpu.CompilerParams(collective_id=collective_id, has_side_effects=True, vmem_limit_bytes=ROOM),
         cost_estimate=pl.CostEstimate(flops=0, bytes_accessed=LINK_COST, transcendentals=0),
         name=name,
-    )(part, kept, scale, base, gain, share, small, sent, place, *arrays)
+    )(part, kept, scale, base, gain, share, small, sent, place, *stacks, *extra, *arrays)
 
 
 CHUNKS = 4
@@ -1269,6 +1357,42 @@
     return by_rows(unproject_kernel, 256, [d_pre, pre, scale], [w_in], outs, CAP // STEP, 2 * CAP * D * w_in.shape[1], "unproject")
 
 
+def blocks_kernel(shard, a, x, b, y, *outs):
+    tall = a.shape[1]
+    first, second = dg(a[...], x[...], TN).astype(BF), dg(b[...], y[...], TN).astype(BF)
+    for i, out in enumerate(outs):
+        @pl.when(pl.program_id(0) == i)
+        def _():
+            out[:tall] = first
+            out[tall:] = second
+
+
+def grad_blocks(m, device, a, x, b, y):
+    wide, tall = x.shape[1] // m, a.shape[1] + b.shape[1]
+    if wide % 128:
+        both = jnp.concatenate([dg(a, x, TN), dg(b, y, TN)], axis=0).astype(BF)
+        return [lax.dynamic_slice_in_dim(both, lax.rem(device + i, m) * wide, wide, 1) for i in range(m)]
+
+    def side(i, shard):
+        return (0, lax.rem(shard[0] + i, m))
+
+    def fixed(i, shard):
+        return (0, 0)
+
+    return pl.pallas_call(
+        blocks_kernel,
+        grid_spec=pltpu.PrefetchScalarGridSpec(
+            num_scalar_prefetch=1, grid=(m,),
+            in_specs=[pl.BlockSpec(a.shape, fixed, pipeline_mode=pl.Buffered(1)), pl.BlockSpec((CAP, wide), side),
+                      pl.BlockSpec(b.shape, fixed, pipeline_mode=pl.Buffered(1)), pl.BlockSpec((CAP, wide), side)],
+            out_specs=[pl.BlockSpec((tall, wide), fixed)] * m),
+        out_shape=[jax.ShapeDtypeStruct((tall, wide), BF)] * m,
+        compiler_params=pltpu.CompilerParams(dimension_semantics=("arbitrary",), vmem_limit_bytes=ROOM),
+        cost_estimate=pl.CostEstimate(flops=2 * CAP * tall * x.shape[1], bytes_accessed=12 * 2**20, transcendentals=0),
+        name="gradient_blocks",
+    )(device[None], a, x, b, y)
+
+
 PRE = 1152
 GROUP = ("head", "tensor")
 
@@ -1302,21 +1426,23 @@
     return weights.transpose(1, 0, 2).reshape(weights.shape[1], -1)
 
 
-def swap_ring(*grads):
+def gather_ring(piece):
     shards, device = lax.axis_size("shard"), lax.axis_index("shard")
-    wide = grads[0].shape[1] // shards
-
-    def block(i):
-        at = lax.rem(device + i, shards) * wide
-        return jnp.concatenate([lax.dynamic_slice_in_dim(g, at, wide, 1) for g in grads], axis=0)
-
-    total = block(0).astype(F32)
+    wide = piece.shape[1]
+    whole = jnp.zeros((piece.shape[0], shards * wide), piece.dtype)
+    for i in range(shards):
+        came = lax.ppermute(piece, "shard", [(o, (o + i) % shards) for o in range(shards)]) if i else piece
+        whole = lax.dynamic_update_slice_in_dim(whole, came, lax.rem(device - i + shards, shards) * wide, 1)
+    return whole
+
+
+def swap_ring(a, x, b, y):
+    shards, device = lax.axis_size("shard"), lax.axis_index("shard")
+    blocks = grad_blocks(shards, device, a, x, b, y)
+    total = blocks[0].astype(F32)
     for i in range(1, shards):
-        total = total + lax.ppermute(block(i), "shard", [(a, (a + i) % shards) for a in range(shards)]).astype(F32)
-    ends = [0]
-    for g in grads:
-        ends.append(ends[-1] + g.shape[0])
-    return [total[i:j] for i, j in zip(ends, ends[1:])]
+        total = total + lax.ppermute(blocks[i], "shard", [(o, (o + i) % shards) for o in range(shards)]).astype(F32)
+    return total[:a.shape[1]], total[a.shape[1]:]
 
 
 def sum_blocks(blocks):
@@ -1339,10 +1465,10 @@
 
     n = lax.axis_size("head")
     side = side_by_side(w_up.shape[0])
-    x_rows, rows_full, sent_slot, recv_slot, pos, filled_f, w_in, w_o = z_gather(
-        n, seq_lengths, dealing, own_rows, per_peer, 1, "gather_rows", shards, ("gather", side), (w_piece, w_out))
-    w_o = level(w_o)
-    rows_full, cot_piece = lax.optimization_barrier((rows_full, cotangent))
+    x_rows, rows_full, sent_slot, recv_slot, pos, filled_f, w_in = z_gather(
+        n, seq_lengths, dealing, own_rows, per_peer, 1, "gather_rows", shards, ("gather",), (w_piece,))
+    rows_full, cot_piece, w_out = lax.optimization_barrier((rows_full, cotangent, w_out))
+    w_o = gather_ring(w_out)
     cot_full = full_rows(cot_piece)
     pre, normed, scale_one = project(rows_full, gain_mixer[None, :], w_in)
     mixed, *saved = mixer_fwd(pre, pos, filled_f, taps, head_gain)
@@ -1354,19 +1480,17 @@
         held_full, cot_full, gain_ffn[None, :], w_ug, w_u, w_d)
     down_kind, d_w_down = column_blocks(mm(product, cot_full, TN).astype(BF), shards)
     gate_kind, d_w_ug = column_blocks(mm(d_gate, normed_two, TN).astype(BF), shards)
-    d_w_u = mm(d_up, normed_two, TN).astype(BF)
     ffn_gain_part = lax.dynamic_slice_in_dim(gain_ffn, col_start, width)[None, :]
     d_hidden, d_branch_full, _, ffn_gain_grad, d_w_ug, d_w_down = z_turn(
         n, d_normed_two, cotangent, 4, "turn_normed_two", shards, (gate_kind, down_kind), (d_w_ug, d_w_down),
         norm=(held_low, scale_two, ffn_gain_part, share_two))
     out_part = mm(product, w_d).astype(BF)
     out_part, d_branch_full = lax.optimization_barrier((out_part, d_branch_full))
-    d_w_u, d_w_out = swap_ring(d_w_u, mm(mixed, d_branch_full, TN).astype(BF))
+    d_w_u, d_w_out = swap_ring(d_up, normed_two, mixed, d_branch_full)
     out_sum = shares(out_part)
     d_mixed = mm(d_branch_full, w_o, NT)
     d_pre, d_taps, d_head_gain = mixer_bwd(d_mixed, pre, pos, filled_f, taps, head_gain, saved)
     d_normed, share_one = unproject(d_pre, pre, scale_one, w_in)
-    d_w_in = mm(normed, d_pre, TN).astype(BF).reshape(shards, w_piece.shape[0], PRE)
     d_normed, out_sum = lax.optimization_barrier((d_normed, out_sum))
     block_out = (hidden + out_sum).astype(BF)
     mixer_gain_part = lax.dynamic_slice_in_dim(gain_mixer, col_start, width)[None, :]
@@ -1374,10 +1498,9 @@
         jnp.sum(d_taps, axis=1), jnp.zeros((1, width), F32), jnp.sum(ffn_gain_grad, axis=0)[None, :],
         jnp.pad(jnp.sum(d_head_gain, axis=0), (0, width - HD))[None, :],
         jnp.zeros((1, width), F32)], axis=0)
-    d_tokens, summed, d_w_in = z_finish(
+    d_tokens, summed, d_w_ug, d_w_down, d_w_in = z_finish(
         n, d_normed, x_rows, scale_one, d_hidden, mixer_gain_part, share_one, small,
-        sent_slot, recv_slot, per_peer, 6, "finish_rows", shards, ("swap",), (d_w_in,))
-    d_tokens = d_tokens.reshape(REAL_DEV, 1, width)
+        sent_slot, recv_slot, per_peer, 6, "finish_rows", shards, normed, d_pre, (d_w_ug, d_w_down))
     d_w_in = sum_blocks(d_w_in)
     by_row = summed.transpose(1, 0, 2).reshape(16, D)
     d_conv = by_row[:12].reshape(CONV, 3, D)
@@ -1388,7 +1511,7 @@
         d_w_in[:, cut[0]:cut[1]], d_w_in[:, cut[1]:cut[2]], d_w_in[:, cut[2]:cut[3]], d_w_in[:, cut[3]:cut[4]],
         d_w_in[:, 4 * width:4 * width + w_beta.shape[1]],
         d_conv, d_gain_heads, d_w_out, by_row[13],
-        sum_blocks(d_w_ug).T, d_w_u.T, sum_blocks(d_w_down),
+        d_w_ug.T, d_w_u.T, d_w_down,
     )
 
 

time: 577 us -> 547 us (0.948)
  matrix products: 53 us -> 32.9 us
  other arithmetic: 16 us -> 9.36 us
    dot_general x8 -> x5, matrix products: 53 us -> 32.9 us  [mm(): return lax.dot_general(left, right, dims, preferred_element_type=F32)]
    pallas_call x1 -> x2, Pallas kernels: 72.4 us -> 87.7 us  [the longest x1 76.8 us: z_finish(): pl.pallas_call(functools.partial(finish_kernel, n, width, m, kinds, int(f...]
    pallas_call x1, Pallas kernels: 78.7 us -> 70.4 us  [z_gather(): pl.pallas_call(functools.partial(gather_kernel, n, width, m, kinds), out_...]
    pallas_call x1, Pallas kernels: 35.5 us -> 28.8 us  [mixer_fwd(): pl.pallas_call(fwd_kernel, out_shape=outs, in_specs=[VM] * 5, out_specs=[...]
  transfers between devices with their start and end apart: 5 -> 8, of which waited for: 1 -> 0; matrix products, arithmetic and copies ran while one was open for 8% -> 4% of each run, Pallas kernels for 18% -> 20%
where the time goes in v4:
time: 547 us; the launch traced here: 540 us
  Pallas kernels  456 us (83%)
  matrix products  32.9 us (6%)
  local copies, waits for them, and re-layouts  18.3 us (3%)
  between operations  14.8 us (3%)
  starting transfers between devices  9.39 us (2%)
  other arithmetic  9.36 us (2%)
    pallas_call x2, Pallas kernels, z_turn(): pl.pallas_call(functools.partial(turn_kernel, n, width, m, kinds, norm is...  171 us
    pallas_call x1, Pallas kernels, z_finish(): pl.pallas_call(functools.partial(finish_kernel, n, width, m, kinds, int(f...  76.8 us
    pallas_call x1, Pallas kernels, z_gather(): pl.pallas_call(functools.partial(gather_kernel, n, width, m, kinds), out_...  70.4 us
    pallas_call x3, Pallas kernels, by_rows(): pl.pallas_call(kernel, grid=(CAP // rows,), out_shape=shapes, in_specs=sp...  58.5 us
    pallas_call x1, Pallas kernels, mixer_bwd(): pl.pallas_call(bwd_kernel, out_shape=outs, in_specs=[VM] * 6 + [pl.BlockS...  39.6 us
    dot_general x5, matrix products, mm(): return lax.dot_general(left, right, dims, preferred_element_type=F32)  32.9 us
    pallas_call x1, Pallas kernels, mixer_fwd(): pl.pallas_call(fwd_kernel, out_shape=outs, in_specs=[VM] * 5, out_specs=[...  28.8 us
    pallas_call x1, Pallas kernels, grad_blocks(): pl.pallas_call(blocks_kernel, grid_spec=pltpu.PrefetchScalarGridSpec(num_...  11 us
  transfers between devices with their start and end apart: 8, of which 0 were waited for; matrix products, arithmetic and copies ran while one was open for 4% of the time, Pallas kernels for 20%

profile of v4, /device:TPU:0, one launch (start us, length us, event | category | flops | bytes accessed | tf_op | source)
XLA Modules:
  0.0 540.3 jit_solution(8213926517249621003)
XLA Ops:
  8.2 3.1 concatenate.6.refs_3_
  11.3 70.4 %gather_rows.1 = (bf16[1280,256]{1,0:T(8,128)(2,1)}, bf16[1280,2048]{1,0:T(8,128)(2,1)}, s32[1152,1]{1,0:T(8,128)}, s32[1,1280]{1,0:T(1,128)}, s32[1280,1]{1,0:T...) custom-call(s32[16]{0:T(128)} %refs_0_.1, s32[16]{0:T(128)} %refs_1_.1, bf16[1152,256]{1,0:T(8,128)(2,1)} %bitcast.31, ...), custom_call_target="tpu_custom_call" | custom-call | bytes 157286400 | tf_op jit(solution)/shard_map/gather_rows/pallas_call | solution.py:616
  81.8 1.7 collective-permute-start.1
  83.5 3.0 collective-permute-start.2
  86.6 13.5 %project.1 = (f32[1280,1152]{1,0:T(8,128)}, bf16[1280,2048]{1,0:T(8,128)(2,1)}, f32[1280,1]{1,0:T(8,128)}) custom-call(bf16[1280,2048]{1,0:T(8,128)(2,1)} %get-tuple-element.78.x, f32[1,2048]{1,0:T(1,128)} %bitcast.43, bf16[2048,1152]{1,0:T(8,128)(2,1)} %get-tuple-element.79.w), custom_call_target="tpu_custom_call" | custom-call | flops 6039797760 | bytes 20971520 | tf_op jit(solution)/shard_map/project/pallas_call | solution.py:1285
  100.9 1.3 dynamic_slice.6
  102.2 28.8 %mixer_forward.1 = (bf16[1280,256]{1,0:T(8,128)(2,1)}, f32[1280,768]{1,0:T(8,128)}, f32[1280,512]{1,0:T(8,128)}, f32[1280,256]{1,0:T(8,128)}, f32[1280,256]{1,0:...) custom-call(f32[1280,1152]{1,0:T(8,128)} %get-tuple-element.80.pre, ...), custom_call_target="tpu_custom_call" | custom-call | bytes 146800640 | tf_op jit(solution)/shard_map/mixer_forward/pallas_call | solution.py:164
  131.2 4.9 convolution_convert_fusion.1.refs_0_
  136.1 83.3 %turn_branch.1 = (f32[1280,256]{1,0:T(8,128)}, bf16[1280,2048]{1,0:T(8,128)(2,1)}, bf16[1280,256]{1,0:T(8,128)(2,1)}, bf16[704,2048]{1,0:T(8,128)(2,1)}, bf16[70...) custom-call(bf16[1280,2048]{1,0:T(8,128)(2,1)} %convolution_convert_fusion.1.refs_0_, ...), custom_call_target="tpu_custom_call" | custom-call | bytes 157286400 | tf_op jit(solution)/shard_map/turn_branch/pallas_call | solution.py:1257
  219.4 31.6 %feed_forward.1 = (bf16[1280,2048]{1,0:T(8,128)(2,1)}, bf16[1280,704]{1,0:T(8,128)(2,1)}, bf16[1280,704]{1,0:T(8,128)(2,1)}, bf16[1280,704]{1,0:T(8,128)(2,1)}, ...) custom-call(bf16[1280,2048]{1,0:T(8,128)(2,1)} %get-tuple-element.89.x, ...), custom_call_target="tpu_custom_call" | custom-call | flops 18454937600 | bytes 20971520 | tf_op jit(solution)/shard_map/feed_forward/pallas_call | solution.py:1285
  251.1 8.7 %convolution_convert_fusion.2.refs_7_ = bf16[704,2048]{1,0:T(8,128)(2,1)} fusion(bf16[1280,704]{1,0:T(8,128)(2,1)} %get-tuple-element.94, bf16[1280,2048]{1,0:T(8,128)(2,1)} %all-gather.2.cloned.1.call-done.cot), kind=kOutput, calls=%fused_computation.3 | convolution fusion | flops 3692429312 | bytes 9928704 | tf_op jit(solution)/shard_map/dot_general | solution.py:1401
  259.8 6.0 %convolution_convert_fusion = bf16[1280,2048]{1,0:T(8,128)(2,1)} fusion(bf16[1280,704]{1,0:T(8,128)(2,1)S(1)} %copy-done.11, bf16[704,2048]{1,0:T(8,128)(2,1)S(1)} %copy-done.9), kind=kOutput, calls=%fused_computation.1 | convolution fusion | flops 3693608960 | bytes 9928704 | tf_op jit(solution)/shard_map/dot_general | solution.py:1401
  265.9 8.1 %convolution_convert_fusion.3.refs_6_ = bf16[704,2048]{1,0:T(8,128)(2,1)} fusion(bf16[1280,704]{1,0:T(8,128)(2,1)S(1)} %copy-done.10, bf16[1280,2048]{1,0:T(8,128)(2,1)} %get-tuple-element.100.x), kind=kOutput, calls=%fused_computation.4 | convolution fusion | flops 3692429312 | bytes 9928704 | tf_op jit(solution)/shard_map/dot_general | solution.py:1401
  274.0 87.2 %turn_normed_two.1 = (f32[1280,256]{1,0:T(8,128)}, bf16[1280,2048]{1,0:T(8,128)(2,1)}, bf16[1280,256]{1,0:T(8,128)(2,1)}, f32[8,256]{1,0:T(8,128)}, bf16[4,704,5...) custom-call(bf16[1280,2048]{1,0:T(8,128)(2,1)} %get-tuple-element.95.refs_0_, ...), custom_call_target="tpu_custom_call" | custom-call | bytes 157286400 | tf_op jit(solution)/shard_map/turn_normed_two/pallas_call | solution.py:1257
  361.2 1.3 dynamic_slice.7
  362.5 11.0 %gradient_blocks.1 = (bf16[960,512]{1,0:T(8,128)(2,1)}, bf16[960,512]{1,0:T(8,128)(2,1)}, bf16[960,512]{1,0:T(8,128)(2,1)}, bf16[960,512]{1,0:T(8,128)(2,1)}) custom-call(s32[1]{0:T(128)} %bitcast.12.shard, bf16[1280,704]{1,0:T(8,128)(2,1)} %get-tuple-element.132.a, bf16[1280,2048]{1,0:T(8,128)(2,1)} %get-tuple-element.100.x, ...), custom_call_target="tpu_custom_call" | custom-call | flops 5033164800 | bytes 12582912 | tf_op jit(solution)/shard_map/gradient_blocks/pallas_call | solution.py:1382
  373.5 1.6 collective-permute-start.3
  375.8 2.1 collective-permute-start.5
  378.0 5.2 fusion.2.dmix
  383.1 39.6 %mixer_backward.1 = (bf16[1280,1152]{1,0:T(8,128)(2,1)}, f32[12,8,256]{2,1,0:T(8,128)}, f32[8,128]{1,0:T(8,128)}) custom-call(f32[1280,256]{1,0:T(8,128)} %fusion.2.dmix, f32[1280,1152]{1,0:T(8,128)} %get-tuple-element.80.pre, s32[1280,1]{1,0:T(8,128)} %get-tuple-element.81.pos_ref, f32[1280,1]{1,0:T(8,128)} %get-tuple-element.82.fill_ref, ...), custom_call_target="tpu_custom_call" | custom-call | bytes 209715200 | tf_op jit(solution)/shard_map/mixer_backward/pallas_call | solution.py:302
  424.4 1.9 concatenate.7.refs_6_
  426.3 13.4 %unproject.1 = (bf16[1280,2048]{1,0:T(8,128)(2,1)}, f32[10,8,128]{2,1,0:T(8,128)}) custom-call(bf16[1280,1152]{1,0:T(8,128)(2,1)} %get-tuple-element.113.d_pre.refs_12_, f32[1280,1152]{1,0:T(8,128)} %get-tuple-element.80.pre, f32[1280,1]{1,0:T(8,128)} %get-tuple-element.114.scale.refs_2_, bf16[2048,1152]{1,0:T(8,128)(2,1)} %get-tuple-element.79.w), custom_call_target="tpu_custom_call" | custom-call | flops 6039797760 | bytes 20971520 | tf_op jit(solution)/shard_map/unproject/pallas_call | solution.py:1285
  439.7 1.7 convert_add_fusion
  442.2 1.2 slice_bitcast_fusion
  443.5 1.2 convert_element_type.39
  444.6 76.8 %finish_rows.1 = (f32[1152,1,256]{2,1,0:T(1,128)}, f32[8,16,256]{2,1,0:T(8,128)}, f32[704,512]{1,0:T(8,128)}, f32[704,512]{1,0:T(8,128)}, bf16[4,512,1152]{2,1,0:T(8,128)(2,1)}) custom-call(bf16[1280,2048]{1,0:T(8,128)(2,1)} %get-tuple-element.118.refs_0_, bf16[1280,256]{1,0:T(8,128)(2,1)} %get-tuple-element.87.refs_1_, ...), custom_call_target="tpu_custom_call" | custom-call | bytes 157286400 | tf_op jit(solution)/shard_map/finish_rows/pallas_call | solution.py:962
  521.4 3.3 convert_reduce_fusion
  524.8 1.4 fusion
  528.9 1.0 add_convert_fusion
  529.8 1.0 copy.58
  530.9 1.1 copy.59
  532.0 1.1 copy.60
  (60 shorter events, 8.0 us)
Async XLA Ops:
  7.2 74.6 %copy-start.5 = (bf16[256,512]{1,0:T(8,128)(2,1)S(1)}, bf16[256,512]{1,0:T(8,128)(2,1)}, u32[]{:S(2)}) copy-start(bf16[256,512]{1,0:T(8,128)(2,1)} %param.28) | copy-start | bytes 786436
  7.2 128.9 %all-gather.2.cloned.1.call-start = ((), (), s32[]{:S(2)}) async-start(), calls=%async_computation.1 | async-start | bytes 5898240 | tf_op jit(solution)/shard_map/all_gather | solution.py:1405
  81.7 361.8 %reduce-scatter.2.cloned.1.call-start = ((), (), s32[]{:S(2)}) async-start(), calls=%async_computation.2 | async-start | bytes 5898240 | tf_op jit(solution)/shard_map/reduce_scatter | solution.py:1409
  81.7 49.3 %collective-permute-start = (bf16[256,512]{1,0:T(8,128)(2,1)S(1)}, bf16[256,512]{1,0:T(8,128)(2,1)S(1)}, u32[]{:S(2)}, u32[]{:S(2)}) collective-permute-start(bf16[256,512]{1,0:T(8,128)(2,1)S(1)} %copy-done.5), channel_id=1, source_target_pairs={{0,8},{8,16},{16,24},{24,0},{1,9},{9,17},{17,25},{25,1},{2,10},{10... | collective-permute-start | bytes 786440 | tf_op jit(solution)/shard_map/ppermute | solution.py:1434
  81.8 49.3 %collective-permute-start.1 = (bf16[256,512]{1,0:T(8,128)(2,1)S(1)}, bf16[256,512]{1,0:T(8,128)(2,1)S(1)}, u32[]{:S(2)}, u32[]{:S(2)}) collective-permute-start(bf16[256,512]{1,0:T(8,128)(2,1)S(1)} %copy-done.5), channel_id=1, source_target_pairs={{0,16},{8,24},{16,0},{24,8},{1,17},{9,25},{17,1},{25,9},{2,18},{10... | collective-permute-start | bytes 786440 | tf_op jit(solution)/shard_map/ppermute | solution.py:1434
  83.5 47.6 %collective-permute-start.2 = (bf16[256,512]{1,0:T(8,128)(2,1)S(1)}, bf16[256,512]{1,0:T(8,128)(2,1)S(1)}, u32[]{:S(2)}, u32[]{:S(2)}) collective-permute-start(bf16[256,512]{1,0:T(8,128)(2,1)S(1)} %copy-done.5), channel_id=1, source_target_pairs={{0,24},{8,0},{16,8},{24,16},{1,25},{9,1},{17,9},{25,17},{2,26},{10... | collective-permute-start | bytes 786440 | tf_op jit(solution)/shard_map/ppermute | solution.py:1434
  86.6 13.7 %copy-start.7 = (f32[4,3,256]{2,0,1:T(4,128)S(1)}, f32[4,3,256]{2,0,1:T(4,128)}, u32[]{:S(2)}) copy-start(f32[4,3,256]{2,0,1:T(4,128)} %param.26) | copy-start | bytes 36868
  251.1 8.7 %copy-start.9 = (bf16[704,2048]{1,0:T(8,128)(2,1)S(1)}, bf16[704,2048]{1,0:T(8,128)(2,1)}, u32[]{:S(2)}) copy-start(bf16[704,2048]{1,0:T(8,128)(2,1)} %get-tuple-element.93.w_d) | copy-start | bytes 8650756
  251.1 8.7 %copy-start.11 = (bf16[1280,704]{1,0:T(8,128)(2,1)S(1)}, bf16[1280,704]{1,0:T(8,128)(2,1)}, u32[]{:S(2)}) copy-start(bf16[1280,704]{1,0:T(8,128)(2,1)} %get-tuple-element.94) | copy-start | bytes 5406724
  259.8 6.0 %copy-start.10 = (bf16[1280,704]{1,0:T(8,128)(2,1)S(1)}, bf16[1280,704]{1,0:T(8,128)(2,1)}, u32[]{:S(2)}) copy-start(bf16[1280,704]{1,0:T(8,128)(2,1)} %get-tuple-element.99) | copy-start | bytes 5406724
  373.5 66.2 %collective-permute-start.3 = (bf16[960,512]{1,0:T(8,128)(2,1)}, bf16[960,512]{1,0:T(8,128)(2,1)S(1)}, u32[]{:S(2)}, u32[]{:S(2)}) collective-permute-start(bf16[960,512]{1,0:T(8,128)(2,1)} %get-tuple-element.134), channel_id=1, source_target_pairs={{0,8},{8,16},{16,24},{24,0},{1,9},{9,17},{17,25},{25,1},{2,10},{10... | collective-permute-start | bytes 2949128 | tf_op jit(solution)/shard_map/ppermute | solution.py:1444
  375.0 64.7 %collective-permute-start.4 = (bf16[960,512]{1,0:T(8,128)(2,1)}, bf16[960,512]{1,0:T(8,128)(2,1)S(1)}, u32[]{:S(2)}, u32[]{:S(2)}) collective-permute-start(bf16[960,512]{1,0:T(8,128)(2,1)} %get-tuple-element.135), channel_id=1, source_target_pairs={{0,16},{8,24},{16,0},{24,8},{1,17},{9,25},{17,1},{25,9},{2,18},{10... | collective-permute-start | bytes 2949128 | tf_op jit(solution)/shard_map/ppermute | solution.py:1444
  375.8 63.9 %collective-permute-start.5 = (bf16[960,512]{1,0:T(8,128)(2,1)}, bf16[960,512]{1,0:T(8,128)(2,1)}, u32[]{:S(2)}, u32[]{:S(2)}) collective-permute-start(bf16[960,512]{1,0:T(8,128)(2,1)} %get-tuple-element.136), channel_id=1, source_target_pairs={{0,24},{8,0},{16,8},{24,16},{1,25},{9,1},{17,9},{25,17},{2,26},{10... | collective-permute-start | bytes 2949128 | tf_op jit(solution)/shard_map/ppermute | solution.py:1444
  383.1 41.2 %copy-start.8 = (f32[8,256]{1,0:T(8,128)S(1)}, f32[8,256]{1,0:T(8,128)}, u32[]{:S(2)}) copy-start(f32[8,256]{1,0:T(8,128)} %get-tuple-element.122) | copy-start | bytes 24580
  426.3 13.4 %copy-start.4 = (bf16[960,512]{1,0:T(8,128)(2,1)S(1)}, bf16[960,512]{1,0:T(8,128)(2,1)}, u32[]{:S(2)}) copy-start(bf16[960,512]{1,0:T(8,128)(2,1)} %get-tuple-element.133) | copy-start | bytes 2949124
  524.8 2.1 copy-start.6
  524.8 4.1 copy-start.2
  528.1 1.7 copy-start.3
  528.9 2.0 copy-start.1
  529.8 2.1 copy-start
Sparse Core Ops, SparseCore 0:
  81.8 54.0 all-gather.1
  361.3 58.5 reduce-scatter.1

commit v5 on v4

--- a/solution.py
+++ b/solution.py
@@ -17,6 +17,8 @@
 NB = CAP // BLOCK
 EPSILON = 1e-06
 HEAD_FLOOR = 0.01
+PRE = 1152
+BETA = 16
 F32 = jnp.float32
 BF = jnp.bfloat16
 
@@ -647,13 +649,13 @@
 
 def finish_kernel(n, width, m, kinds, fill, piles, *refs):
     (part, kept, scale, base, gain, share, small, sent, place, *left), (tokens, every, *grads), scratch, carry = carry_of(
-        kinds, m, refs, 9 + piles + 2 * fill, 2 + piles + fill)
+        kinds, m, refs, 9 + piles + 2 * fill, 2 + piles + 2 * fill)
     stacks, left = left[:piles], left[piles:]
     added, grads = grads[:piles], grads[piles:]
     *scratch, pile_sem = scratch
     heaps, scratch = scratch[:piles], scratch[piles:]
     if fill:
-        *scratch, l_buf, r_buf, blocks, l_sem, r_sem, w_s, w_r, w_own = scratch
+        *scratch, l_buf, r_buf, blocks, strips, l_sem, r_sem, w_s, w_r, w_own = scratch
     (low, dgain, outbox, inbox, deal_s, deal_r, held, ours, shard_s, shard_r, group_s, group_r,
      acc, tots, tot_s, tot_r, mine, theirs, from_below, from_above,
      here, core_s, core_r, up_s, up_r, down_s, down_r) = scratch
@@ -735,11 +737,13 @@
         def fetch(i, q):
             return pltpu.make_async_copy(columns(q), l_buf.at[i], l_sem.at[i])
 
+        made = (blocks, strips)
+
         def grad(i, p, src):
-            return pltpu.make_async_remote_copy(src_ref=blocks.at[i], dst_ref=grads[0].at[src], send_sem=w_s.at[i],
-                                                recv_sem=w_r.at[src], device_id=p[0], device_id_type=MESH)
-
-        own_grad = pltpu.make_async_copy(blocks.at[m - 1], grads[0].at[shard], w_own)
+            return [pltpu.make_async_remote_copy(src_ref=made[e].at[i], dst_ref=grads[e].at[src], send_sem=w_s.at[e, i],
+                                                 recv_sem=w_r.at[e, src], device_id=p[0], device_id_type=MESH) for e in range(2)]
+
+        own_grad = [pltpu.make_async_copy(made[e].at[m - 1], grads[e].at[shard], w_own.at[e]) for e in range(2)]
         whole = pltpu.make_async_copy(rhs, r_buf, r_sem)
         whole.start()
         for i, p in enumerate(others):
@@ -750,11 +754,11 @@
             if i == 0:
                 whole.wait()
             fetch(i, shard).wait()
-            blocks[i] = dg(l_buf[i], r_buf[...], TN).astype(BF)
-            if i < m - 1:
-                grad(i, others[i], shard).start()
-            else:
-                own_grad.start()
+            main = blocks.shape[2]
+            strips[i] = dg(r_buf[:, main:main + BETA], l_buf[i], TN).astype(BF)
+            blocks[i] = dg(l_buf[i], r_buf[:, :main], TN).astype(BF)
+            for c in (grad(i, others[i], shard) if i < m - 1 else own_grad):
+                c.start()
 
         multiply(0)
 
@@ -939,24 +943,29 @@
             fall(k).wait_send()
     carry.wait()
     if fill:
-        own_grad.wait()
+        for c in own_grad:
+            c.wait()
         for i, p in enumerate(others):
-            grad(i, p, p[1]).wait_recv()
-            grad(i, p, shard).wait_send()
+            for c in grad(i, p, p[1]):
+                c.wait_recv()
+            for c in grad(i, p, shard):
+                c.wait_send()
 
 
 def z_finish(n, part, kept, scale, base, gain, share, small, sent, place, per_peer, collective_id, name, m, lhs, rhs, stacks):
     rows, width = part.shape[0], part.shape[1] // (2 * n)
     dma = pltpu.SemaphoreType.DMA
-    wide = lhs.shape[1] // m
+    wide, main = lhs.shape[1] // m, 4 * width
     fill = wide % 128 == 0
     if fill:
         kinds, arrays, extra = (), (), [lhs, rhs]
-        made = [jax.ShapeDtypeStruct((m, wide, rhs.shape[1]), BF)]
+        made = [jax.ShapeDtypeStruct((m, wide, main), BF), jax.ShapeDtypeStruct((m, BETA, wide), BF)]
         room = [pltpu.VMEM((m, rows, wide), BF), pltpu.VMEM(rhs.shape, BF), pltpu.VMEM(made[0].shape, BF),
-                dma((m,)), dma, dma((m,)), dma((m,)), dma]
+                pltpu.VMEM(made[1].shape, BF), dma((m,)), dma, dma((2, m)), dma((2, m)), dma((2,))]
     else:
-        kinds, arrays = ("swap",), (dg(lhs, rhs, TN).astype(BF).reshape(m, wide, rhs.shape[1]),)
+        kinds = ("swap", "swap")
+        arrays = (dg(lhs, rhs[:, :main], TN).astype(BF).reshape(m, wide, main),
+                  dg(rhs[:, main:main + BETA], lhs, TN).astype(BF).reshape(BETA, m, wide).transpose(1, 0, 2))
         extra, made, room = [], [], []
     shapes, sems = carried(kinds, m, arrays)
     return pl.pallas_call(
@@ -1307,17 +1316,20 @@
     return scale, (x * scale * gain).astype(BF)
 
 
-def project_kernel(x, gain, w, pre, normed, scale):
+def project_kernel(x, gain, w, wb, pre, normed, scale):
     sc, nb = normal(x[...], gain[...])
     scale[...] = sc
     normed[...] = nb
-    pre[...] = dg(nb, w[...], NN)
-
-
-def project(rows_full, gain, w_in):
+    main = w.shape[1]
+    pre[:, :main] = dg(nb, w[...], NN)
+    pre[:, main:main + BETA] = dg(nb, wb[...], NT)
+    pre[:, main + BETA:] = jnp.zeros((nb.shape[0], PRE - main - BETA), F32)
+
+
+def project(rows_full, gain, w_in, w_bt):
     sd = jax.ShapeDtypeStruct
-    outs = [sd((CAP, w_in.shape[1]), F32), sd((CAP, D), BF), sd((CAP, 1), F32)]
-    return by_rows(project_kernel, 256, [rows_full], [gain, w_in], outs, 0, 2 * CAP * D * w_in.shape[1], "project")
+    outs = [sd((CAP, PRE), F32), sd((CAP, D), BF), sd((CAP, 1), F32)]
+    return by_rows(project_kernel, 256, [rows_full], [gain, w_in, w_bt], outs, 0, 2 * CAP * D * PRE, "project")
 
 
 def ffn_kernel(x, cot, gain, w_ug, w_u, w_d, normed, product, d_gate, d_up, d_normed, scale, share):
@@ -1346,15 +1358,16 @@
                    10 * CAP * D * ff, "feed_forward")
 
 
-def unproject_kernel(d_pre, pre, scale, w, d_normed, share):
+def unproject_kernel(d_pre, pre, scale, w, wb, d_normed, share):
     d = d_pre[...]
-    d_normed[...] = dg(d, w[...], NT).astype(BF)
+    main = w.shape[1]
+    d_normed[...] = (dg(d[:, :main], w[...], NT) + dg(d_pre[:, main:main + BETA], wb[...], NN)).astype(BF)
     lane_sums(d.astype(F32) * pre[...] / scale[...], share)
 
 
-def unproject(d_pre, pre, scale, w_in):
+def unproject(d_pre, pre, scale, w_in, w_bt):
     outs = [jax.ShapeDtypeStruct((CAP, D), BF)]
-    return by_rows(unproject_kernel, 256, [d_pre, pre, scale], [w_in], outs, CAP // STEP, 2 * CAP * D * w_in.shape[1], "unproject")
+    return by_rows(unproject_kernel, 256, [d_pre, pre, scale], [w_in, w_bt], outs, CAP // STEP, 2 * CAP * D * PRE, "unproject")
 
 
 def blocks_kernel(shard, a, x, b, y, *outs):
@@ -1393,7 +1406,6 @@
     )(device[None], a, x, b, y)
 
 
-PRE = 1152
 GROUP = ("head", "tensor")
 
 
@@ -1456,8 +1468,8 @@
     col_start = lax.axis_index(GROUP) * width
     per_peer = (CAP // shards + SEQ_DEV + 15) // 16 * 16
 
-    w_piece = jnp.concatenate(
-        [w_query, w_key, w_value, w_gate, w_beta, jnp.zeros((w_beta.shape[0], PRE - 4 * width - w_beta.shape[1]), BF)], axis=1)
+    w_piece = jnp.concatenate([w_query, w_key, w_value, w_gate], axis=1)
+    b_piece = jnp.pad(w_beta.T, ((0, BETA - w_beta.shape[1]), (0, 0)))
 
     own_rows = tokens.reshape(REAL_DEV, width)
     taps = conv_weight.reshape(3 * CONV, width)
@@ -1465,12 +1477,14 @@
 
     n = lax.axis_size("head")
     side = side_by_side(w_up.shape[0])
-    x_rows, rows_full, sent_slot, recv_slot, pos, filled_f, w_in = z_gather(
-        n, seq_lengths, dealing, own_rows, per_peer, 1, "gather_rows", shards, ("gather",), (w_piece,))
+    x_rows, rows_full, sent_slot, recv_slot, pos, filled_f, w_in, w_bt = z_gather(
+        n, seq_lengths, dealing, own_rows, per_peer, 1, "gather_rows", shards,
+        ("gather", side_by_side(b_piece.shape[1])), (w_piece, b_piece))
+    w_bt = level(w_bt)
     rows_full, cot_piece, w_out = lax.optimization_barrier((rows_full, cotangent, w_out))
     w_o = gather_ring(w_out)
     cot_full = full_rows(cot_piece)
-    pre, normed, scale_one = project(rows_full, gain_mixer[None, :], w_in)
+    pre, normed, scale_one = project(rows_full, gain_mixer[None, :], w_in, w_bt)
     mixed, *saved = mixer_fwd(pre, pos, filled_f, taps, head_gain)
     branch_part, cot_full = lax.optimization_barrier((mm(mixed, w_o).astype(BF), cot_full))
     hidden, held_full, held_low, w_ug, w_u, w_d = z_turn(
@@ -1490,7 +1504,7 @@
     out_sum = shares(out_part)
     d_mixed = mm(d_branch_full, w_o, NT)
     d_pre, d_taps, d_head_gain = mixer_bwd(d_mixed, pre, pos, filled_f, taps, head_gain, saved)
-    d_normed, share_one = unproject(d_pre, pre, scale_one, w_in)
+    d_normed, share_one = unproject(d_pre, pre, scale_one, w_in, w_bt)
     d_normed, out_sum = lax.optimization_barrier((d_normed, out_sum))
     block_out = (hidden + out_sum).astype(BF)
     mixer_gain_part = lax.dynamic_slice_in_dim(gain_mixer, col_start, width)[None, :]
@@ -1498,7 +1512,7 @@
         jnp.sum(d_taps, axis=1), jnp.zeros((1, width), F32), jnp.sum(ffn_gain_grad, axis=0)[None, :],
         jnp.pad(jnp.sum(d_head_gain, axis=0), (0, width - HD))[None, :],
         jnp.zeros((1, width), F32)], axis=0)
-    d_tokens, summed, d_w_ug, d_w_down, d_w_in = z_finish(
+    d_tokens, summed, d_w_ug, d_w_down, d_w_in, d_w_bt = z_finish(
         n, d_normed, x_rows, scale_one, d_hidden, mixer_gain_part, share_one, small,
         sent_slot, recv_slot, per_peer, 6, "finish_rows", shards, normed, d_pre, (d_w_ug, d_w_down))
     d_w_in = sum_blocks(d_w_in)
@@ -1509,7 +1523,7 @@
     return (
         block_out, d_tokens, by_row[12],
         d_w_in[:, cut[0]:cut[1]], d_w_in[:, cut[1]:cut[2]], d_w_in[:, cut[2]:cut[3]], d_w_in[:, cut[3]:cut[4]],
-        d_w_in[:, 4 * width:4 * width + w_beta.shape[1]],
+        sum_blocks(d_w_bt)[:w_beta.shape[1]].T,
         d_conv, d_gain_heads, d_w_out, by_row[13],
         d_w_ug.T, d_w_u.T, d_w_down,
     )

time: 547 us -> 542 us (level)
  no operation moved by 1% of the time
where the time goes in v5:
time: 542 us; the launch traced here: 536 us
  Pallas kernels  451 us (83%)
  matrix products  31.9 us (6%)
  local copies, waits for them, and re-layouts  16.3 us (3%)
  between operations  14.8 us (3%)
  other arithmetic  11.8 us (2%)
  starting transfers between devices  9.4 us (2%)
    pallas_call x2, Pallas kernels, z_turn(): pl.pallas_call(functools.partial(turn_kernel, n, width, m, kinds, norm is...  171 us
    pallas_call x1, Pallas kernels, z_finish(): pl.pallas_call(functools.partial(finish_kernel, n, width, m, kinds, int(f...  72.9 us
    pallas_call x1, Pallas kernels, z_gather(): pl.pallas_call(functools.partial(gather_kernel, n, width, m, kinds), out_...  70.4 us
    pallas_call x3, Pallas kernels, by_rows(): pl.pallas_call(kernel, grid=(CAP // rows,), out_shape=shapes, in_specs=sp...  57.9 us
    pallas_call x1, Pallas kernels, mixer_bwd(): pl.pallas_call(bwd_kernel, out_shape=outs, in_specs=[VM] * 6 + [pl.BlockS...  39.6 us
    dot_general x5, matrix products, mm(): return lax.dot_general(left, right, dims, preferred_element_type=F32)  31.9 us
    pallas_call x1, Pallas kernels, mixer_fwd(): pl.pallas_call(fwd_kernel, out_shape=outs, in_specs=[VM] * 5, out_specs=[...  28.8 us
    pallas_call x1, Pallas kernels, grad_blocks(): pl.pallas_call(blocks_kernel, grid_spec=pltpu.PrefetchScalarGridSpec(num_...  10.9 us
  transfers between devices with their start and end apart: 8, of which 0 were waited for; matrix products, arithmetic and copies ran while one was open for 4% of the time, Pallas kernels for 20%

profile of v5, /device:TPU:0, one launch (start us, length us, event | category | flops | bytes accessed | tf_op | source)
XLA Modules:
  0.0 535.5 jit_solution(17815648327514180587)
XLA Ops:
  7.2 1.3 pad.8.refs_4_
  8.5 2.3 pad_maximum_fusion.refs_3_
  10.9 70.4 %gather_rows.1 = (bf16[1280,256]{1,0:T(8,128)(2,1)}, bf16[1280,2048]{1,0:T(8,128)(2,1)}, s32[1152,1]{1,0:T(8,128)}, s32[1,1280]{1,0:T(1,128)}, s32[1280,1]{1,0:T...) custom-call(s32[16]{0:T(128)} %refs_0_.1, s32[16]{0:T(128)} %refs_1_.1, ...), custom_call_target="tpu_custom_call" | custom-call | bytes 157286400 | tf_op jit(solution)/shard_map/gather_rows/pallas_call | solution.py:618
  81.4 1.7 collective-permute-start.1
  83.1 3.0 collective-permute-start.2
  86.2 13.4 %project.1 = (f32[1280,1152]{1,0:T(8,128)}, bf16[1280,2048]{1,0:T(8,128)(2,1)}, f32[1280,1]{1,0:T(8,128)}) custom-call(bf16[1280,2048]{1,0:T(8,128)(2,1)} %get-tuple-element.80.x, f32[1,2048]{1,0:T(1,128)} %bitcast.47, bf16[2048,1024]{1,0:T(8,128)(2,1)} %get-tuple-element.81.w, bf16[16,2048]{1,0:T(8,128)(2,1)} %get-tuple-element.82.wb), custom_call_target="tpu_custom_call" | custom-call | flops 6039797760 | bytes 20971520 | tf_op jit(solution)/shard_map/project/pallas_call | solution.py:1294
  100.3 1.3 dynamic_slice.6
  101.7 28.8 %mixer_forward.1 = (bf16[1280,256]{1,0:T(8,128)(2,1)}, f32[1280,768]{1,0:T(8,128)}, f32[1280,512]{1,0:T(8,128)}, f32[1280,256]{1,0:T(8,128)}, f32[1280,256]{1,0:...) custom-call(f32[1280,1152]{1,0:T(8,128)} %get-tuple-element.83.pre, ...), custom_call_target="tpu_custom_call" | custom-call | bytes 146800640 | tf_op jit(solution)/shard_map/mixer_forward/pallas_call | solution.py:166
  131.6 3.8 convolution_convert_fusion.1.refs_0_
  135.4 83.6 %turn_branch.1 = (f32[1280,256]{1,0:T(8,128)}, bf16[1280,2048]{1,0:T(8,128)(2,1)}, bf16[1280,256]{1,0:T(8,128)(2,1)}, bf16[704,2048]{1,0:T(8,128)(2,1)}, bf16[70...) custom-call(bf16[1280,2048]{1,0:T(8,128)(2,1)} %convolution_convert_fusion.1.refs_0_, ...), custom_call_target="tpu_custom_call" | custom-call | bytes 157286400 | tf_op jit(solution)/shard_map/turn_branch/pallas_call | solution.py:1266
  219.0 31.7 %feed_forward.1 = (bf16[1280,2048]{1,0:T(8,128)(2,1)}, bf16[1280,704]{1,0:T(8,128)(2,1)}, bf16[1280,704]{1,0:T(8,128)(2,1)}, bf16[1280,704]{1,0:T(8,128)(2,1)}, ...) custom-call(bf16[1280,2048]{1,0:T(8,128)(2,1)} %get-tuple-element.92.x, ...), custom_call_target="tpu_custom_call" | custom-call | flops 18454937600 | bytes 20971520 | tf_op jit(solution)/shard_map/feed_forward/pallas_call | solution.py:1294
  250.7 8.8 %convolution_convert_fusion.2.refs_7_ = bf16[704,2048]{1,0:T(8,128)(2,1)} fusion(bf16[1280,704]{1,0:T(8,128)(2,1)} %get-tuple-element.97, bf16[1280,2048]{1,0:T(8,128)(2,1)} %all-gather.2.cloned.1.call-done.cot), kind=kOutput, calls=%fused_computation.3 | convolution fusion | flops 3692429312 | bytes 9928704 | tf_op jit(solution)/shard_map/dot_general | solution.py:1413
  259.4 6.0 %convolution_convert_fusion = bf16[1280,2048]{1,0:T(8,128)(2,1)} fusion(bf16[1280,704]{1,0:T(8,128)(2,1)S(1)} %copy-done.13, bf16[704,2048]{1,0:T(8,128)(2,1)S(1)} %copy-done.11), kind=kOutput, calls=%fused_computation.1 | convolution fusion | flops 3693608960 | bytes 9928704 | tf_op jit(solution)/shard_map/dot_general | solution.py:1413
  265.4 8.1 %convolution_convert_fusion.3.refs_6_ = bf16[704,2048]{1,0:T(8,128)(2,1)} fusion(bf16[1280,704]{1,0:T(8,128)(2,1)S(1)} %copy-done.12, bf16[1280,2048]{1,0:T(8,128)(2,1)} %get-tuple-element.103.x), kind=kOutput, calls=%fused_computation.4 | convolution fusion | flops 3692429312 | bytes 9928704 | tf_op jit(solution)/shard_map/dot_general | solution.py:1413
  273.5 87.2 %turn_normed_two.1 = (f32[1280,256]{1,0:T(8,128)}, bf16[1280,2048]{1,0:T(8,128)(2,1)}, bf16[1280,256]{1,0:T(8,128)(2,1)}, f32[8,256]{1,0:T(8,128)}, bf16[4,704,5...) custom-call(bf16[1280,2048]{1,0:T(8,128)(2,1)} %get-tuple-element.98.refs_0_, ...), custom_call_target="tpu_custom_call" | custom-call | bytes 157286400 | tf_op jit(solution)/shard_map/turn_normed_two/pallas_call | solution.py:1266
  360.7 1.3 dynamic_slice.7
  362.1 10.9 %gradient_blocks.1 = (bf16[960,512]{1,0:T(8,128)(2,1)}, bf16[960,512]{1,0:T(8,128)(2,1)}, bf16[960,512]{1,0:T(8,128)(2,1)}, bf16[960,512]{1,0:T(8,128)(2,1)}) custom-call(s32[1]{0:T(128)} %bitcast.14.shard, bf16[1280,704]{1,0:T(8,128)(2,1)} %get-tuple-element.136.a, bf16[1280,2048]{1,0:T(8,128)(2,1)} %get-tuple-element.103.x, ...), custom_call_target="tpu_custom_call" | custom-call | flops 5033164800 | bytes 12582912 | tf_op jit(solution)/shard_map/gradient_blocks/pallas_call | solution.py:1395
  373.0 1.5 collective-permute-start.3
  375.2 2.2 collective-permute-start.5
  377.4 5.2 fusion.2.dmix
  382.7 39.6 %mixer_backward.1 = (bf16[1280,1152]{1,0:T(8,128)(2,1)}, f32[12,8,256]{2,1,0:T(8,128)}, f32[8,128]{1,0:T(8,128)}) custom-call(f32[1280,256]{1,0:T(8,128)} %fusion.2.dmix, f32[1280,1152]{1,0:T(8,128)} %get-tuple-element.83.pre, s32[1280,1]{1,0:T(8,128)} %get-tuple-element.84.pos_ref, f32[1280,1]{1,0:T(8,128)} %get-tuple-element.85.fill_ref, ...), custom_call_target="tpu_custom_call" | custom-call | bytes 209715200 | tf_op jit(solution)/shard_map/mixer_backward/pallas_call | solution.py:304
  423.9 1.9 concatenate.7.refs_6_
  425.8 12.9 %unproject.1 = (bf16[1280,2048]{1,0:T(8,128)(2,1)}, f32[10,8,128]{2,1,0:T(8,128)}) custom-call(bf16[1280,1152]{1,0:T(8,128)(2,1)} %get-tuple-element.116.d_pre.refs_12_, f32[1280,1152]{1,0:T(8,128)} %get-tuple-element.83.pre, f32[1280,1]{1,0:T(8,128)} %get-tuple-element.117.scale.refs_2_, bf16[2048,1024]{1,0:T(8,128)(2,1)} %get-tuple-element.81.w, ...), custom_call_target="tpu_custom_call" | custom-call | flops 6039797760 | bytes 20971520 | tf_op jit(solution)/shard_map/unproject/pallas_call | solution.py:1294
  438.8 1.7 convert_add_fusion
  441.3 1.2 slice_bitcast_fusion
  442.5 1.2 convert_element_type.44
  443.7 72.9 %finish_rows.1 = (f32[1152,1,256]{2,1,0:T(1,128)}, f32[8,16,256]{2,1,0:T(8,128)}, f32[704,512]{1,0:T(8,128)}, f32[704,512]{1,0:T(8,128)}, bf16[4,512,1024]{2,1,0:T(8,128)(2,1)}, /*index=5*/bf16[4,16,512]{2,1,0:T(8,128)(2,1)}) custom-call(bf16[1280,2048]{1,0:T(8,128)(2,1)} %get-tuple-element.121.refs_0_, bf16[1280,256]{1,0:T(8,128)(2,1)} %get-tuple-element.90.refs_1_, ...), custom_call_target="tpu_custom_call" | custom-call | bytes 157286400 | tf_op jit(solution)/shard_map/finish_rows/pallas_call | solution.py:971
  516.6 3.4 convert_reduce_fusion
  520.1 1.4 fusion
  525.0 1.0 copy.43
  526.0 1.1 copy.44
  527.1 1.1 copy.45
  (63 shorter events, 8.8 us)
Async XLA Ops:
  7.2 128.2 %all-gather.2.cloned.1.call-start = ((), (), s32[]{:S(2)}) async-start(), calls=%async_computation.1 | async-start | bytes 5898240 | tf_op jit(solution)/shard_map/all_gather | solution.py:1417
  8.5 72.8 %copy-start.6 = (bf16[256,512]{1,0:T(8,128)(2,1)S(1)}, bf16[256,512]{1,0:T(8,128)(2,1)}, u32[]{:S(2)}) copy-start(bf16[256,512]{1,0:T(8,128)(2,1)} %param.28) | copy-start | bytes 786436
  81.3 361.2 %reduce-scatter.2.cloned.1.call-start = ((), (), s32[]{:S(2)}) async-start(), calls=%async_computation.2 | async-start | bytes 5898240 | tf_op jit(solution)/shard_map/reduce_scatter | solution.py:1421
  81.3 49.2 %collective-permute-start = (bf16[256,512]{1,0:T(8,128)(2,1)S(1)}, bf16[256,512]{1,0:T(8,128)(2,1)S(1)}, u32[]{:S(2)}, u32[]{:S(2)}) collective-permute-start(bf16[256,512]{1,0:T(8,128)(2,1)S(1)} %copy-done.6), channel_id=1, source_target_pairs={{0,8},{8,16},{16,24},{24,0},{1,9},{9,17},{17,25},{25,1},{2,10},{10... | collective-permute-start | bytes 786440 | tf_op jit(solution)/shard_map/ppermute | solution.py:1446
  81.4 49.1 %collective-permute-start.1 = (bf16[256,512]{1,0:T(8,128)(2,1)S(1)}, bf16[256,512]{1,0:T(8,128)(2,1)S(1)}, u32[]{:S(2)}, u32[]{:S(2)}) collective-permute-start(bf16[256,512]{1,0:T(8,128)(2,1)S(1)} %copy-done.6), channel_id=1, source_target_pairs={{0,16},{8,24},{16,0},{24,8},{1,17},{9,25},{17,1},{25,9},{2,18},{10... | collective-permute-start | bytes 786440 | tf_op jit(solution)/shard_map/ppermute | solution.py:1446
  83.1 47.4 %collective-permute-start.2 = (bf16[256,512]{1,0:T(8,128)(2,1)S(1)}, bf16[256,512]{1,0:T(8,128)(2,1)S(1)}, u32[]{:S(2)}, u32[]{:S(2)}) collective-permute-start(bf16[256,512]{1,0:T(8,128)(2,1)S(1)} %copy-done.6), channel_id=1, source_target_pairs={{0,24},{8,0},{16,8},{24,16},{1,25},{9,1},{17,9},{25,17},{2,26},{10... | collective-permute-start | bytes 786440 | tf_op jit(solution)/shard_map/ppermute | solution.py:1446
  86.2 13.5 %copy-start.9 = (f32[4,3,256]{2,0,1:T(4,128)S(1)}, f32[4,3,256]{2,0,1:T(4,128)}, u32[]{:S(2)}) copy-start(f32[4,3,256]{2,0,1:T(4,128)} %param.26) | copy-start | bytes 36868
  130.5 1.1 copy-start.3
  250.7 8.8 %copy-start.11 = (bf16[704,2048]{1,0:T(8,128)(2,1)S(1)}, bf16[704,2048]{1,0:T(8,128)(2,1)}, u32[]{:S(2)}) copy-start(bf16[704,2048]{1,0:T(8,128)(2,1)} %get-tuple-element.96.w_d) | copy-start | bytes 8650756
  250.7 8.8 %copy-start.13 = (bf16[1280,704]{1,0:T(8,128)(2,1)S(1)}, bf16[1280,704]{1,0:T(8,128)(2,1)}, u32[]{:S(2)}) copy-start(bf16[1280,704]{1,0:T(8,128)(2,1)} %get-tuple-element.97) | copy-start | bytes 5406724
  259.4 6.0 %copy-start.12 = (bf16[1280,704]{1,0:T(8,128)(2,1)S(1)}, bf16[1280,704]{1,0:T(8,128)(2,1)}, u32[]{:S(2)}) copy-start(bf16[1280,704]{1,0:T(8,128)(2,1)} %get-tuple-element.102) | copy-start | bytes 5406724
  373.0 65.8 %collective-permute-start.3 = (bf16[960,512]{1,0:T(8,128)(2,1)}, bf16[960,512]{1,0:T(8,128)(2,1)S(1)}, u32[]{:S(2)}, u32[]{:S(2)}) collective-permute-start(bf16[960,512]{1,0:T(8,128)(2,1)} %get-tuple-element.138), channel_id=1, source_target_pairs={{0,8},{8,16},{16,24},{24,0},{1,9},{9,17},{17,25},{25,1},{2,10},{10... | collective-permute-start | bytes 2949128 | tf_op jit(solution)/shard_map/ppermute | solution.py:1456
  374.5 64.2 %collective-permute-start.4 = (bf16[960,512]{1,0:T(8,128)(2,1)}, bf16[960,512]{1,0:T(8,128)(2,1)S(1)}, u32[]{:S(2)}, u32[]{:S(2)}) collective-permute-start(bf16[960,512]{1,0:T(8,128)(2,1)} %get-tuple-element.139), channel_id=1, source_target_pairs={{0,16},{8,24},{16,0},{24,8},{1,17},{9,25},{17,1},{25,9},{2,18},{10... | collective-permute-start | bytes 2949128 | tf_op jit(solution)/shard_map/ppermute | solution.py:1456
  375.2 63.6 %collective-permute-start.5 = (bf16[960,512]{1,0:T(8,128)(2,1)}, bf16[960,512]{1,0:T(8,128)(2,1)}, u32[]{:S(2)}, u32[]{:S(2)}) collective-permute-start(bf16[960,512]{1,0:T(8,128)(2,1)} %get-tuple-element.140), channel_id=1, source_target_pairs={{0,24},{8,0},{16,8},{24,16},{1,25},{9,1},{17,9},{25,17},{2,26},{10... | collective-permute-start | bytes 2949128 | tf_op jit(solution)/shard_map/ppermute | solution.py:1456
  382.7 41.2 %copy-start.10 = (f32[8,256]{1,0:T(8,128)S(1)}, f32[8,256]{1,0:T(8,128)}, u32[]{:S(2)}) copy-start(f32[8,256]{1,0:T(8,128)} %get-tuple-element.125) | copy-start | bytes 24580
  425.8 12.9 %copy-start.5 = (bf16[960,512]{1,0:T(8,128)(2,1)S(1)}, bf16[960,512]{1,0:T(8,128)(2,1)}, u32[]{:S(2)}) copy-start(bf16[960,512]{1,0:T(8,128)(2,1)} %get-tuple-element.137) | copy-start | bytes 2949124
  520.0 1.4 copy-start.7
  520.0 3.4 copy-start.8
  520.1 4.0 copy-start.2
  522.7 2.3 copy-start.4
  524.0 2.0 copy-start.1
  525.0 2.1 copy-start
Sparse Core Ops, SparseCore 0:
  81.4 53.9 all-gather.1
  360.8 58.5 reduce-scatter.1

commit v6 on v5

--- a/solution.py
+++ b/solution.py
@@ -657,7 +657,7 @@
     if fill:
         *scratch, l_buf, r_buf, blocks, strips, l_sem, r_sem, w_s, w_r, w_own = scratch
     (low, dgain, outbox, inbox, deal_s, deal_r, held, ours, shard_s, shard_r, group_s, group_r,
-     acc, tots, tot_s, tot_r, mine, theirs, from_below, from_above,
+     acc, tots, wide_t, tot_s, tot_r, mine, theirs, from_below, from_above,
      here, core_s, core_r, up_s, up_r, down_s, down_r) = scratch
     h, t, up, down, across = places()
 
@@ -814,9 +814,11 @@
     arrive(h)
     for i, p in enumerate(peers):
         tot_copy(i, p[0], p[1]).wait_recv()
-    tots[me] = share[...]
+    v = share[...]
     for i, p in enumerate(peers):
-        tots[me] = tots[me] + tots[p[1]]
+        v = v + tots[p[1]]
+    for i in range(CAP // STEP):
+        wide_t[i] = jnp.broadcast_to(v[i:i + 1, :], (8, 128))
     dgain[...] = jnp.zeros_like(dgain)
     gains = gain[...]
     eighth = jnp.full((8, 128), 0.125, BF)
@@ -858,7 +860,7 @@
     def close(get):
         def step(i, c):
             r = pl.ds(pl.multiple_of(i * STEP, STEP), STEP)
-            hi, lo = split(tots[me, i])
+            hi, lo = split(wide_t[i])
             total_r = dg(hi, eighth, TN) + dg(lo, eighth, TN)
             sc = scale[r, :]
             kp = kept[r, :].astype(F32)
@@ -977,7 +979,8 @@
         scratch_shapes=[pltpu.VMEM(a.shape, BF) for a in stacks] + [pltpu.VMEM((rows, width), BF), pltpu.VMEM((8, width), F32)]
         + [pltpu.VMEM((m, per_peer, width), BF)] * 2 + [dma((m,))] * 2
         + [pltpu.VMEM((m,) + small.shape, F32), pltpu.VMEM(small.shape, F32), dma((m,)), dma((m,)), dma((2 * n,)), dma((2 * n,))]
-        + [pltpu.VMEM((rows, width), F32), pltpu.VMEM((2 * n, rows // STEP, 8, STEP), F32), dma((2 * n,)), dma((2 * n,))]
+        + [pltpu.VMEM((rows, width), F32), pltpu.VMEM((2 * n, 16, 128), F32), pltpu.VMEM((rows // STEP, 8, STEP), F32),
+           dma((2 * n,)), dma((2 * n,))]
         + [pltpu.VMEM((n, rows, width), BF)] * 2 + [pltpu.VMEM((n - 1, rows, width), BF)] * 2
         + [dma((n,))] * 3 + [dma((n - 1,))] * 4 + room + [dma((len(stacks),))] + sems,
         compiler_params=pltpu.CompilerParams(collective_id=collective_id, has_side_effects=True, vmem_limit_bytes=ROOM),
@@ -995,8 +998,8 @@
 def turn_kernel(n, width, m, kinds, norm, *refs):
     if norm:
         (part, kept, scale, base, gain, share), (out, full, low, dgain), scratch, carry = carry_of(kinds, m, refs, 6, 4)
-        tots, tot_s, tot_r = scratch[-3:]
-        scratch = scratch[:-3]
+        tots, wide_t, tot_s, tot_r = scratch[-4:]
+        scratch = scratch[:-4]
     else:
         (part, base), (out, full, low), scratch, carry = carry_of(kinds, m, refs, 2, 3, True)
     (mine, theirs, from_below, from_above, here, core_s, core_r, up_s, up_r, down_s, down_r,
@@ -1102,9 +1105,11 @@
     def gather_totals():
         for i, p in enumerate(group_peers(n)):
             tot_copy(i, p[0], p[1]).wait_recv()
-        tots[me] = share[...]
+        v = share[...]
         for i, p in enumerate(group_peers(n)):
-            tots[me] = tots[me] + tots[p[1]]
+            v = v + tots[p[1]]
+        for i in range(UNITS):
+            wide_t[i] = jnp.broadcast_to(v[i:i + 1, :], (8, 128))
 
     def last(r, s):
         u = SUBS * r + s
@@ -1132,7 +1137,7 @@
             set_out(u)
 
     def close(u):
-        hi, lo = split(tots[me, u])
+        hi, lo = split(wide_t[u])
         eighth = jnp.full((8, 128), 0.125, BF)
         total_r = (dg(hi, eighth, TN) + dg(lo, eighth, TN))[:UNIT]
         sc = scale[rows(u), :]
@@ -1262,7 +1267,7 @@
     more = []
     if norm is not None:
         outs, out_specs = outs + [shape((8, width), F32)], out_specs + [VM]
-        more = [pltpu.VMEM((2 * n, UNITS, 8, 128), F32), dma((2 * n,)), dma((2 * n,))]
+        more = [pltpu.VMEM((2 * n, 16, 128), F32), pltpu.VMEM((UNITS, 8, 128), F32), dma((2 * n,)), dma((2 * n,))]
     return pl.pallas_call(
         functools.partial(turn_kernel, n, width, m, kinds, norm is not None),
         out_shape=outs + shapes,
@@ -1436,6 +1441,10 @@
     if weights.ndim == 2:
         return weights
     return weights.transpose(1, 0, 2).reshape(weights.shape[1], -1)
+
+
+def sixteen(share):
+    return jnp.pad(share[:, 0, :], ((0, 16 - share.shape[0]), (0, 0)))
 
 
 def gather_ring(piece):
@@ -1497,7 +1506,7 @@
     ffn_gain_part = lax.dynamic_slice_in_dim(gain_ffn, col_start, width)[None, :]
     d_hidden, d_branch_full, _, ffn_gain_grad, d_w_ug, d_w_down = z_turn(
         n, d_normed_two, cotangent, 4, "turn_normed_two", shards, (gate_kind, down_kind), (d_w_ug, d_w_down),
-        norm=(held_low, scale_two, ffn_gain_part, share_two))
+        norm=(held_low, scale_two, ffn_gain_part, sixteen(share_two)))
     out_part = mm(product, w_d).astype(BF)
     out_part, d_branch_full = lax.optimization_barrier((out_part, d_branch_full))
     d_w_u, d_w_out = swap_ring(d_up, normed_two, mixed, d_branch_full)
@@ -1513,7 +1522,7 @@
         jnp.pad(jnp.sum(d_head_gain, axis=0), (0, width - HD))[None, :],
         jnp.zeros((1, width), F32)], axis=0)
     d_tokens, summed, d_w_ug, d_w_down, d_w_in, d_w_bt = z_finish(
-        n, d_normed, x_rows, scale_one, d_hidden, mixer_gain_part, share_one, small,
+        n, d_normed, x_rows, scale_one, d_hidden, mixer_gain_part, sixteen(share_one), small,
         sent_slot, recv_slot, per_peer, 6, "finish_rows", shards, normed, d_pre, (d_w_ug, d_w_down))
     d_w_in = sum_blocks(d_w_in)
     by_row = summed.transpose(1, 0, 2).reshape(16, D)

time: 542 us -> 537 us (level)
  Pallas kernels: 451 us -> 444 us
    pallas_call x2, Pallas kernels: 171 us -> 164 us  [z_turn(): pl.pallas_call(functools.partial(turn_kernel, n, width, m, kinds, norm is...]
where the time goes in v6:
time: 537 us; the launch traced here: 530 us
  Pallas kernels  444 us (83%)
  matrix products  31.9 us (6%)
  local copies, waits for them, and re-layouts  18.3 us (3%)
  between operations  14.8 us (3%)
  other arithmetic  11.8 us (2%)
  starting transfers between devices  9.49 us (2%)
    pallas_call x2, Pallas kernels, z_turn(): pl.pallas_call(functools.partial(turn_kernel, n, width, m, kinds, norm is...  164 us
    pallas_call x1, Pallas kernels, z_finish(): pl.pallas_call(functools.partial(finish_kernel, n, width, m, kinds, int(f...  72.7 us
    pallas_call x1, Pallas kernels, z_gather(): pl.pallas_call(functools.partial(gather_kernel, n, width, m, kinds), out_...  70.4 us
    pallas_call x3, Pallas kernels, by_rows(): pl.pallas_call(kernel, grid=(CAP // rows,), out_shape=shapes, in_specs=sp...  58 us
    pallas_call x1, Pallas kernels, mixer_bwd(): pl.pallas_call(bwd_kernel, out_shape=outs, in_specs=[VM] * 6 + [pl.BlockS...  39.4 us
    dot_general x5, matrix products, mm(): return lax.dot_general(left, right, dims, preferred_element_type=F32)  31.9 us
    pallas_call x1, Pallas kernels, mixer_fwd(): pl.pallas_call(fwd_kernel, out_shape=outs, in_specs=[VM] * 5, out_specs=[...  28.8 us
    pallas_call x1, Pallas kernels, grad_blocks(): pl.pallas_call(blocks_kernel, grid_spec=pltpu.PrefetchScalarGridSpec(num_...  11.1 us
  transfers between devices with their start and end apart: 8, of which 0 were waited for; matrix products, arithmetic and copies ran while one was open for 4% of the time, Pallas kernels for 20%

profile of v6, /device:TPU:0, one launch (start us, length us, event | category | flops | bytes accessed | tf_op | source)
XLA Modules:
  0.0 530.5 jit_solution(3137259770891385872)
XLA Ops:
  7.2 1.3 pad.12.refs_4_
  8.5 2.3 pad_maximum_fusion.refs_3_
  10.9 70.4 %gather_rows.1 = (bf16[1280,256]{1,0:T(8,128)(2,1)}, bf16[1280,2048]{1,0:T(8,128)(2,1)}, s32[1152,1]{1,0:T(8,128)}, s32[1,1280]{1,0:T(1,128)}, s32[1280,1]{1,0:T...) custom-call(s32[16]{0:T(128)} %refs_0_.1, s32[16]{0:T(128)} %refs_1_.1, ...), custom_call_target="tpu_custom_call" | custom-call | bytes 157286400 | tf_op jit(solution)/shard_map/gather_rows/pallas_call | solution.py:618
  81.4 1.7 collective-permute-start.1
  83.1 3.0 collective-permute-start.2
  86.2 13.4 %project.1 = (f32[1280,1152]{1,0:T(8,128)}, bf16[1280,2048]{1,0:T(8,128)(2,1)}, f32[1280,1]{1,0:T(8,128)}) custom-call(bf16[1280,2048]{1,0:T(8,128)(2,1)} %get-tuple-element.80.x, f32[1,2048]{1,0:T(1,128)} %bitcast.51, bf16[2048,1024]{1,0:T(8,128)(2,1)} %get-tuple-element.81.w, bf16[16,2048]{1,0:T(8,128)(2,1)} %get-tuple-element.82.wb), custom_call_target="tpu_custom_call" | custom-call | flops 6039797760 | bytes 20971520 | tf_op jit(solution)/shard_map/project/pallas_call | solution.py:1299
  100.4 1.3 dynamic_slice.6
  101.7 28.8 %mixer_forward.1 = (bf16[1280,256]{1,0:T(8,128)(2,1)}, f32[1280,768]{1,0:T(8,128)}, f32[1280,512]{1,0:T(8,128)}, f32[1280,256]{1,0:T(8,128)}, f32[1280,256]{1,0:...) custom-call(f32[1280,1152]{1,0:T(8,128)} %get-tuple-element.83.pre, ...), custom_call_target="tpu_custom_call" | custom-call | bytes 146800640 | tf_op jit(solution)/shard_map/mixer_forward/pallas_call | solution.py:166
  131.6 3.8 convolution_convert_fusion.1.refs_0_
  135.4 83.6 %turn_branch.1 = (f32[1280,256]{1,0:T(8,128)}, bf16[1280,2048]{1,0:T(8,128)(2,1)}, bf16[1280,256]{1,0:T(8,128)(2,1)}, bf16[704,2048]{1,0:T(8,128)(2,1)}, bf16[70...) custom-call(bf16[1280,2048]{1,0:T(8,128)(2,1)} %convolution_convert_fusion.1.refs_0_, ...), custom_call_target="tpu_custom_call" | custom-call | bytes 157286400 | tf_op jit(solution)/shard_map/turn_branch/pallas_call | solution.py:1271
  219.0 31.6 %feed_forward.1 = (bf16[1280,2048]{1,0:T(8,128)(2,1)}, bf16[1280,704]{1,0:T(8,128)(2,1)}, bf16[1280,704]{1,0:T(8,128)(2,1)}, bf16[1280,704]{1,0:T(8,128)(2,1)}, ...) custom-call(bf16[1280,2048]{1,0:T(8,128)(2,1)} %get-tuple-element.92.x, ...), custom_call_target="tpu_custom_call" | custom-call | flops 18454937600 | bytes 20971520 | tf_op jit(solution)/shard_map/feed_forward/pallas_call | solution.py:1299
  250.7 8.7 %convolution_convert_fusion.2.refs_7_ = bf16[704,2048]{1,0:T(8,128)(2,1)} fusion(bf16[1280,704]{1,0:T(8,128)(2,1)} %get-tuple-element.97, bf16[1280,2048]{1,0:T(8,128)(2,1)} %all-gather.2.cloned.1.call-done.cot), kind=kOutput, calls=%fused_computation.3 | convolution fusion | flops 3692429312 | bytes 9928704 | tf_op jit(solution)/shard_map/dot_general | solution.py:1418
  259.5 6.0 %convolution_convert_fusion = bf16[1280,2048]{1,0:T(8,128)(2,1)} fusion(bf16[1280,704]{1,0:T(8,128)(2,1)S(1)} %copy-done.14, bf16[704,2048]{1,0:T(8,128)(2,1)S(1)} %copy-done.12), kind=kOutput, calls=%fused_computation.1 | convolution fusion | flops 3693608960 | bytes 9928704 | tf_op jit(solution)/shard_map/dot_general | solution.py:1418
  266.1 8.1 %convolution_convert_fusion.3.refs_6_ = bf16[704,2048]{1,0:T(8,128)(2,1)} fusion(bf16[1280,704]{1,0:T(8,128)(2,1)S(1)} %copy-done.13, bf16[1280,2048]{1,0:T(8,128)(2,1)} %get-tuple-element.103.x), kind=kOutput, calls=%fused_computation.4 | convolution fusion | flops 3692429312 | bytes 9928704 | tf_op jit(solution)/shard_map/dot_general | solution.py:1418
  274.2 80.2 %turn_normed_two.1 = (f32[1280,256]{1,0:T(8,128)}, bf16[1280,2048]{1,0:T(8,128)(2,1)}, bf16[1280,256]{1,0:T(8,128)(2,1)}, f32[8,256]{1,0:T(8,128)}, bf16[4,704,5...) custom-call(bf16[1280,2048]{1,0:T(8,128)(2,1)} %get-tuple-element.98.refs_0_, ...), custom_call_target="tpu_custom_call" | custom-call | bytes 157286400 | tf_op jit(solution)/shard_map/turn_normed_two/pallas_call | solution.py:1271
  354.4 1.3 dynamic_slice.7
  355.8 11.1 %gradient_blocks.1 = (bf16[960,512]{1,0:T(8,128)(2,1)}, bf16[960,512]{1,0:T(8,128)(2,1)}, bf16[960,512]{1,0:T(8,128)(2,1)}, bf16[960,512]{1,0:T(8,128)(2,1)}) custom-call(s32[1]{0:T(128)} %bitcast.16.shard, bf16[1280,704]{1,0:T(8,128)(2,1)} %get-tuple-element.136.a, bf16[1280,2048]{1,0:T(8,128)(2,1)} %get-tuple-element.103.x, ...), custom_call_target="tpu_custom_call" | custom-call | flops 5033164800 | bytes 12582912 | tf_op jit(solution)/shard_map/gradient_blocks/pallas_call | solution.py:1400
  366.9 1.6 collective-permute-start.3
  369.1 2.4 collective-permute-start.5
  371.4 5.2 fusion.2.dmix
  376.7 39.4 %mixer_backward.1 = (bf16[1280,1152]{1,0:T(8,128)(2,1)}, f32[12,8,256]{2,1,0:T(8,128)}, f32[8,128]{1,0:T(8,128)}) custom-call(f32[1280,256]{1,0:T(8,128)} %fusion.2.dmix, f32[1280,1152]{1,0:T(8,128)} %get-tuple-element.83.pre, s32[1280,1]{1,0:T(8,128)} %get-tuple-element.84.pos_ref, f32[1280,1]{1,0:T(8,128)} %get-tuple-element.85.fill_ref, ...), custom_call_target="tpu_custom_call" | custom-call | bytes 209715200 | tf_op jit(solution)/shard_map/mixer_backward/pallas_call | solution.py:304
  417.7 12.9 %unproject.1 = (bf16[1280,2048]{1,0:T(8,128)(2,1)}, f32[10,8,128]{2,1,0:T(8,128)}) custom-call(bf16[1280,1152]{1,0:T(8,128)(2,1)} %get-tuple-element.116.d_pre.refs_12_, f32[1280,1152]{1,0:T(8,128)} %get-tuple-element.83.pre, f32[1280,1]{1,0:T(8,128)} %get-tuple-element.117.scale.refs_2_, bf16[2048,1024]{1,0:T(8,128)(2,1)} %get-tuple-element.81.w, ...), custom_call_target="tpu_custom_call" | custom-call | flops 6039797760 | bytes 20971520 | tf_op jit(solution)/shard_map/unproject/pallas_call | solution.py:1299
  432.1 1.9 concatenate.7.refs_6_
  434.0 1.7 convert_add_fusion
  436.5 1.2 slice_bitcast_fusion
  437.7 1.2 convert_element_type.46
  438.9 72.7 %finish_rows.1 = (f32[1152,1,256]{2,1,0:T(1,128)}, f32[8,16,256]{2,1,0:T(8,128)}, f32[704,512]{1,0:T(8,128)}, f32[704,512]{1,0:T(8,128)}, bf16[4,512,1024]{2,1,0:T(8,128)(2,1)}, /*index=5*/bf16[4,16,512]{2,1,0:T(8,128)(2,1)}) custom-call(bf16[1280,2048]{1,0:T(8,128)(2,1)} %get-tuple-element.121.refs_0_, bf16[1280,256]{1,0:T(8,128)(2,1)} %get-tuple-element.90.refs_1_, ...), custom_call_target="tpu_custom_call" | custom-call | bytes 157286400 | tf_op jit(solution)/shard_map/finish_rows/pallas_call | solution.py:973
  511.6 3.4 convert_reduce_fusion
  515.0 1.4 fusion
  520.0 1.0 copy.47
  521.0 1.1 copy.48
  522.1 1.1 copy.49
  (70 shorter events, 10.7 us)
Async XLA Ops:
  7.2 128.3 %all-gather.2.cloned.1.call-start = ((), (), s32[]{:S(2)}) async-start(), calls=%async_computation.1 | async-start | bytes 5898240 | tf_op jit(solution)/shard_map/all_gather | solution.py:1422
  8.5 72.8 %copy-start.6 = (bf16[256,512]{1,0:T(8,128)(2,1)S(1)}, bf16[256,512]{1,0:T(8,128)(2,1)}, u32[]{:S(2)}) copy-start(bf16[256,512]{1,0:T(8,128)(2,1)} %param.28) | copy-start | bytes 786436
  81.3 356.5 %reduce-scatter.2.cloned.1.call-start = ((), (), s32[]{:S(2)}) async-start(), calls=%async_computation.2 | async-start | bytes 5898240 | tf_op jit(solution)/shard_map/reduce_scatter | solution.py:1426
  81.3 49.2 %collective-permute-start = (bf16[256,512]{1,0:T(8,128)(2,1)S(1)}, bf16[256,512]{1,0:T(8,128)(2,1)S(1)}, u32[]{:S(2)}, u32[]{:S(2)}) collective-permute-start(bf16[256,512]{1,0:T(8,128)(2,1)S(1)} %copy-done.6), channel_id=1, source_target_pairs={{0,8},{8,16},{16,24},{24,0},{1,9},{9,17},{17,25},{25,1},{2,10},{10... | collective-permute-start | bytes 786440 | tf_op jit(solution)/shard_map/ppermute | solution.py:1455
  81.4 49.2 %collective-permute-start.1 = (bf16[256,512]{1,0:T(8,128)(2,1)S(1)}, bf16[256,512]{1,0:T(8,128)(2,1)S(1)}, u32[]{:S(2)}, u32[]{:S(2)}) collective-permute-start(bf16[256,512]{1,0:T(8,128)(2,1)S(1)} %copy-done.6), channel_id=1, source_target_pairs={{0,16},{8,24},{16,0},{24,8},{1,17},{9,25},{17,1},{25,9},{2,18},{10... | collective-permute-start | bytes 786440 | tf_op jit(solution)/shard_map/ppermute | solution.py:1455
  83.1 47.5 %collective-permute-start.2 = (bf16[256,512]{1,0:T(8,128)(2,1)S(1)}, bf16[256,512]{1,0:T(8,128)(2,1)S(1)}, u32[]{:S(2)}, u32[]{:S(2)}) collective-permute-start(bf16[256,512]{1,0:T(8,128)(2,1)S(1)} %copy-done.6), channel_id=1, source_target_pairs={{0,24},{8,0},{16,8},{24,16},{1,25},{9,1},{17,9},{25,17},{2,26},{10... | collective-permute-start | bytes 786440 | tf_op jit(solution)/shard_map/ppermute | solution.py:1455
  86.2 13.5 %copy-start.10 = (f32[4,3,256]{2,0,1:T(4,128)S(1)}, f32[4,3,256]{2,0,1:T(4,128)}, u32[]{:S(2)}) copy-start(f32[4,3,256]{2,0,1:T(4,128)} %param.26) | copy-start | bytes 36868
  130.5 1.1 copy-start.3
  250.7 8.8 %copy-start.12 = (bf16[704,2048]{1,0:T(8,128)(2,1)S(1)}, bf16[704,2048]{1,0:T(8,128)(2,1)}, u32[]{:S(2)}) copy-start(bf16[704,2048]{1,0:T(8,128)(2,1)} %get-tuple-element.96.w_d) | copy-start | bytes 8650756
  250.7 8.8 %copy-start.14 = (bf16[1280,704]{1,0:T(8,128)(2,1)S(1)}, bf16[1280,704]{1,0:T(8,128)(2,1)}, u32[]{:S(2)}) copy-start(bf16[1280,704]{1,0:T(8,128)(2,1)} %get-tuple-element.97) | copy-start | bytes 5406724
  259.5 6.0 %copy-start.9 = (f32[16,8,128]{2,1,0:T(8,128)S(1)}, f32[16,8,128]{2,1,0:T(8,128)}, u32[]{:S(2)}) copy-start(f32[16,8,128]{2,1,0:T(8,128)} %get-tuple-element.101) | copy-start | bytes 196612
  259.5 6.6 %copy-start.13 = (bf16[1280,704]{1,0:T(8,128)(2,1)S(1)}, bf16[1280,704]{1,0:T(8,128)(2,1)}, u32[]{:S(2)}) copy-start(bf16[1280,704]{1,0:T(8,128)(2,1)} %get-tuple-element.102) | copy-start | bytes 5406724
  366.9 67.1 %collective-permute-start.3 = (bf16[960,512]{1,0:T(8,128)(2,1)}, bf16[960,512]{1,0:T(8,128)(2,1)S(1)}, u32[]{:S(2)}, u32[]{:S(2)}) collective-permute-start(bf16[960,512]{1,0:T(8,128)(2,1)} %get-tuple-element.138), channel_id=1, source_target_pairs={{0,8},{8,16},{16,24},{24,0},{1,9},{9,17},{17,25},{25,1},{2,10},{10... | collective-permute-start | bytes 2949128 | tf_op jit(solution)/shard_map/ppermute | solution.py:1465
  368.5 65.5 %collective-permute-start.4 = (bf16[960,512]{1,0:T(8,128)(2,1)}, bf16[960,512]{1,0:T(8,128)(2,1)S(1)}, u32[]{:S(2)}, u32[]{:S(2)}) collective-permute-start(bf16[960,512]{1,0:T(8,128)(2,1)} %get-tuple-element.139), channel_id=1, source_target_pairs={{0,16},{8,24},{16,0},{24,8},{1,17},{9,25},{17,1},{25,9},{2,18},{10... | collective-permute-start | bytes 2949128 | tf_op jit(solution)/shard_map/ppermute | solution.py:1465
  369.1 64.9 %collective-permute-start.5 = (bf16[960,512]{1,0:T(8,128)(2,1)}, bf16[960,512]{1,0:T(8,128)(2,1)}, u32[]{:S(2)}, u32[]{:S(2)}) collective-permute-start(bf16[960,512]{1,0:T(8,128)(2,1)} %get-tuple-element.140), channel_id=1, source_target_pairs={{0,24},{8,0},{16,8},{24,16},{1,25},{9,1},{17,9},{25,17},{2,26},{10... | collective-permute-start | bytes 2949128 | tf_op jit(solution)/shard_map/ppermute | solution.py:1465
  376.7 41.0 %copy-start.11 = (f32[8,256]{1,0:T(8,128)S(1)}, f32[8,256]{1,0:T(8,128)}, u32[]{:S(2)}) copy-start(f32[8,256]{1,0:T(8,128)} %get-tuple-element.125) | copy-start | bytes 24580
  417.7 16.3 %copy-start.5 = (bf16[960,512]{1,0:T(8,128)(2,1)S(1)}, bf16[960,512]{1,0:T(8,128)(2,1)}, u32[]{:S(2)}) copy-start(bf16[960,512]{1,0:T(8,128)(2,1)} %get-tuple-element.137) | copy-start | bytes 2949124
  515.0 1.4 copy-start.7
  515.0 3.4 copy-start.8
  515.0 4.0 copy-start.2
  517.7 2.3 copy-start.4
  519.0 2.0 copy-start.1
  520.0 2.1 copy-start
Sparse Core Ops, SparseCore 0:
  81.4 53.9 all-gather.1
  354.6 58.6 reduce-scatter.1

commit v7 on v6

--- a/solution.py
+++ b/solution.py
@@ -136,7 +136,7 @@
             out.append(s - d3(m_out[e], s) + b_s[e])
         return tuple(out)
     zs = jnp.zeros((HD, HD), F32)
-    lax.fori_loop(0, NB, phase_b, (zs, zs))
+    lax.fori_loop(0, NB // 4, four_times(phase_b), (zs, zs))
     keep(9)
     def phase_c(i, _):
         todo = [(n, pl.ds(pl.multiple_of(n * BLOCK, BLOCK), BLOCK), h, slice(h*HD, (h+1)*HD)) for n in (4*i, 4*i+1, 4*i+2, 4*i+3) for h in range(heads)]
@@ -222,7 +222,7 @@
             out.append((d - d3(m_in[e], d, TN) + ee) * goes_on(pos_ref, n))
         return tuple(out)
     zs = jnp.zeros((HD, HD), F32)
-    lax.fori_loop(0, NB, phase_b, (zs, zs))
+    lax.fori_loop(0, NB // 4, four_times(phase_b), (zs, zs))
     for i in (7, 9, 0, 3, 4):
         fetch(i).wait()
 

time: 537 us -> 536 us (level)
  transfers between devices with their start and end apart: 8 -> 8, of which waited for: 0 -> 1; matrix products, arithmetic and copies ran while one was open for 4% -> 4% of each run, Pallas kernels for 20% -> 20%
where the time goes in v7:
time: 536 us; the launch traced here: 530 us
  Pallas kernels  442 us (82%)
  matrix products  31.9 us (6%)
  local copies, waits for them, and re-layouts  18.3 us (3%)
  between operations  14.8 us (3%)
  other arithmetic  11.8 us (2%)
  starting transfers between devices  9.49 us (2%)
    pallas_call x2, Pallas kernels, z_turn(): pl.pallas_call(functools.partial(turn_kernel, n, width, m, kinds, norm is...  164 us
    pallas_call x1, Pallas kernels, z_finish(): pl.pallas_call(functools.partial(finish_kernel, n, width, m, kinds, int(f...  72.7 us
    pallas_call x1, Pallas kernels, z_gather(): pl.pallas_call(functools.partial(gather_kernel, n, width, m, kinds), out_...  70.4 us
    pallas_call x3, Pallas kernels, by_rows(): pl.pallas_call(kernel, grid=(CAP // rows,), out_shape=shapes, in_specs=sp...  57.9 us
    pallas_call x1, Pallas kernels, mixer_bwd(): pl.pallas_call(bwd_kernel, out_shape=outs, in_specs=[VM] * 6 + [pl.BlockS...  38.5 us
    dot_general x5, matrix products, mm(): return lax.dot_general(left, right, dims, preferred_element_type=F32)  31.9 us
    pallas_call x1, Pallas kernels, mixer_fwd(): pl.pallas_call(fwd_kernel, out_shape=outs, in_specs=[VM] * 5, out_specs=[...  28 us
    pallas_call x1, Pallas kernels, grad_blocks(): pl.pallas_call(blocks_kernel, grid_spec=pltpu.PrefetchScalarGridSpec(num_...  11.1 us
  transfers between devices with their start and end apart: 8, of which 1 were waited for; matrix products, arithmetic and copies ran while one was open for 4% of the time, Pallas kernels for 20%

profile of v7, /device:TPU:0, one launch (start us, length us, event | category | flops | bytes accessed | tf_op | source)
XLA Modules:
  0.0 529.6 jit_solution(6039193319911540795)
XLA Ops:
  7.2 1.3 pad.12.refs_4_
  8.5 2.3 pad_maximum_fusion.refs_3_
  10.9 70.4 %gather_rows.1 = (bf16[1280,256]{1,0:T(8,128)(2,1)}, bf16[1280,2048]{1,0:T(8,128)(2,1)}, s32[1152,1]{1,0:T(8,128)}, s32[1,1280]{1,0:T(1,128)}, s32[1280,1]{1,0:T...) custom-call(s32[16]{0:T(128)} %refs_0_.1, s32[16]{0:T(128)} %refs_1_.1, ...), custom_call_target="tpu_custom_call" | custom-call | bytes 157286400 | tf_op jit(solution)/shard_map/gather_rows/pallas_call | solution.py:618
  81.4 1.7 collective-permute-start.1
  83.1 3.0 collective-permute-start.2
  86.2 13.4 %project.1 = (f32[1280,1152]{1,0:T(8,128)}, bf16[1280,2048]{1,0:T(8,128)(2,1)}, f32[1280,1]{1,0:T(8,128)}) custom-call(bf16[1280,2048]{1,0:T(8,128)(2,1)} %get-tuple-element.80.x, f32[1,2048]{1,0:T(1,128)} %bitcast.51, bf16[2048,1024]{1,0:T(8,128)(2,1)} %get-tuple-element.81.w, bf16[16,2048]{1,0:T(8,128)(2,1)} %get-tuple-element.82.wb), custom_call_target="tpu_custom_call" | custom-call | flops 6039797760 | bytes 20971520 | tf_op jit(solution)/shard_map/project/pallas_call | solution.py:1299
  100.4 1.3 dynamic_slice.6
  101.7 28.0 %mixer_forward.1 = (bf16[1280,256]{1,0:T(8,128)(2,1)}, f32[1280,768]{1,0:T(8,128)}, f32[1280,512]{1,0:T(8,128)}, f32[1280,256]{1,0:T(8,128)}, f32[1280,256]{1,0:...) custom-call(f32[1280,1152]{1,0:T(8,128)} %get-tuple-element.83.pre, ...), custom_call_target="tpu_custom_call" | custom-call | bytes 146800640 | tf_op jit(solution)/shard_map/mixer_forward/pallas_call | solution.py:166
  130.8 3.8 convolution_convert_fusion.1.refs_0_
  135.4 83.6 %turn_branch.1 = (f32[1280,256]{1,0:T(8,128)}, bf16[1280,2048]{1,0:T(8,128)(2,1)}, bf16[1280,256]{1,0:T(8,128)(2,1)}, bf16[704,2048]{1,0:T(8,128)(2,1)}, bf16[70...) custom-call(bf16[1280,2048]{1,0:T(8,128)(2,1)} %convolution_convert_fusion.1.refs_0_, ...), custom_call_target="tpu_custom_call" | custom-call | bytes 157286400 | tf_op jit(solution)/shard_map/turn_branch/pallas_call | solution.py:1271
  219.0 31.6 %feed_forward.1 = (bf16[1280,2048]{1,0:T(8,128)(2,1)}, bf16[1280,704]{1,0:T(8,128)(2,1)}, bf16[1280,704]{1,0:T(8,128)(2,1)}, bf16[1280,704]{1,0:T(8,128)(2,1)}, ...) custom-call(bf16[1280,2048]{1,0:T(8,128)(2,1)} %get-tuple-element.92.x, ...), custom_call_target="tpu_custom_call" | custom-call | flops 18454937600 | bytes 20971520 | tf_op jit(solution)/shard_map/feed_forward/pallas_call | solution.py:1299
  250.7 8.7 %convolution_convert_fusion.2.refs_7_ = bf16[704,2048]{1,0:T(8,128)(2,1)} fusion(bf16[1280,704]{1,0:T(8,128)(2,1)} %get-tuple-element.97, bf16[1280,2048]{1,0:T(8,128)(2,1)} %all-gather.2.cloned.1.call-done.cot), kind=kOutput, calls=%fused_computation.3 | convolution fusion | flops 3692429312 | bytes 9928704 | tf_op jit(solution)/shard_map/dot_general | solution.py:1418
  259.5 6.0 %convolution_convert_fusion = bf16[1280,2048]{1,0:T(8,128)(2,1)} fusion(bf16[1280,704]{1,0:T(8,128)(2,1)S(1)} %copy-done.14, bf16[704,2048]{1,0:T(8,128)(2,1)S(1)} %copy-done.12), kind=kOutput, calls=%fused_computation.1 | convolution fusion | flops 3693608960 | bytes 9928704 | tf_op jit(solution)/shard_map/dot_general | solution.py:1418
  266.1 8.1 %convolution_convert_fusion.3.refs_6_ = bf16[704,2048]{1,0:T(8,128)(2,1)} fusion(bf16[1280,704]{1,0:T(8,128)(2,1)S(1)} %copy-done.13, bf16[1280,2048]{1,0:T(8,128)(2,1)} %get-tuple-element.103.x), kind=kOutput, calls=%fused_computation.4 | convolution fusion | flops 3692429312 | bytes 9928704 | tf_op jit(solution)/shard_map/dot_general | solution.py:1418
  274.2 80.2 %turn_normed_two.1 = (f32[1280,256]{1,0:T(8,128)}, bf16[1280,2048]{1,0:T(8,128)(2,1)}, bf16[1280,256]{1,0:T(8,128)(2,1)}, f32[8,256]{1,0:T(8,128)}, bf16[4,704,5...) custom-call(bf16[1280,2048]{1,0:T(8,128)(2,1)} %get-tuple-element.98.refs_0_, ...), custom_call_target="tpu_custom_call" | custom-call | bytes 157286400 | tf_op jit(solution)/shard_map/turn_normed_two/pallas_call | solution.py:1271
  354.4 1.3 dynamic_slice.7
  355.8 11.1 %gradient_blocks.1 = (bf16[960,512]{1,0:T(8,128)(2,1)}, bf16[960,512]{1,0:T(8,128)(2,1)}, bf16[960,512]{1,0:T(8,128)(2,1)}, bf16[960,512]{1,0:T(8,128)(2,1)}) custom-call(s32[1]{0:T(128)} %bitcast.16.shard, bf16[1280,704]{1,0:T(8,128)(2,1)} %get-tuple-element.136.a, bf16[1280,2048]{1,0:T(8,128)(2,1)} %get-tuple-element.103.x, ...), custom_call_target="tpu_custom_call" | custom-call | flops 5033164800 | bytes 12582912 | tf_op jit(solution)/shard_map/gradient_blocks/pallas_call | solution.py:1400
  366.9 1.6 collective-permute-start.3
  369.1 2.4 collective-permute-start.5
  371.4 5.2 fusion.2.dmix
  376.7 38.5 %mixer_backward.1 = (bf16[1280,1152]{1,0:T(8,128)(2,1)}, f32[12,8,256]{2,1,0:T(8,128)}, f32[8,128]{1,0:T(8,128)}) custom-call(f32[1280,256]{1,0:T(8,128)} %fusion.2.dmix, f32[1280,1152]{1,0:T(8,128)} %get-tuple-element.83.pre, s32[1280,1]{1,0:T(8,128)} %get-tuple-element.84.pos_ref, f32[1280,1]{1,0:T(8,128)} %get-tuple-element.85.fill_ref, ...), custom_call_target="tpu_custom_call" | custom-call | bytes 209715200 | tf_op jit(solution)/shard_map/mixer_backward/pallas_call | solution.py:304
  416.8 12.9 %unproject.1 = (bf16[1280,2048]{1,0:T(8,128)(2,1)}, f32[10,8,128]{2,1,0:T(8,128)}) custom-call(bf16[1280,1152]{1,0:T(8,128)(2,1)} %get-tuple-element.116.d_pre.refs_12_, f32[1280,1152]{1,0:T(8,128)} %get-tuple-element.83.pre, f32[1280,1]{1,0:T(8,128)} %get-tuple-element.117.scale.refs_2_, bf16[2048,1024]{1,0:T(8,128)(2,1)} %get-tuple-element.81.w, ...), custom_call_target="tpu_custom_call" | custom-call | flops 6039797760 | bytes 20971520 | tf_op jit(solution)/shard_map/unproject/pallas_call | solution.py:1299
  431.2 1.9 concatenate.7.refs_6_
  433.1 1.7 convert_add_fusion
  435.6 1.2 slice_bitcast_fusion
  436.8 1.2 convert_element_type.46
  438.0 72.7 %finish_rows.1 = (f32[1152,1,256]{2,1,0:T(1,128)}, f32[8,16,256]{2,1,0:T(8,128)}, f32[704,512]{1,0:T(8,128)}, f32[704,512]{1,0:T(8,128)}, bf16[4,512,1024]{2,1,0:T(8,128)(2,1)}, /*index=5*/bf16[4,16,512]{2,1,0:T(8,128)(2,1)}) custom-call(bf16[1280,2048]{1,0:T(8,128)(2,1)} %get-tuple-element.121.refs_0_, bf16[1280,256]{1,0:T(8,128)(2,1)} %get-tuple-element.90.refs_1_, ...), custom_call_target="tpu_custom_call" | custom-call | bytes 157286400 | tf_op jit(solution)/shard_map/finish_rows/pallas_call | solution.py:973
  510.7 3.4 convert_reduce_fusion
  514.2 1.4 fusion
  519.1 1.0 copy.47
  520.1 1.1 copy.48
  521.2 1.1 copy.49
  (70 shorter events, 11.4 us)
Async XLA Ops:
  7.2 128.2 %all-gather.2.cloned.1.call-start = ((), (), s32[]{:S(2)}) async-start(), calls=%async_computation.1 | async-start | bytes 5898240 | tf_op jit(solution)/shard_map/all_gather | solution.py:1422
  8.5 72.8 %copy-start.6 = (bf16[256,512]{1,0:T(8,128)(2,1)S(1)}, bf16[256,512]{1,0:T(8,128)(2,1)}, u32[]{:S(2)}) copy-start(bf16[256,512]{1,0:T(8,128)(2,1)} %param.28) | copy-start | bytes 786436
  81.3 355.6 %reduce-scatter.2.cloned.1.call-start = ((), (), s32[]{:S(2)}) async-start(), calls=%async_computation.2 | async-start | bytes 5898240 | tf_op jit(solution)/shard_map/reduce_scatter | solution.py:1426
  81.3 48.4 %collective-permute-start = (bf16[256,512]{1,0:T(8,128)(2,1)S(1)}, bf16[256,512]{1,0:T(8,128)(2,1)S(1)}, u32[]{:S(2)}, u32[]{:S(2)}) collective-permute-start(bf16[256,512]{1,0:T(8,128)(2,1)S(1)} %copy-done.6), channel_id=1, source_target_pairs={{0,8},{8,16},{16,24},{24,0},{1,9},{9,17},{17,25},{25,1},{2,10},{10... | collective-permute-start | bytes 786440 | tf_op jit(solution)/shard_map/ppermute | solution.py:1455
  81.4 48.4 %collective-permute-start.1 = (bf16[256,512]{1,0:T(8,128)(2,1)S(1)}, bf16[256,512]{1,0:T(8,128)(2,1)S(1)}, u32[]{:S(2)}, u32[]{:S(2)}) collective-permute-start(bf16[256,512]{1,0:T(8,128)(2,1)S(1)} %copy-done.6), channel_id=1, source_target_pairs={{0,16},{8,24},{16,0},{24,8},{1,17},{9,25},{17,1},{25,9},{2,18},{10... | collective-permute-start | bytes 786440 | tf_op jit(solution)/shard_map/ppermute | solution.py:1455
  83.1 46.7 %collective-permute-start.2 = (bf16[256,512]{1,0:T(8,128)(2,1)S(1)}, bf16[256,512]{1,0:T(8,128)(2,1)S(1)}, u32[]{:S(2)}, u32[]{:S(2)}) collective-permute-start(bf16[256,512]{1,0:T(8,128)(2,1)S(1)} %copy-done.6), channel_id=1, source_target_pairs={{0,24},{8,0},{16,8},{24,16},{1,25},{9,1},{17,9},{25,17},{2,26},{10... | collective-permute-start | bytes 786440 | tf_op jit(solution)/shard_map/ppermute | solution.py:1455
  86.2 13.5 %copy-start.10 = (f32[4,3,256]{2,0,1:T(4,128)S(1)}, f32[4,3,256]{2,0,1:T(4,128)}, u32[]{:S(2)}) copy-start(f32[4,3,256]{2,0,1:T(4,128)} %param.26) | copy-start | bytes 36868
  129.7 1.1 copy-start.3
  250.7 8.8 %copy-start.12 = (bf16[704,2048]{1,0:T(8,128)(2,1)S(1)}, bf16[704,2048]{1,0:T(8,128)(2,1)}, u32[]{:S(2)}) copy-start(bf16[704,2048]{1,0:T(8,128)(2,1)} %get-tuple-element.96.w_d) | copy-start | bytes 8650756
  250.7 8.8 %copy-start.14 = (bf16[1280,704]{1,0:T(8,128)(2,1)S(1)}, bf16[1280,704]{1,0:T(8,128)(2,1)}, u32[]{:S(2)}) copy-start(bf16[1280,704]{1,0:T(8,128)(2,1)} %get-tuple-element.97) | copy-start | bytes 5406724
  259.5 6.0 %copy-start.9 = (f32[16,8,128]{2,1,0:T(8,128)S(1)}, f32[16,8,128]{2,1,0:T(8,128)}, u32[]{:S(2)}) copy-start(f32[16,8,128]{2,1,0:T(8,128)} %get-tuple-element.101) | copy-start | bytes 196612
  259.5 6.6 %copy-start.13 = (bf16[1280,704]{1,0:T(8,128)(2,1)S(1)}, bf16[1280,704]{1,0:T(8,128)(2,1)}, u32[]{:S(2)}) copy-start(bf16[1280,704]{1,0:T(8,128)(2,1)} %get-tuple-element.102) | copy-start | bytes 5406724
  366.9 66.2 %collective-permute-start.3 = (bf16[960,512]{1,0:T(8,128)(2,1)}, bf16[960,512]{1,0:T(8,128)(2,1)S(1)}, u32[]{:S(2)}, u32[]{:S(2)}) collective-permute-start(bf16[960,512]{1,0:T(8,128)(2,1)} %get-tuple-element.138), channel_id=1, source_target_pairs={{0,8},{8,16},{16,24},{24,0},{1,9},{9,17},{17,25},{25,1},{2,10},{10... | collective-permute-start | bytes 2949128 | tf_op jit(solution)/shard_map/ppermute | solution.py:1465
  368.5 64.6 %collective-permute-start.4 = (bf16[960,512]{1,0:T(8,128)(2,1)}, bf16[960,512]{1,0:T(8,128)(2,1)S(1)}, u32[]{:S(2)}, u32[]{:S(2)}) collective-permute-start(bf16[960,512]{1,0:T(8,128)(2,1)} %get-tuple-element.139), channel_id=1, source_target_pairs={{0,16},{8,24},{16,0},{24,8},{1,17},{9,25},{17,1},{25,9},{2,18},{10... | collective-permute-start | bytes 2949128 | tf_op jit(solution)/shard_map/ppermute | solution.py:1465
  369.1 64.0 %collective-permute-start.5 = (bf16[960,512]{1,0:T(8,128)(2,1)}, bf16[960,512]{1,0:T(8,128)(2,1)}, u32[]{:S(2)}, u32[]{:S(2)}) collective-permute-start(bf16[960,512]{1,0:T(8,128)(2,1)} %get-tuple-element.140), channel_id=1, source_target_pairs={{0,24},{8,0},{16,8},{24,16},{1,25},{9,1},{17,9},{25,17},{2,26},{10... | collective-permute-start | bytes 2949128 | tf_op jit(solution)/shard_map/ppermute | solution.py:1465
  376.7 40.1 %copy-start.11 = (f32[8,256]{1,0:T(8,128)S(1)}, f32[8,256]{1,0:T(8,128)}, u32[]{:S(2)}) copy-start(f32[8,256]{1,0:T(8,128)} %get-tuple-element.125) | copy-start | bytes 24580
  416.8 16.3 %copy-start.5 = (bf16[960,512]{1,0:T(8,128)(2,1)S(1)}, bf16[960,512]{1,0:T(8,128)(2,1)}, u32[]{:S(2)}) copy-start(bf16[960,512]{1,0:T(8,128)(2,1)} %get-tuple-element.137) | copy-start | bytes 2949124
  514.1 1.4 copy-start.7
  514.1 3.4 copy-start.8
  514.1 4.0 copy-start.2
  516.8 2.3 copy-start.4
  518.1 2.0 copy-start.1
  519.1 2.1 copy-start
Sparse Core Ops, SparseCore 0:
  81.4 53.9 all-gather.1
  354.6 58.6 reduce-scatter.1
